TPU v7x, 32 devices: a whole 2x2x4 slice. The times are simulated.
32 devices in a mesh: group: 2 (over y), expert: 4 (over x, core), seq: 4 (over z).
Axes of the slice: x: 2, y: 2, z: 4, core: 2. Of those that a mesh axis runs over, the one named last changes fastest.
Arguments:
- tokens: bfloat16 [4096, 2048], P(('group', 'expert', 'seq')), parts along dimension 0, may hold values from -6 to 6
- grad_out: bfloat16 [4096, 2048], P(('group', 'expert', 'seq')), parts along dimension 0, may hold values from -6 to 6
- probs: bfloat16 [4096, 8], P(('group', 'expert', 'seq')), parts along dimension 0, may hold values from 0.049804688 to 0.5
- routes: int32 [4096, 8], P(('group', 'expert')), parts along dimension 0, may hold values from 0 to 15, all different within a row; in each aligned block of 128 rows (0 to 127, 128 to 255, ...) at most 80 rows name the same one
- w_gate: bfloat16 [16, 2048, 384], P(('expert', 'seq')), may hold values from -0.3125 to 0.3125
- w_up: bfloat16 [16, 2048, 384], P(('expert', 'seq')), may hold values from -0.3125 to 0.3125
- w_down: bfloat16 [16, 384, 2048], P(('expert', 'seq')), may hold values from -0.125 to 0.125
- gate_pre: bfloat16 [32, 1280, 384], P(('group', 'expert', 'seq')), parts along dimension 0, may hold values from -6 to 6
- up_pre: bfloat16 [32, 1280, 384], P(('group', 'expert', 'seq')), parts along dimension 0, may hold values from -0.59765625 to 0.59765625
Outputs:
- grad_tokens: bfloat16 [4096, 2048], P(('group', 'expert', 'seq')), parts along dimension 0
- grad_probs: bfloat16 [4096, 8], P(('group', 'expert', 'seq')), parts along dimension 0
- grad_gate: bfloat16 [32, 2048, 384], P(('group', 'expert', 'seq')), parts along dimension 0
- grad_up: bfloat16 [32, 2048, 384], P(('group', 'expert', 'seq')), parts along dimension 0
- grad_down: bfloat16 [32, 384, 2048], P(('group', 'expert', 'seq')), parts along dimension 0
There are 2 independent parts, one for each index of `group`. A program takes and returns all parts, laid end to end along the dimension named above; an argument that names none is the same for every part. Nothing has to cross between parts.
Inputs may be any that keep to these rules, and one draw needn't show every extreme that they name: `routes`: each row names 8 different experts; within every aligned block of 128 tokens no expert is named by more than 80 tokens, a bound that some block reaches.
All inputs are finite; a program needn't handle non-finite values.
Results may differ from a plain program's by a relative error of at most 0.006.
Values may be sent and summed in bfloat16 or wider, within the bound.
No kernel may reach another device: no remote copies, remote signals or barrier semaphores. Data moves between devices by JAX's collectives and lax.ppermute only.
A program may use at most 128 MiB of HBM per device.

v0:
```python
import jax
import jax.numpy as jnp
from jax import lax
from jax.sharding import PartitionSpec as P


def with_zero(values):
    return jnp.concatenate([values, jnp.zeros((1,) + values.shape[1:], values.dtype)], axis=0)


def block_positions(blocks, experts, slot_cap):
    labels = jnp.arange(experts, dtype=jnp.int32)
    hits = jnp.sum((blocks[..., None] == labels).astype(jnp.int32), axis=-2)
    before = jnp.cumsum(hits, axis=-2) - hits
    ranked = jnp.take_along_axis(before, blocks, axis=-1)
    return blocks * slot_cap + ranked


def invert(places, length):
    entries = places.shape[0]
    return (
        jnp.full((length,), entries, jnp.int32).at[places].set(jnp.arange(entries, dtype=jnp.int32))
    )


def expert_backward(rows_x, rows_dy, rows_p, gate_w, up_w, down_w, gate_in, up_in):
    gate_f = gate_in.astype(jnp.float32)
    up_f = up_in.astype(jnp.float32)
    logistic = jax.nn.sigmoid(gate_f)
    active = gate_f * logistic
    hidden = active * up_f
    back_rows = jnp.dot(rows_dy, down_w.T, preferred_element_type=jnp.float32)
    slot_dprob = jnp.sum(back_rows * hidden, axis=1).astype(jnp.bfloat16)
    weight = rows_p.astype(jnp.float32)[:, None]
    d_hidden = weight * back_rows
    d_up = (d_hidden * active).astype(jnp.bfloat16)
    d_gate = (d_hidden * up_f * logistic * (1.0 + gate_f * (1.0 - logistic))).astype(jnp.bfloat16)
    scaled = (weight * hidden).astype(jnp.bfloat16)
    slot_dx = (
        jnp.dot(d_gate, gate_w.T, preferred_element_type=jnp.float32)
        + jnp.dot(d_up, up_w.T, preferred_element_type=jnp.float32)
    ).astype(jnp.bfloat16)
    grad_gate = jnp.dot(rows_x.T, d_gate, preferred_element_type=jnp.float32).astype(jnp.bfloat16)
    grad_up = jnp.dot(rows_x.T, d_up, preferred_element_type=jnp.float32).astype(jnp.bfloat16)
    grad_down = jnp.dot(scaled.T, rows_dy, preferred_element_type=jnp.float32).astype(jnp.bfloat16)
    return (slot_dx, slot_dprob, grad_gate, grad_up, grad_down)


def local(tokens, grad_out, probs, routes, w_gate, w_up, w_down, gate_pre, up_pre):
    seq_count = lax.axis_size("seq")
    expert_count = lax.axis_size("expert")
    experts = seq_count * expert_count
    token_count = tokens.shape[0]
    chosen = probs.shape[1]
    width = tokens.shape[1]
    slot_cap = gate_pre.shape[1] // experts
    seq_place = lax.axis_index("seq")
    places = block_positions(routes.reshape(seq_count, token_count, chosen), experts, slot_cap)
    own_places = lax.dynamic_index_in_dim(places, seq_place, 0, keepdims=False)
    lookup = invert(own_places.reshape(-1), experts * slot_cap)
    row_index = lookup // chosen
    send_x = with_zero(tokens)[row_index].reshape(experts, slot_cap, width)
    send_dy = with_zero(grad_out)[row_index].reshape(experts, slot_cap, width)
    send_p = with_zero(probs.reshape(-1))[lookup].reshape(experts, slot_cap)
    got_x, got_dy, got_p = (
        lax.all_to_all(send_x, ("expert", "seq"), split_axis=0, concat_axis=0, tiled=True),
        lax.all_to_all(send_dy, ("expert", "seq"), split_axis=0, concat_axis=0, tiled=True),
        lax.all_to_all(send_p, ("expert", "seq"), split_axis=0, concat_axis=0, tiled=True),
    )
    slot_dx, slot_dprob, grad_gate, grad_up, grad_down = expert_backward(
        got_x.reshape(-1, width),
        got_dy.reshape(-1, width),
        got_p.reshape(-1),
        w_gate[0],
        w_up[0],
        w_down[0],
        gate_pre[0],
        up_pre[0],
    )
    back_x, back_p = (
        lax.all_to_all(
            slot_dx.reshape(experts, slot_cap, width),
            ("expert", "seq"),
            split_axis=0,
            concat_axis=0,
            tiled=True,
        ),
        lax.all_to_all(
            slot_dprob.reshape(experts, slot_cap),
            ("expert", "seq"),
            split_axis=0,
            concat_axis=0,
            tiled=True,
        ),
    )
    flat_x = back_x.reshape(-1, width)
    summed = jnp.zeros((token_count, width), jnp.float32)
    for column in range(chosen):
        summed = summed + flat_x[own_places[:, column]].astype(jnp.float32)
    grad_tokens = summed.astype(jnp.bfloat16)
    grad_probs = back_p.reshape(-1)[own_places]
    return (grad_tokens, grad_probs, grad_gate[None], grad_up[None], grad_down[None])


def solution(mesh):
    return jax.shard_map(
        local,
        mesh=mesh,
        in_specs=(
            P(("group", "expert", "seq"), None),
            P(("group", "expert", "seq"), None),
            P(("group", "expert", "seq"), None),
            P(("group", "expert"), None),
            P(("expert", "seq"), None, None),
            P(("expert", "seq"), None, None),
            P(("expert", "seq"), None, None),
            P(("group", "expert", "seq"), None, None),
            P(("group", "expert", "seq"), None, None),
        ),
        out_specs=(
            P(("group", "expert", "seq"), None),
            P(("group", "expert", "seq"), None),
            P(("group", "expert", "seq"), None, None),
            P(("group", "expert", "seq"), None, None),
            P(("group", "expert", "seq"), None, None),
        ),
        check_vma=False,
    )
```

profile of v0, /device:TPU:0, one launch (start us, length us, event | category | flops | bytes accessed | tf_op | source)
XLA Modules:
  0.0 488.9 jit_solution(16145992555323394870)
XLA Ops:
  0.7 0.9 copy.45
  1.6 0.1 reshape.177
  1.7 0.8 copy.46
  2.5 0.8 copy.50
  3.4 0.1 fusion.32
  3.5 0.1 reshape.287
  3.6 0.1 copy.47
  3.8 0.1 copy.48
  3.9 0.3 reduce_window_sum.11
  4.2 34.4 %gather_fusion.12 = s32[4096]{0:T(1024)S(1)} fusion(s32[4,128,16]{2,1,0:T(8,128)S(1)} %sub.12, s32[4096]{0:T(1024)S(1)} %reshape.287), kind=kCustom, calls=%fused_computation.12 | custom fusion | bytes 81920 | tf_op jit(solution)/shard_map/jit(take_along_axis)/gather | solution.py:15
  38.5 0.2 reshape.290
  38.7 0.7 compare_select_fusion.1
  39.4 0.1 reshape.180
  39.5 4.3 scatter_custom_fusion
  43.9 8.0 %gather_fusion = bf16[1280]{0:T(1024)(128)(2,1)S(1)} fusion(bf16[1025]{0:T(1024)(128)(2,1)S(1)} %pad_maximum_fusion, s32[2048]{0:T(1024)S(1)} %get-tuple-element.41), kind=kCustom, calls=%fused_computation | custom fusion | bytes 10240 | tf_op jit(solution)/shard_map/gather | solution.py:64
  51.9 0.7 all_to_all.25
  52.6 7.4 %all-to-all-start = ((bf16[16,1,80]{2,1,0:T(2,128)(2,1)}), bf16[16,1,80]{2,1,0:T(2,128)(2,1)S(1)}, u32[]{:S(2)}, u32[]{:S(2)}) async-start(bf16[16,1,80]{2,1,0:T(2,128)(2,1)} %all_to_all.25), calls=%async_computation | async-start | bytes 16384 | tf_op jit(solution)/shard_map/all_to_all | solution.py:68
  60.0 6.2 %gather_fusion.1 = bf16[1280,2048]{1,0:T(8,128)(2,1)} fusion(bf16[129,2048]{1,0:T(8,128)(2,1)S(1)} %concatenate.10, s32[2048]{0:T(1024)S(1)} %get-tuple-element.40), kind=kCustom, calls=%fused_computation.1 | custom fusion | bytes 10490880 | tf_op jit(solution)/shard_map/gather | solution.py:63
  66.2 6.1 %all-to-all-start.1 = ((bf16[16,80,2048]{2,1,0:T(8,128)(2,1)}), bf16[16,80,2048]{2,1,0:T(8,128)(2,1)}, u32[]{:S(2)}, u32[]{:S(2)}) async-start(bf16[16,80,2048]{2,1,0:T(8,128)(2,1)} %bitcast.106), calls=%async_computation.1 | async-start | bytes 10485760 | tf_op jit(solution)/shard_map/all_to_all | solution.py:67
  72.4 6.2 %gather_fusion.11 = bf16[1280,2048]{1,0:T(8,128)(2,1)} fusion(bf16[129,2048]{1,0:T(8,128)(2,1)S(1)} %concatenate.11, s32[2048]{0:T(1024)S(1)} %get-tuple-element.40), kind=kCustom, calls=%fused_computation.11 | custom fusion | bytes 10490880 | tf_op jit(solution)/shard_map/gather | solution.py:62
  78.6 110.6 %all-to-all-done.1 = bf16[16,80,2048]{2,1,0:T(8,128)(2,1)} async-done(((bf16[16,80,2048]{2,1,0:T(8,128)(2,1)}), bf16[16,80,2048]{2,1,0:T(8,128)(2,1)}, u32[]{:S(2)}, u32[]{:S(2)}) %all-to-all-start.1) | async-done | bytes 5242912 | tf_op jit(solution)/shard_map/all_to_all | solution.py:67
  189.3 4.7 all-to-all-start.4
  194.0 1.3 copy.55
  195.4 0.6 copy.54
  196.1 7.8 %fusion.12 = (bf16[1280]{0:T(1024)(128)(2,1)S(1)}, bf16[1280,384]{0,1:T(8,128)(2,1)}, bf16[1280,384]{0,1:T(8,128)(2,1)}) fusion(bf16[1,1280,384]{1,2,0:T(8,128)(2,1)S(1)} %copy.54, bf16[1,1280,384]{1,2,0:T(8,128)(2,1)} %copy.55, f32[1280]{0:T(1024)S(1)} %reshape.188, bf16[1280,2048]{1,0:T(8,128)(2,1)} %bitcast.4, bf16[1,384,2048]{2,1,0:T(8,128)(2,1)} %param.15), kind=kOutput, calls=%fused_computation.35 | convolution fusion | flops 2022603520 | bytes 10755584 | tf_op jit(solution)/shard_map/dot_general | solution.py:32
  203.9 0.7 convert_element_type.127
  204.6 7.0 %fusion.23 = f32[1280,2048]{1,0:T(8,128)} fusion(bf16[1280,384]{0,1:T(8,128)(2,1)} %get-tuple-element.28, bf16[1,2048,384]{2,1,0:T(8,128)(2,1)S(1)} %copy-done), kind=kOutput, calls=%fused_computation.47 | convolution fusion | flops 2013265920 | bytes 13041664 | tf_op jit(solution)/shard_map/dot_general | solution.py:40
  211.6 99.3 %all-to-all-done.4 = bf16[16,80,2048]{2,1,0:T(8,128)(2,1)} async-done(((bf16[16,80,2048]{2,1,0:T(8,128)(2,1)}), bf16[16,80,2048]{2,1,0:T(8,128)(2,1)}, u32[]{:S(2)}, u32[]{:S(2)}) %all-to-all-start.4) | async-done | bytes 5242912 | tf_op jit(solution)/shard_map/all_to_all | solution.py:66
  310.9 3.7 all-to-all-start.3
  314.5 7.5 %add_convert_fusion = bf16[1280,2048]{1,0:T(8,128)(2,1)} fusion(f32[1280,2048]{1,0:T(8,128)} %fusion.23, bf16[1280,384]{0,1:T(8,128)(2,1)} %get-tuple-element.29, bf16[1,2048,384]{2,1,0:T(8,128)(2,1)S(1)} %copy-done.1), kind=kOutput, calls=%fused_computation.14 | convolution fusion | flops 2018508800 | bytes 18284544 | tf_op jit(solution)/shard_map/dot_general | solution.py:41
  322.0 6.0 %all-to-all-start.2 = ((bf16[16,80,2048]{2,1,0:T(8,128)(2,1)}), bf16[16,80,2048]{2,1,0:T(8,128)(2,1)}, u32[]{:S(2)}, u32[]{:S(2)}) async-start(bf16[16,80,2048]{2,1,0:T(8,128)(2,1)} %bitcast.107), calls=%async_computation.2 | async-start | bytes 10485760 | tf_op jit(solution)/shard_map/all_to_all | solution.py:81
  328.1 0.1 reshape.273
  328.3 6.7 %fusion.4 = bf16[1,2048,384]{2,1,0:T(8,128)(2,1)} fusion(bf16[1280,2048]{1,0:T(8,128)(2,1)} %bitcast.23, bf16[1280,384]{0,1:T(8,128)(2,1)S(1)} %copy-done.8), kind=kOutput, calls=%fused_computation.25 | convolution fusion | flops 2014052352 | bytes 7798784 | tf_op jit(solution)/shard_map/dot_general | solution.py:44
  335.0 6.7 %fusion.3 = bf16[1,2048,384]{2,1,0:T(8,128)(2,1)} fusion(bf16[1280,2048]{1,0:T(8,128)(2,1)} %bitcast.23, bf16[1280,384]{0,1:T(8,128)(2,1)S(1)} %copy-done.7), kind=kOutput, calls=%fused_computation.24 | convolution fusion | flops 2014052352 | bytes 7798784 | tf_op jit(solution)/shard_map/dot_general | solution.py:43
  341.7 6.1 %fusion.5 = bf16[1,384,2048]{2,1,0:T(8,128)(2,1)} fusion(bf16[1280,2048]{1,0:T(8,128)(2,1)} %bitcast.4, bf16[1,1280,384]{1,2,0:T(8,128)(2,1)S(1)} %copy-done.6, bf16[1,1280,384]{1,2,0:T(8,128)(2,1)S(1)} %copy-done.4, f32[1280]{0:T(1024)S(1)} %reshape.188), kind=kOutput, calls=%fused_computation.26 | convolution fusion | flops 2018476032 | bytes 8786944 | tf_op jit(solution)/shard_map/dot_general | solution.py:45
  347.9 7.0 %gather_fusion.10 = bf16[1024]{0:T(1024)(128)(2,1)S(1)} fusion(bf16[1280]{0:T(1024)(128)(2,1)S(1)} %reshape.185, s32[1024]{0:T(1024)S(1)} %broadcast_clamp_fusion), kind=kCustom, calls=%fused_computation.10 | custom fusion | bytes 8192 | tf_op jit(solution)/shard_map/gather | solution.py:101
  354.9 0.1 reshape.272
  355.0 0.7 copy.58
  355.7 89.2 %all-to-all-done.2 = bf16[16,80,2048]{2,1,0:T(8,128)(2,1)} async-done(((bf16[16,80,2048]{2,1,0:T(8,128)(2,1)}), bf16[16,80,2048]{2,1,0:T(8,128)(2,1)}, u32[]{:S(2)}, u32[]{:S(2)}) %all-to-all-start.2) | async-done | bytes 5242912 | tf_op jit(solution)/shard_map/all_to_all | solution.py:81
  444.9 4.6 gather_fusion.9
  449.5 4.6 gather_fusion.8
  454.1 4.6 gather_fusion.7
  458.7 5.4 %gather_fusion.6 = bf16[128,2048]{1,0:T(8,128)(2,1)} fusion(bf16[1280,2048]{1,0:T(8,128)(2,1)} %bitcast.11, s32[1024]{0:T(1024)S(1)} %get-tuple-element.45), kind=kCustom, calls=%fused_computation.6 | custom fusion | bytes 1049088 | tf_op jit(solution)/shard_map/gather | solution.py:99
  464.1 5.4 %gather_fusion.5 = bf16[128,2048]{1,0:T(8,128)(2,1)} fusion(bf16[1280,2048]{1,0:T(8,128)(2,1)} %bitcast.11, s32[1024]{0:T(1024)S(1)} %get-tuple-element.46), kind=kCustom, calls=%fused_computation.5 | custom fusion | bytes 1049088 | tf_op jit(solution)/shard_map/gather | solution.py:99
  469.6 5.4 %gather_fusion.4 = bf16[128,2048]{1,0:T(8,128)(2,1)} fusion(bf16[1280,2048]{1,0:T(8,128)(2,1)} %bitcast.11, s32[1024]{0:T(1024)S(1)} %get-tuple-element.47), kind=kCustom, calls=%fused_computation.4 | custom fusion | bytes 1049088 | tf_op jit(solution)/shard_map/gather | solution.py:99
  475.0 5.4 %gather_fusion.3 = bf16[128,2048]{1,0:T(8,128)(2,1)} fusion(bf16[1280,2048]{1,0:T(8,128)(2,1)} %bitcast.11, s32[1024]{0:T(1024)S(1)} %get-tuple-element.48), kind=kCustom, calls=%fused_computation.3 | custom fusion | bytes 1049088 | tf_op jit(solution)/shard_map/gather | solution.py:99
  480.4 5.4 %gather_fusion.2 = bf16[128,2048]{1,0:T(8,128)(2,1)} fusion(bf16[1280,2048]{1,0:T(8,128)(2,1)} %bitcast.11, s32[1024]{0:T(1024)S(1)} %get-tuple-element.49), kind=kCustom, calls=%fused_computation.2 | custom fusion | bytes 1049088 | tf_op jit(solution)/shard_map/gather | solution.py:99
  485.8 3.1 add_convert_fusion.1
  (50 shorter events, 0.7 us)
Async XLA Ops:
  0.6 204.0 %copy-start = (bf16[1,2048,384]{2,1,0:T(8,128)(2,1)S(1)}, bf16[1,2048,384]{2,1,0:T(8,128)(2,1)}, u32[]{:S(2)}) copy-start(bf16[1,2048,384]{2,1,0:T(8,128)(2,1)} %param.13) | copy-start | bytes 4718596
  39.4 4.4 copy-start.9
  43.9 16.0 %copy-start.11 = (bf16[128,2048]{1,0:T(8,128)(2,1)S(1)}, bf16[128,2048]{1,0:T(8,128)(2,1)}, u32[]{:S(2)}) copy-start(bf16[128,2048]{1,0:T(8,128)(2,1)} %param.10) | copy-start | bytes 1572868
  52.6 13.7 %all-to-all-start = ((bf16[16,1,80]{2,1,0:T(2,128)(2,1)}), bf16[16,1,80]{2,1,0:T(2,128)(2,1)S(1)}, u32[]{:S(2)}, u32[]{:S(2)}) async-start(bf16[16,1,80]{2,1,0:T(2,128)(2,1)} %all_to_all.25), calls=%async_computation | async-start | bytes 16384 | tf_op jit(solution)/shard_map/all_to_all | solution.py:68
  66.2 6.1 %copy-start.12 = (bf16[128,2048]{1,0:T(8,128)(2,1)S(1)}, bf16[128,2048]{1,0:T(8,128)(2,1)}, u32[]{:S(2)}) copy-start(bf16[128,2048]{1,0:T(8,128)(2,1)} %param.9) | copy-start | bytes 1572868
  66.2 123.0 %all-to-all-start.1 = ((bf16[16,80,2048]{2,1,0:T(8,128)(2,1)}), bf16[16,80,2048]{2,1,0:T(8,128)(2,1)}, u32[]{:S(2)}, u32[]{:S(2)}) async-start(bf16[16,80,2048]{2,1,0:T(8,128)(2,1)} %bitcast.106), calls=%async_computation.1 | async-start | bytes 10485760 | tf_op jit(solution)/shard_map/all_to_all | solution.py:67
  189.3 4.7 copy-start.2
  189.3 121.6 %all-to-all-start.4 = ((bf16[16,80,2048]{2,1,0:T(8,128)(2,1)}), bf16[16,80,2048]{2,1,0:T(8,128)(2,1)}, u32[]{:S(2)}, u32[]{:S(2)}) async-start(bf16[16,80,2048]{2,1,0:T(8,128)(2,1)} %bitcast.105), calls=%async_computation.4 | async-start | bytes 10485760 | tf_op jit(solution)/shard_map/all_to_all | solution.py:66
  194.0 1.3 copy-start.3
  196.0 7.9 %copy-start.5 = (bf16[1,1280,384]{1,2,0:T(8,128)(2,1)}, bf16[1,1280,384]{1,2,0:T(8,128)(2,1)S(1)}, u32[]{:S(2)}) copy-start(bf16[1,1280,384]{1,2,0:T(8,128)(2,1)S(1)} %copy.54) | copy-start | bytes 2949124
  204.6 109.9 %copy-start.1 = (bf16[1,2048,384]{2,1,0:T(8,128)(2,1)S(1)}, bf16[1,2048,384]{2,1,0:T(8,128)(2,1)}, u32[]{:S(2)}) copy-start(bf16[1,2048,384]{2,1,0:T(8,128)(2,1)} %param.14) | copy-start | bytes 4718596
  310.9 11.2 %all-to-all-start.3 = ((bf16[16,1,80]{2,1,0:T(2,128)(2,1)}), bf16[16,1,80]{2,1,0:T(2,128)(2,1)S(1)}, u32[]{:S(2)}, u32[]{:S(2)}) async-start(bf16[16,1,80]{2,1,0:T(2,128)(2,1)} %convert_element_type.127), calls=%async_computation.3 | async-start | bytes 16384 | tf_op jit(solution)/shard_map/all_to_all | solution.py:88
  322.0 6.0 %copy-start.10 = (s32[1,128,8]{2,1,0:T(8,128)S(1)}, s32[1,128,8]{2,1,0:T(8,128)}, u32[]{:S(2)}) copy-start(s32[1,128,8]{2,1,0:T(8,128)} %copy-done.9) | copy-start | bytes 12292
  322.0 6.0 %copy-start.13 = (s32[128,8,1]{1,0,2:T(8,128)S(1)}, s32[128,8,1]{1,0,2:T(8,128)}, u32[]{:S(2)}) copy-start(s32[128,8,1]{1,0,2:T(8,128)} %get-tuple-element.25) | copy-start | bytes 12292
  322.0 6.2 %copy-start.8 = (bf16[1280,384]{0,1:T(8,128)(2,1)S(1)}, bf16[1280,384]{0,1:T(8,128)(2,1)}, u32[]{:S(2)}) copy-start(bf16[1280,384]{0,1:T(8,128)(2,1)} %get-tuple-element.29) | copy-start | bytes 2949124
  322.0 122.9 %all-to-all-start.2 = ((bf16[16,80,2048]{2,1,0:T(8,128)(2,1)}), bf16[16,80,2048]{2,1,0:T(8,128)(2,1)}, u32[]{:S(2)}, u32[]{:S(2)}) async-start(bf16[16,80,2048]{2,1,0:T(8,128)(2,1)} %bitcast.107), calls=%async_computation.2 | async-start | bytes 10485760 | tf_op jit(solution)/shard_map/all_to_all | solution.py:81
  328.3 6.7 %copy-start.7 = (bf16[1280,384]{0,1:T(8,128)(2,1)S(1)}, bf16[1280,384]{0,1:T(8,128)(2,1)}, u32[]{:S(2)}) copy-start(bf16[1280,384]{0,1:T(8,128)(2,1)} %get-tuple-element.28) | copy-start | bytes 2949124
  335.0 6.7 %copy-start.4 = (bf16[1,1280,384]{1,2,0:T(8,128)(2,1)S(1)}, bf16[1,1280,384]{1,2,0:T(8,128)(2,1)}, u32[]{:S(2)}) copy-start(bf16[1,1280,384]{1,2,0:T(8,128)(2,1)} %copy.55) | copy-start | bytes 2949124
  335.0 6.7 %copy-start.6 = (bf16[1,1280,384]{1,2,0:T(8,128)(2,1)S(1)}, bf16[1,1280,384]{1,2,0:T(8,128)(2,1)}, u32[]{:S(2)}) copy-start(bf16[1,1280,384]{1,2,0:T(8,128)(2,1)} %copy-done.5) | copy-start | bytes 2949124
where the time goes:
time: 490 us; the launch traced here: 489 us
  waiting for transfers between devices  299 us (61%)
  local copies, waits for them, and re-layouts  115 us (23%)
  matrix products  41.7 us (9%)
  starting transfers between devices  27.8 us (6%)
    all_to_all x1, waiting for transfers between devices, local(): lax.all_to_all(send_dy, ('expert', 'seq'), split_axis=0, concat_axis=0, t...  111 us
    all_to_all x1, waiting for transfers between devices, local(): lax.all_to_all(send_x, ('expert', 'seq'), split_axis=0, concat_axis=0, ti...  99.3 us
    all_to_all x1, waiting for transfers between devices, local(): lax.all_to_all(slot_dx.reshape(experts, slot_cap, width), ('expert', 'seq...  89.2 us
    gather x8, local copies, waits for them, and re-layouts, local(): summed = summed + flat_x[own_places[:, column]].astype(jnp.float32)  40.8 us
    gather x3, local copies, waits for them, and re-layouts, block_positions(): ranked = jnp.take_along_axis(before, blocks, axis=-1)  34.7 us
  transfers between devices with their start and end apart: 5, of which 4 were waited for; matrix products, arithmetic and copies ran while one was open for 13% of the time, Pallas kernels for 0%

commit v1 on v0

--- a/solution.py
+++ b/solution.py
@@ -1,6 +1,10 @@
+import functools
+
 import jax
 import jax.numpy as jnp
 from jax import lax
+from jax.experimental import pallas as pl
+from jax.experimental.pallas import tpu as pltpu
 from jax.sharding import PartitionSpec as P
 
 
@@ -46,7 +50,7 @@
     return (slot_dx, slot_dprob, grad_gate, grad_up, grad_down)
 
 
-def local(tokens, grad_out, probs, routes, w_gate, w_up, w_down, gate_pre, up_pre):
+def exchange_local(tokens, grad_out, probs, routes, w_gate, w_up, w_down, gate_pre, up_pre):
     seq_count = lax.axis_size("seq")
     expert_count = lax.axis_size("expert")
     experts = seq_count * expert_count
@@ -100,6 +104,297 @@
     grad_tokens = summed.astype(jnp.bfloat16)
     grad_probs = back_p.reshape(-1)[own_places]
     return (grad_tokens, grad_probs, grad_gate[None], grad_up[None], grad_down[None])
+
+
+TILE = 512
+
+
+def dot_nt(a, b):
+    return lax.dot_general(a, b, (((1,), (1,)), ((), ())), preferred_element_type=jnp.float32)
+
+
+def dot_tn(a, b):
+    return lax.dot_general(a, b, (((0,), (0,)), ((), ())), preferred_element_type=jnp.float32)
+
+
+def slot_hits(slot_ref, block, slot_cap):
+    slots = slot_ref[block]
+    shape = (slot_cap, slots.shape[1])
+    return lax.broadcasted_iota(jnp.int32, shape, 0) == jnp.broadcast_to(slots, shape)
+
+
+def as_bf16(hits):
+    return jnp.where(hits, 1.0, 0.0).astype(jnp.bfloat16)
+
+
+def round_kernel(
+    ids_ref, slot_ref, prob_ref, dy0, dy1, dy2, dy3, down_ref, gate_w_ref, up_w_ref, gate_ref, up_ref,
+    dx0, dx1, dx2, dx3, rows_ref, dgu_ref, scaled_ref, dprob_ref,
+    back_ref,
+):
+    pieces, results = (dy0, dy1, dy2, dy3), (dx0, dx1, dx2, dx3)
+    slot_cap, hid = gate_ref.shape[1:]
+    width = dy0.shape[1]
+    blocks = [ids_ref[i] for i in range(4)]
+    hits = [slot_hits(slot_ref, block, slot_cap) for block in blocks]
+    select = [as_bf16(h) for h in hits]
+    back_ref[...] = jnp.zeros_like(back_ref)
+
+    def project(step, carry):
+        cols = pl.ds(pl.multiple_of(step * TILE, TILE), TILE)
+        for i in range(4):
+            rows = jnp.dot(select[i], pieces[i][:, cols], preferred_element_type=jnp.float32)
+            rows_ref[i * slot_cap:(i + 1) * slot_cap, cols] = rows.astype(jnp.bfloat16)
+        back_ref[...] += dot_nt(rows_ref[:, cols], down_ref[:, cols])
+        return carry
+
+    lax.fori_loop(0, width // TILE, project, 0)
+    for i in range(4):
+        span = slice(i * slot_cap, (i + 1) * slot_cap)
+        gate_f = gate_ref[blocks[i]].astype(jnp.float32)
+        up_f = up_ref[blocks[i]].astype(jnp.float32)
+        back_rows = back_ref[span, :]
+        probs = jnp.broadcast_to(prob_ref[blocks[i]], hits[i].shape)
+        weight = jnp.sum(jnp.where(hits[i], probs, 0.0), axis=1, keepdims=True)
+        logistic = jax.nn.sigmoid(gate_f)
+        active = gate_f * logistic
+        hidden = active * up_f
+        dprob = jnp.sum(back_rows * hidden, axis=1, keepdims=True)
+        dprob = jnp.broadcast_to(dprob, hits[i].shape)
+        dprob_ref[i] = jnp.sum(jnp.where(hits[i], dprob, 0.0), axis=0, keepdims=True)
+        d_hidden = weight * back_rows
+        slope = logistic * (1.0 + gate_f * (1.0 - logistic))
+        dgu_ref[span, :hid] = (d_hidden * up_f * slope).astype(jnp.bfloat16)
+        dgu_ref[span, hid:] = (d_hidden * active).astype(jnp.bfloat16)
+        scaled_ref[span, :] = (weight * hidden).astype(jnp.bfloat16)
+
+    def unproject(step, carry):
+        cols = pl.ds(pl.multiple_of(step * TILE, TILE), TILE)
+        slot_dx = dot_nt(dgu_ref[:, :hid], gate_w_ref[cols, :])
+        slot_dx = (slot_dx + dot_nt(dgu_ref[:, hid:], up_w_ref[cols, :])).astype(jnp.bfloat16)
+        for i in range(4):
+            span = slice(i * slot_cap, (i + 1) * slot_cap)
+            results[i][:, cols] = dot_tn(select[i], slot_dx[span, :]).astype(jnp.bfloat16)
+        return carry
+
+    lax.fori_loop(0, width // TILE, unproject, 0)
+
+
+def round_backward(ids, slots, probs, pieces, down_w, gate_w, up_w, gate_in, up_in):
+    rows, width = pieces[0].shape
+    slot_cap, hid = gate_in.shape[1:]
+    taken = 4 * slot_cap
+    half = jnp.bfloat16
+    vmem = pl.BlockSpec(memory_space=pltpu.VMEM)
+    flops = 2 * taken * width * (3 * hid + 2 * rows)
+    moved = 2 * (3 * width * hid + 8 * rows * width + taken * (width + 5 * hid))
+    out = pl.pallas_call(
+        round_kernel,
+        out_shape=[jax.ShapeDtypeStruct((rows, width), half)] * 4
+        + [
+            jax.ShapeDtypeStruct((taken, width), half),
+            jax.ShapeDtypeStruct((taken, 2 * hid), half),
+            jax.ShapeDtypeStruct((taken, hid), half),
+            jax.ShapeDtypeStruct((4, 1, rows), jnp.float32),
+        ],
+        in_specs=[pl.BlockSpec(memory_space=pltpu.SMEM)] + [vmem] * 11,
+        out_specs=[vmem] * 8,
+        scratch_shapes=[pltpu.VMEM((taken, hid), jnp.float32)],
+        compiler_params=pltpu.CompilerParams(vmem_limit_bytes=48 << 20),
+        cost_estimate=pl.CostEstimate(flops=flops, bytes_accessed=moved, transcendentals=taken * hid),
+    )(ids, slots, probs, *pieces, down_w, gate_w, up_w, gate_in, up_in)
+    return out[:4], out[4], out[5], out[6], out[7]
+
+
+def weight_kernel(rounds, slot_cap, ids_ref, slot_ref, *refs):
+    count = 4 * rounds
+    pieces, rows = refs[:count], refs[count:count + rounds]
+    dgu, scaled = refs[count + rounds:count + 2 * rounds], refs[count + 2 * rounds:count + 3 * rounds]
+    gate_out, up_out, down_out, all_x, all_dy, all_dgu, all_scaled = refs[count + 3 * rounds:]
+    taken = 4 * slot_cap
+    hid = gate_out.shape[1]
+
+    @pl.when(pl.program_id(0) == 0)
+    def _():
+        for r in range(rounds):
+            all_dgu[r * taken:(r + 1) * taken, :] = dgu[r][...]
+            all_scaled[r * taken:(r + 1) * taken, :] = scaled[r][...]
+
+    for i in range(count):
+        select = as_bf16(slot_hits(slot_ref, ids_ref[i], slot_cap))
+        picked = jnp.dot(select, pieces[i][...], preferred_element_type=jnp.float32)
+        all_x[i * slot_cap:(i + 1) * slot_cap, :] = picked.astype(jnp.bfloat16)
+    for r in range(rounds):
+        all_dy[r * taken:(r + 1) * taken, :] = rows[r][...]
+    grads = dot_tn(all_x[...], all_dgu[...])
+    gate_out[...] = grads[:, :hid].astype(jnp.bfloat16)
+    up_out[...] = grads[:, hid:].astype(jnp.bfloat16)
+    down_out[...] = dot_tn(all_scaled[...], all_dy[...]).astype(jnp.bfloat16)
+
+
+def weight_grads(ids, slots, pieces, rows, dgu, scaled, slot_cap):
+    rounds, count = len(rows), len(pieces)
+    size, width = pieces[0].shape
+    taken, hid = scaled[0].shape
+    half = jnp.bfloat16
+
+    def columns(height):
+        return pl.BlockSpec((height, TILE), lambda i: (0, i))
+
+    def whole(shape):
+        return pl.BlockSpec(shape, lambda i: (0,) * len(shape))
+
+    total = rounds * taken
+    flops = 2 * total * width * (3 * hid + size)
+    moved = 2 * (count * size * width + total * (width + 3 * hid) + 3 * width * hid)
+    return pl.pallas_call(
+        functools.partial(weight_kernel, rounds, slot_cap),
+        grid=(width // TILE,),
+        out_shape=[
+            jax.ShapeDtypeStruct((width, hid), half),
+            jax.ShapeDtypeStruct((width, hid), half),
+            jax.ShapeDtypeStruct((hid, width), half),
+        ],
+        in_specs=[pl.BlockSpec(memory_space=pltpu.SMEM), whole(slots.shape)]
+        + [columns(size)] * count
+        + [columns(taken)] * rounds
+        + [whole((taken, 2 * hid))] * rounds
+        + [whole((taken, hid))] * rounds,
+        out_specs=[
+            pl.BlockSpec((TILE, hid), lambda i: (i, 0)),
+            pl.BlockSpec((TILE, hid), lambda i: (i, 0)),
+            columns(hid),
+        ],
+        scratch_shapes=[
+            pltpu.VMEM((total, TILE), half),
+            pltpu.VMEM((total, TILE), half),
+            pltpu.VMEM((total, 2 * hid), half),
+            pltpu.VMEM((total, hid), half),
+        ],
+        compiler_params=pltpu.CompilerParams(vmem_limit_bytes=56 << 20),
+        cost_estimate=pl.CostEstimate(flops=flops, bytes_accessed=moved, transcendentals=0),
+    )(ids, slots, *pieces, *rows, *dgu, *scaled)
+
+
+class Links:
+    def __init__(self, depth):
+        self.depth, self.arrived = depth, []
+
+    def send(self, value, axis, pairs):
+        if len(self.arrived) >= self.depth:
+            value = lax.optimization_barrier((value, self.arrived[-self.depth]))[0]
+        got = lax.ppermute(value, axis, pairs)
+        self.arrived.append(got)
+        return got
+
+
+def gather_local(tokens, grad_out, probs, routes, w_gate, w_up, w_down, gate_pre, up_pre):
+    seq_count = lax.axis_size("seq")
+    experts = seq_count * lax.axis_size("expert")
+    token_count, width = tokens.shape
+    chosen = probs.shape[1]
+    slot_cap = gate_pre.shape[1] // experts
+    seq_place, expert_place = lax.axis_index("seq"), lax.axis_index("expert")
+    core_pairs = [(i, i ^ 1) for i in range(4)]
+    side_pairs = [(i, i ^ 2) for i in range(4)]
+    shifts = sorted(range(seq_count), key=lambda s: (min(s, seq_count - s), s))
+    side, line = Links(2), Links(2)
+
+    def shift(value, by):
+        return line.send(value, "seq", [(i, (i + by) % seq_count) for i in range(seq_count)])
+
+    def across(value):
+        return side.send(value, "expert", side_pairs)
+
+    def other_core(value):
+        return lax.ppermute(value, "expert", core_pairs)
+
+    def block_of(s):
+        place = (seq_place - s) % seq_count
+        return [(expert_place ^ flip) * seq_count + place for flip in (0, 2, 1, 3)]
+
+    ids = {s: jnp.stack(block_of(s)).astype(jnp.int32) for s in shifts}
+
+    dy, x = {0: grad_out}, {0: tokens}
+    dy_side, x_side = {}, {}
+    for s in shifts[1:3]:
+        dy[s] = shift(grad_out, s)
+    dy_side[0] = across(grad_out)
+    x_side[0] = across(tokens)
+
+    own_routes = lax.dynamic_slice_in_dim(routes, seq_place * token_count, token_count, 0)
+    labels = jnp.arange(experts, dtype=jnp.int32)
+    match = own_routes[:, :, None] == labels
+    hits = jnp.sum(match.astype(jnp.int32), axis=1)
+    before = jnp.cumsum(hits, axis=0) - hits
+    slot_of = jnp.where(hits > 0, before, -1).astype(jnp.bfloat16)
+    prob_of = jnp.sum(jnp.where(match, probs[:, :, None], 0), axis=1).astype(jnp.bfloat16)
+    info = jnp.stack([slot_of.T, prob_of.T], axis=1)
+    info = lax.all_to_all(info, ("expert", "seq"), split_axis=0, concat_axis=0, tiled=True)
+    slots = info[:, :1, :].astype(jnp.int32)
+    probs_in = info[:, 1:, :].astype(jnp.float32)
+
+    gate_in = gate_pre.reshape(experts, slot_cap, -1)
+    up_in = up_pre.reshape(experts, slot_cap, -1)
+    for s in shifts[3:]:
+        dy[s] = shift(grad_out, s)
+    rows, dgu, scaled, dprob, own, away, sums = {}, {}, {}, {}, {}, {}, {}
+
+    def start_return(s):
+        pieces = (dy[s], dy_side[s], other_core(dy[s]), other_core(dy_side[s]))
+        dx, rows[s], dgu[s], scaled[s], dprob[s] = round_backward(
+            ids[s], slots, probs_in, pieces, w_down[0], w_gate[0], w_up[0], gate_in, up_in
+        )
+        own[s] = (dx[0], other_core(dx[2]))
+        away[s] = add(dx[1], other_core(dx[3]))
+
+    def add(*terms):
+        total = terms[0].astype(jnp.float32)
+        for term in terms[1:]:
+            total = total + term.astype(jnp.float32)
+        return total.astype(jnp.bfloat16)
+
+    for s in shifts[1:]:
+        dy_side[s] = across(dy[s])
+    for s in shifts[1:]:
+        x[s] = shift(tokens, s)
+    for s in shifts:
+        start_return(s)
+        arrived = across(away[s])
+        sums[s] = (*own[s], arrived)
+        if s:
+            sums[s] = (shift(add(*sums[s]), -s),)
+    for s in shifts[1:]:
+        x_side[s] = across(x[s])
+    grad_tokens = add(*[term for s in shifts for term in sums[s]])
+
+    pieces = []
+    for s in shifts:
+        pieces += [x[s], x_side[s], other_core(x[s]), other_core(x_side[s])]
+    grad_gate, grad_up, grad_down = weight_grads(
+        jnp.concatenate([ids[s] for s in shifts]),
+        slots,
+        pieces,
+        [rows[s] for s in shifts],
+        [dgu[s] for s in shifts],
+        [scaled[s] for s in shifts],
+        slot_cap,
+    )
+    order = jnp.concatenate([ids[s] for s in shifts])
+    dense = jnp.concatenate([dprob[s] for s in shifts], axis=0)[:, 0, :]
+    placed = jnp.sum(jnp.where((labels[:, None] == order)[:, :, None], dense, 0.0), axis=1)
+    back = lax.all_to_all(
+        placed.astype(jnp.bfloat16)[:, None, :], ("expert", "seq"), split_axis=0, concat_axis=0, tiled=True
+    )
+    grad_probs = jnp.sum(jnp.where(match, back[:, 0, :].T[:, None, :], 0), axis=2).astype(jnp.bfloat16)
+    return (grad_tokens, grad_probs, grad_gate[None], grad_up[None], grad_down[None])
+
+
+def local(tokens, grad_out, probs, routes, w_gate, w_up, w_down, gate_pre, up_pre):
+    experts = lax.axis_size("seq") * lax.axis_size("expert")
+    gathers = experts * tokens.shape[0] <= 2 * gate_pre.shape[1]
+    plan = gather_local if gathers and lax.axis_size("expert") == 4 else exchange_local
+    return plan(tokens, grad_out, probs, routes, w_gate, w_up, w_down, gate_pre, up_pre)
 
 
 def solution(mesh):

time: 490 us -> 225 us (0.46)
  waiting for transfers between devices: 299 us -> 71.4 us
  local copies, waits for them, and re-layouts: 115 us -> 11.9 us
  Pallas kernels: 0 us -> 48.2 us
  matrix products: 41.7 us -> 0 us
  blocking collectives: 0 us -> 33.2 us
  starting transfers between devices: 27.8 us -> 47.3 us
  other arithmetic: 4.35 us -> 11.4 us
    all_to_all x5 -> x1, waiting for transfers between devices: 299 us -> 19.4 us  [gather_local(): lax.all_to_all(info, ('expert', 'seq'), split_axis=0, concat_axis=0, tile...]
    gather x16 -> x0, local copies, waits for them, and re-layouts: 103 us -> none  [the longest x8 40.8 us: local(): summed = summed + flat_x[own_places[:, column]].astype(jnp.float32)]
    ppermute x0 -> x45, waiting for transfers between devices: none -> 52 us  [the longest x21 49.5 us: send(): got = lax.ppermute(value, axis, pairs)]
    pallas_call x0 -> x5, Pallas kernels: none -> 48.2 us  [the longest x4 35.5 us: round_backward(): pl.pallas_call(round_kernel, out_shape=[jax.ShapeDtypeStruct((rows, width...]
    ppermute x0 -> x45, starting transfers between devices: none -> 42.1 us  [the longest x21 37.6 us: send(): got = lax.ppermute(value, axis, pairs)]
    dot_general x6 -> x0, matrix products: 41.7 us -> none  [the longest x1 7.82 us: expert_backward(): back_rows = jnp.dot(rows_dy, down_w.T, preferred_element_type=jnp.float32)]
    all_to_all x0 -> x1, blocking collectives: none -> 33.2 us  [gather_local(): lax.all_to_all(placed.astype(jnp.bfloat16)[:, None, :], ('expert', 'seq')...]
    all_to_all x5 -> x1, starting transfers between devices: 27.8 us -> 5.19 us  [gather_local(): lax.all_to_all(info, ('expert', 'seq'), split_axis=0, concat_axis=0, tile...]
  transfers between devices with their start and end apart: 5 -> 46, of which waited for: 4 -> 12; matrix products, arithmetic and copies ran while one was open for 13% -> 5% of each run, Pallas kernels for 0% -> 16%
where the time goes in v1:
time: 225 us
  waiting for transfers between devices  71.4 us (32%)
  Pallas kernels  48.2 us (21%)
  starting transfers between devices  47.3 us (21%)
  blocking collectives  33.2 us (15%)
  local copies, waits for them, and re-layouts  11.9 us (5%)
  other arithmetic  11.4 us (5%)
    ppermute x21, waiting for transfers between devices, send(): got = lax.ppermute(value, axis, pairs)  49.5 us
    ppermute x21, starting transfers between devices, send(): got = lax.ppermute(value, axis, pairs)  37.6 us
    pallas_call x4, Pallas kernels, round_backward(): pl.pallas_call(round_kernel, out_shape=[jax.ShapeDtypeStruct((rows, width...  35.5 us
    all_to_all x1, blocking collectives, gather_local(): lax.all_to_all(placed.astype(jnp.bfloat16)[:, None, :], ('expert', 'seq')...  33.2 us
    all_to_all x1, waiting for transfers between devices, gather_local(): lax.all_to_all(info, ('expert', 'seq'), split_axis=0, concat_axis=0, tile...  19.4 us
    pallas_call x1, Pallas kernels, weight_grads(): pl.pallas_call(functools.partial(weight_kernel, rounds, slot_cap), grid=(...  12.7 us
    unnamed x79, local copies, waits for them, and re-layouts  11.6 us
    convert_element_type x8, other arithmetic, add(): return total.astype(jnp.bfloat16)  8.84 us
  transfers between devices with their start and end apart: 46, of which 12 were waited for; matrix products, arithmetic and copies ran while one was open for 5% of the time, Pallas kernels for 16%

profile of v1, /device:TPU:0, one launch (start us, length us, event | category | flops | bytes accessed | tf_op | source)
XLA Modules:
  0.0 224.6 jit_solution(17219263815642213010)
XLA Ops:
  0.6 3.1 %collective-permute-start.9 = (bf16[128,2048]{1,0:T(8,128)(2,1)}, bf16[128,2048]{1,0:T(8,128)(2,1)S(1)}, u32[]{:S(2)}, u32[]{:S(2)}) collective-permute-start(bf16[128,2048]{1,0:T(8,128)(2,1)} %dy0.1), channel_id=1, source_target_pairs={{0,1},{1,2},{2,3},{3,0},{4,5},{5,6},{6,7},{7,4},{8,9},{9,10},{10,1... | collective-permute-start | bytes 1572872 | tf_op jit(solution)/shard_map/ppermute | solution.py:286
  3.7 1.5 collective-permute-start
  5.2 2.2 %collective-permute-start.5 = (bf16[128,2048]{1,0:T(8,128)(2,1)}, bf16[128,2048]{1,0:T(8,128)(2,1)S(1)}, u32[]{:S(2)}, u32[]{:S(2)}) collective-permute-start(bf16[128,2048]{1,0:T(8,128)(2,1)} %dy0.1), channel_id=1, source_target_pairs={{0,3},{1,0},{2,1},{3,2},{4,7},{5,4},{6,5},{7,6},{8,11},{9,8},{10,9... | collective-permute-start | bytes 1572872 | tf_op jit(solution)/shard_map/ppermute | solution.py:286
  8.2 10.5 %collective-permute-done.9.dy0 = bf16[128,2048]{1,0:T(8,128)(2,1)S(1)} collective-permute-done((bf16[128,2048]{1,0:T(8,128)(2,1)}, bf16[128,2048]{1,0:T(8,128)(2,1)S(1)}, u32[]{:S(2)}, u32[]{:S(2)}) %collective-permute-start.9) | collective-permute-done | bytes 524320 | tf_op jit(solution)/shard_map/ppermute | solution.py:286
  18.8 16.7 %collective-permute-start.15 = (bf16[128,2048]{1,0:T(8,128)(2,1)}, bf16[128,2048]{1,0:T(8,128)(2,1)S(1)}, u32[]{:S(2)}, u32[]{:S(2)}) collective-permute-start(bf16[128,2048]{1,0:T(8,128)(2,1)} %dy0.1), channel_id=1, source_target_pairs={{0,2},{1,3},{2,0},{3,1},{4,6},{5,7},{6,4},{7,5},{8,10},{9,11},{10,... | collective-permute-start | bytes 1572872 | tf_op jit(solution)/shard_map/ppermute | solution.py:286
  35.5 1.5 collective-permute-start.10
  37.0 0.8 copy-done.4
  39.2 5.2 %all-to-all-start = ((bf16[16,2,128]{2,1,0:T(2,128)(2,1)}), bf16[16,2,128]{2,1,0:T(2,128)(2,1)S(1)}, u32[]{:S(2)}, u32[]{:S(2)}) async-start(bf16[16,2,128]{2,1,0:T(2,128)(2,1)} %pad_maximum_fusion), calls=%async_computation | async-start | bytes 16384 | tf_op jit(solution)/shard_map/all_to_all | solution.py:333
  44.5 19.4 %all-to-all-done = bf16[16,2,128]{2,1,0:T(2,128)(2,1)S(1)} async-done(((bf16[16,2,128]{2,1,0:T(2,128)(2,1)}), bf16[16,2,128]{2,1,0:T(2,128)(2,1)S(1)}, u32[]{:S(2)}, u32[]{:S(2)}) %all-to-all-start) | async-done | bytes 8224 | tf_op jit(solution)/shard_map/all_to_all | solution.py:333
  64.6 0.8 copy-done.8
  65.4 1.4 collective-permute-start.16
  67.0 1.2 copy-done.1
  68.2 1.0 copy-done.3
  69.3 1.0 copy-done.5
  70.3 1.0 copy-done.9
  71.4 9.0 %shard_map.128 = (bf16[128,2048]{1,0:T(8,128)(2,1)S(1)}, bf16[128,2048]{1,0:T(8,128)(2,1)S(1)}, bf16[128,2048]{1,0:T(8,128)(2,1)S(1)}, bf16[128,2048]{1,0:T(8,12...) custom-call(s32[4]{0:T(128)S(1)} %pad_add_fusion.ids_ref, ...), custom_call_target="tpu_custom_call" | custom-call | flops 1845493760 | bytes 11452416 | tf_op jit(solution)/shard_map/pallas_call | solution.py:191
  80.3 0.8 copy-done.6
  81.1 0.8 copy-done.13
  81.9 0.8 copy-done.15
  84.7 8.8 %shard_map.129 = (bf16[128,2048]{1,0:T(8,128)(2,1)S(1)}, bf16[128,2048]{1,0:T(8,128)(2,1)S(1)}, bf16[128,2048]{1,0:T(8,128)(2,1)S(1)}, bf16[128,2048]{1,0:T(8,12...) custom-call(s32[4]{0:T(128)S(1)} %pad_add_fusion.1.ids_ref, ...), custom_call_target="tpu_custom_call" | custom-call | flops 1845493760 | bytes 11452416 | tf_op jit(solution)/shard_map/pallas_call | solution.py:191
  94.1 1.2 add_convert_fusion.7
  95.2 1.7 collective-permute-start.18
  97.1 8.9 %shard_map.130 = (bf16[128,2048]{1,0:T(8,128)(2,1)S(1)}, bf16[128,2048]{1,0:T(8,128)(2,1)S(1)}, bf16[128,2048]{1,0:T(8,128)(2,1)}, bf16[128,2048]{1,0:T(8,128)(2...) custom-call(s32[4]{0:T(128)S(1)} %pad_add_fusion.2.ids_ref, ...), custom_call_target="tpu_custom_call" | custom-call | flops 1845493760 | bytes 11452416 | tf_op jit(solution)/shard_map/pallas_call | solution.py:191
  105.9 0.8 copy-done.17
  107.8 8.9 %shard_map.131 = (bf16[128,2048]{1,0:T(8,128)(2,1)S(1)}, bf16[128,2048]{1,0:T(8,128)(2,1)S(1)}, bf16[128,2048]{1,0:T(8,128)(2,1)}, bf16[128,2048]{1,0:T(8,128)(2...) custom-call(s32[4]{0:T(128)S(1)} %pad_add_fusion.3.ids_ref, ...), custom_call_target="tpu_custom_call" | custom-call | flops 1845493760 | bytes 11452416 | tf_op jit(solution)/shard_map/pallas_call | solution.py:191
  117.4 1.5 collective-permute-start.17
  118.9 0.9 add_convert_fusion.4
  119.8 1.8 collective-permute-done.8
  122.1 0.9 add_convert_fusion.2
  123.0 9.9 %collective-permute-done.17 = bf16[128,2048]{1,0:T(8,128)(2,1)} collective-permute-done((bf16[128,2048]{1,0:T(8,128)(2,1)S(1)}, bf16[128,2048]{1,0:T(8,128)(2,1)}, u32[]{:S(2)}, u32[]{:S(2)}) %collective-permute-start.17) | collective-permute-done | bytes 524320 | tf_op jit(solution)/shard_map/ppermute | solution.py:286
  133.8 0.8 collective-permute-start.32
  134.7 1.4 add_convert_fusion.5
  136.1 8.0 %collective-permute-done.24 = bf16[128,2048]{1,0:T(8,128)(2,1)} collective-permute-done((bf16[128,2048]{1,0:T(8,128)(2,1)}, bf16[128,2048]{1,0:T(8,128)(2,1)}, u32[]{:S(2)}, u32[]{:S(2)}) %collective-permute-start.24) | collective-permute-done | bytes 524320 | tf_op jit(solution)/shard_map/ppermute | solution.py:286
  144.2 2.2 collective-permute-done.26.refs_12_
  146.9 0.8 collective-permute-start.19
  147.7 7.2 %collective-permute-done.32 = bf16[128,2048]{1,0:T(8,128)(2,1)} collective-permute-done((bf16[128,2048]{1,0:T(8,128)(2,1)}, bf16[128,2048]{1,0:T(8,128)(2,1)}, u32[]{:S(2)}, u32[]{:S(2)}) %collective-permute-start.32) | collective-permute-done | bytes 524320 | tf_op jit(solution)/shard_map/ppermute | solution.py:286
  154.9 0.9 collective-permute-start.36
  155.8 1.4 add_convert_fusion.3
  157.3 1.5 add_convert_fusion.1
  158.8 2.0 collective-permute-done.19
  160.8 7.8 %collective-permute-done.36.refs_5_ = bf16[128,2048]{1,0:T(8,128)(2,1)S(1)} collective-permute-done((bf16[128,2048]{1,0:T(8,128)(2,1)}, bf16[128,2048]{1,0:T(8,128)(2,1)S(1)}, u32[]{:S(2)}, u32[]{:S(2)}) %collective-permute-start.36) | collective-permute-done | bytes 524320 | tf_op jit(solution)/shard_map/ppermute | solution.py:286
  169.8 1.0 collective-permute-start.39
  170.8 1.1 collective-permute-start.42
  172.0 33.2 %all_to_all.10 = bf16[16,1,128]{2,1,0:T(2,128)(2,1)S(1)} all-to-all(bf16[16,1,128]{2,1,0:T(2,128)(2,1)S(1)} %copy.48), channel_id=1, replica_groups=mesh['group'=2,'expert'=4,'seq'=4] {'expert','seq'}, dimensions={0} | all-to-all | bytes 8192 | tf_op jit(solution)/shard_map/all_to_all | solution.py:386
  207.0 1.3 add_convert_fusion
  208.3 1.1 collective-permute-done.43.refs_14_
  210.8 0.8 copy-done.38
  211.7 12.7 %shard_map.132 = (bf16[2048,384]{1,0:T(8,128)(2,1)}, bf16[2048,384]{1,0:T(8,128)(2,1)}, bf16[384,2048]{1,0:T(8,128)(2,1)}) custom-call(s32[16]{0:T(128)} %copy-done.25, s32[16,1,128]{2,1,0:T(1,128)} %copy-done.12, bf16[128,2048]{1,0:T(8,128)(2,1)} %refs_0_.1, bf16[128,2048]{1,0:T(8,128)(2,1)} %collective-permute-done.6.refs_1_, ...), custom_call_target="tpu_custom_call" | custom-call | flops 6710886400 | bytes 21299200 | tf_op jit(solution)/shard_map/pallas_call | solution.py:250
  (158 shorter events, 14.1 us)
Async XLA Ops:
  0.6 18.1 %collective-permute-start.9 = (bf16[128,2048]{1,0:T(8,128)(2,1)}, bf16[128,2048]{1,0:T(8,128)(2,1)S(1)}, u32[]{:S(2)}, u32[]{:S(2)}) collective-permute-start(bf16[128,2048]{1,0:T(8,128)(2,1)} %dy0.1), channel_id=1, source_target_pairs={{0,1},{1,2},{2,3},{3,0},{4,5},{5,6},{6,7},{7,4},{8,9},{9,10},{10,1... | collective-permute-start | bytes 1572872 | tf_op jit(solution)/shard_map/ppermute | solution.py:286
  3.7 31.7 %collective-permute-start = (bf16[128,2048]{1,0:T(8,128)(2,1)}, bf16[128,2048]{1,0:T(8,128)(2,1)S(1)}, u32[]{:S(2)}, u32[]{:S(2)}) collective-permute-start(bf16[128,2048]{1,0:T(8,128)(2,1)} %dy0.1), channel_id=1, source_target_pairs={{0,8},{4,12},{8,0},{12,4},{1,9},{5,13},{9,1},{13,5},{2,10},{6,14},... | collective-permute-start | bytes 1572872 | tf_op jit(solution)/shard_map/ppermute | solution.py:286
  5.2 31.7 %collective-permute-start.5 = (bf16[128,2048]{1,0:T(8,128)(2,1)}, bf16[128,2048]{1,0:T(8,128)(2,1)S(1)}, u32[]{:S(2)}, u32[]{:S(2)}) collective-permute-start(bf16[128,2048]{1,0:T(8,128)(2,1)} %dy0.1), channel_id=1, source_target_pairs={{0,3},{1,0},{2,1},{3,2},{4,7},{5,4},{6,5},{7,6},{8,11},{9,8},{10,9... | collective-permute-start | bytes 1572872 | tf_op jit(solution)/shard_map/ppermute | solution.py:286
  7.5 57.2 %collective-permute-start.1 = (bf16[128,2048]{1,0:T(8,128)(2,1)}, bf16[128,2048]{1,0:T(8,128)(2,1)S(1)}, u32[]{:S(2)}, u32[]{:S(2)}) collective-permute-start(bf16[128,2048]{1,0:T(8,128)(2,1)} %dy0.1), channel_id=1, source_target_pairs={{0,4},{4,0},{8,12},{12,8},{1,5},{5,1},{9,13},{13,9},{2,6},{6,2},{1... | collective-permute-start | bytes 1572872 | tf_op jit(solution)/shard_map/ppermute | solution.py:310
  7.5 31.0 %collective-permute-start.6 = (bf16[128,2048]{1,0:T(8,128)(2,1)}, bf16[128,2048]{1,0:T(8,128)(2,1)}, u32[]{:S(2)}, u32[]{:S(2)}) collective-permute-start(bf16[128,2048]{1,0:T(8,128)(2,1)} %refs_0_.1), channel_id=1, source_target_pairs={{0,8},{4,12},{8,0},{12,4},{1,9},{5,13},{9,1},{13,5},{2,10},{6,14},... | collective-permute-start | bytes 1572872 | tf_op jit(solution)/shard_map/ppermute | solution.py:286
  18.8 45.1 %collective-permute-start.15 = (bf16[128,2048]{1,0:T(8,128)(2,1)}, bf16[128,2048]{1,0:T(8,128)(2,1)S(1)}, u32[]{:S(2)}, u32[]{:S(2)}) collective-permute-start(bf16[128,2048]{1,0:T(8,128)(2,1)} %dy0.1), channel_id=1, source_target_pairs={{0,2},{1,3},{2,0},{3,1},{4,6},{5,7},{6,4},{7,5},{8,10},{9,11},{10,... | collective-permute-start | bytes 1572872 | tf_op jit(solution)/shard_map/ppermute | solution.py:286
  35.5 29.2 %collective-permute-start.10 = (bf16[128,2048]{1,0:T(8,128)(2,1)S(1)}, bf16[128,2048]{1,0:T(8,128)(2,1)}, u32[]{:S(2)}, u32[]{:S(2)}) collective-permute-start(bf16[128,2048]{1,0:T(8,128)(2,1)S(1)} %collective-permute-done.9.dy0), channel_id=1, source_target_pairs={{0,8},{4,12},{8,0},{12,4},{1,9},{5,13},{9,1},{13,5},{2,10},{6,14},... | collective-permute-start | bytes 1572872 | tf_op jit(solution)/shard_map/ppermute | solution.py:286
  37.0 29.8 %collective-permute-start.2 = (bf16[128,2048]{1,0:T(8,128)(2,1)S(1)}, bf16[128,2048]{1,0:T(8,128)(2,1)}, u32[]{:S(2)}, u32[]{:S(2)}) collective-permute-start(bf16[128,2048]{1,0:T(8,128)(2,1)S(1)} %collective-permute-done.dy1), channel_id=1, source_target_pairs={{0,4},{4,0},{8,12},{12,8},{1,5},{5,1},{9,13},{13,9},{2,6},{6,2},{1... | collective-permute-start | bytes 1572872 | tf_op jit(solution)/shard_map/ppermute | solution.py:310
  38.5 44.9 %collective-permute-start.25 = (bf16[128,2048]{1,0:T(8,128)(2,1)}, bf16[128,2048]{1,0:T(8,128)(2,1)}, u32[]{:S(2)}, u32[]{:S(2)}) collective-permute-start(bf16[128,2048]{1,0:T(8,128)(2,1)} %refs_0_.1), channel_id=1, source_target_pairs={{0,1},{1,2},{2,3},{3,0},{4,5},{5,6},{6,7},{7,4},{8,9},{9,10},{10,1... | collective-permute-start | bytes 1572872 | tf_op jit(solution)/shard_map/ppermute | solution.py:286
  39.2 24.7 %all-to-all-start = ((bf16[16,2,128]{2,1,0:T(2,128)(2,1)}), bf16[16,2,128]{2,1,0:T(2,128)(2,1)S(1)}, u32[]{:S(2)}, u32[]{:S(2)}) async-start(bf16[16,2,128]{2,1,0:T(2,128)(2,1)} %pad_maximum_fusion), calls=%async_computation | async-start | bytes 16384 | tf_op jit(solution)/shard_map/all_to_all | solution.py:333
  63.9 20.3 %collective-permute-start.7 = (bf16[128,2048]{1,0:T(8,128)(2,1)S(1)}, bf16[128,2048]{1,0:T(8,128)(2,1)}, u32[]{:S(2)}, u32[]{:S(2)}) collective-permute-start(bf16[128,2048]{1,0:T(8,128)(2,1)S(1)} %collective-permute-done.5.dy0), channel_id=1, source_target_pairs={{0,8},{4,12},{8,0},{12,4},{1,9},{5,13},{9,1},{13,5},{2,10},{6,14},... | collective-permute-start | bytes 1572872 | tf_op jit(solution)/shard_map/ppermute | solution.py:286
  64.6 19.3 %collective-permute-start.11 = (bf16[128,2048]{1,0:T(8,128)(2,1)S(1)}, bf16[128,2048]{1,0:T(8,128)(2,1)}, u32[]{:S(2)}, u32[]{:S(2)}) collective-permute-start(bf16[128,2048]{1,0:T(8,128)(2,1)S(1)} %collective-permute-done.9.dy0), channel_id=1, source_target_pairs={{0,4},{4,0},{8,12},{12,8},{1,5},{5,1},{9,13},{13,9},{2,6},{6,2},{1... | collective-permute-start | bytes 1572872 | tf_op jit(solution)/shard_map/ppermute | solution.py:310
  65.4 28.0 %collective-permute-start.16 = (bf16[128,2048]{1,0:T(8,128)(2,1)S(1)}, bf16[128,2048]{1,0:T(8,128)(2,1)}, u32[]{:S(2)}, u32[]{:S(2)}) collective-permute-start(bf16[128,2048]{1,0:T(8,128)(2,1)S(1)} %collective-permute-done.15.dy0), channel_id=1, source_target_pairs={{0,8},{4,12},{8,0},{12,4},{1,9},{5,13},{9,1},{13,5},{2,10},{6,14},... | collective-permute-start | bytes 1572872 | tf_op jit(solution)/shard_map/ppermute | solution.py:286
  66.8 17.7 %collective-permute-start.12 = (bf16[128,2048]{1,0:T(8,128)(2,1)}, bf16[128,2048]{1,0:T(8,128)(2,1)}, u32[]{:S(2)}, u32[]{:S(2)}) collective-permute-start(bf16[128,2048]{1,0:T(8,128)(2,1)} %collective-permute-done.10.dy1), channel_id=1, source_target_pairs={{0,4},{4,0},{8,12},{12,8},{1,5},{5,1},{9,13},{13,9},{2,6},{6,2},{1... | collective-permute-start | bytes 1572872 | tf_op jit(solution)/shard_map/ppermute | solution.py:310
  83.4 10.5 %collective-permute-start.4 = (bf16[128,2048]{1,0:T(8,128)(2,1)}, bf16[128,2048]{1,0:T(8,128)(2,1)}, u32[]{:S(2)}, u32[]{:S(2)}) collective-permute-start(bf16[128,2048]{1,0:T(8,128)(2,1)} %get-tuple-element.60), channel_id=1, source_target_pairs={{0,4},{4,0},{8,12},{12,8},{1,5},{5,1},{9,13},{13,9},{2,6},{6,2},{1... | collective-permute-start | bytes 1572872 | tf_op jit(solution)/shard_map/ppermute | solution.py:310
  83.9 11.3 %collective-permute-start.20 = (bf16[128,2048]{1,0:T(8,128)(2,1)S(1)}, bf16[128,2048]{1,0:T(8,128)(2,1)S(1)}, u32[]{:S(2)}, u32[]{:S(2)}) collective-permute-start(bf16[128,2048]{1,0:T(8,128)(2,1)S(1)} %collective-permute-done.5.dy0), channel_id=1, source_target_pairs={{0,4},{4,0},{8,12},{12,8},{1,5},{5,1},{9,13},{13,9},{2,6},{6,2},{1... | collective-permute-start | bytes 1572872 | tf_op jit(solution)/shard_map/ppermute | solution.py:310
  84.2 22.6 %collective-permute-start.28 = (bf16[128,2048]{1,0:T(8,128)(2,1)S(1)}, bf16[128,2048]{1,0:T(8,128)(2,1)S(1)}, u32[]{:S(2)}, u32[]{:S(2)}) collective-permute-start(bf16[128,2048]{1,0:T(8,128)(2,1)S(1)} %collective-permute-done.15.dy0), channel_id=1, source_target_pairs={{0,4},{4,0},{8,12},{12,8},{1,5},{5,1},{9,13},{13,9},{2,6},{6,2},{1... | collective-permute-start | bytes 1572872 | tf_op jit(solution)/shard_map/ppermute | solution.py:310
  84.5 12.5 %collective-permute-start.21 = (bf16[128,2048]{1,0:T(8,128)(2,1)}, bf16[128,2048]{1,0:T(8,128)(2,1)S(1)}, u32[]{:S(2)}, u32[]{:S(2)}) collective-permute-start(bf16[128,2048]{1,0:T(8,128)(2,1)} %collective-permute-done.7.dy1), channel_id=1, source_target_pairs={{0,4},{4,0},{8,12},{12,8},{1,5},{5,1},{9,13},{13,9},{2,6},{6,2},{1... | collective-permute-start | bytes 1572872 | tf_op jit(solution)/shard_map/ppermute | solution.py:310
  93.5 23.8 %collective-permute-start.14 = (bf16[128,2048]{1,0:T(8,128)(2,1)S(1)}, bf16[128,2048]{1,0:T(8,128)(2,1)S(1)}, u32[]{:S(2)}, u32[]{:S(2)}) collective-permute-start(bf16[128,2048]{1,0:T(8,128)(2,1)S(1)} %get-tuple-element.67), channel_id=1, source_target_pairs={{0,4},{4,0},{8,12},{12,8},{1,5},{5,1},{9,13},{13,9},{2,6},{6,2},{1... | collective-permute-start | bytes 1572872 | tf_op jit(solution)/shard_map/ppermute | solution.py:310
  93.8 13.4 %collective-permute-start.29 = (bf16[128,2048]{1,0:T(8,128)(2,1)}, bf16[128,2048]{1,0:T(8,128)(2,1)S(1)}, u32[]{:S(2)}, u32[]{:S(2)}) collective-permute-start(bf16[128,2048]{1,0:T(8,128)(2,1)} %collective-permute-done.16.dy1), channel_id=1, source_target_pairs={{0,4},{4,0},{8,12},{12,8},{1,5},{5,1},{9,13},{13,9},{2,6},{6,2},{1... | collective-permute-start | bytes 1572872 | tf_op jit(solution)/shard_map/ppermute | solution.py:310
  95.2 37.7 %collective-permute-start.18 = (bf16[128,2048]{1,0:T(8,128)(2,1)}, bf16[128,2048]{1,0:T(8,128)(2,1)S(1)}, u32[]{:S(2)}, u32[]{:S(2)}) collective-permute-start(bf16[128,2048]{1,0:T(8,128)(2,1)} %refs_0_.1), channel_id=1, source_target_pairs={{0,3},{1,0},{2,1},{3,2},{4,7},{5,4},{6,5},{7,6},{8,11},{9,8},{10,9... | collective-permute-start | bytes 1572872 | tf_op jit(solution)/shard_map/ppermute | solution.py:286
  97.0 36.5 %collective-permute-start.13 = (bf16[128,2048]{1,0:T(8,128)(2,1)S(1)}, bf16[128,2048]{1,0:T(8,128)(2,1)}, u32[]{:S(2)}, u32[]{:S(2)}) collective-permute-start(bf16[128,2048]{1,0:T(8,128)(2,1)S(1)} %get-tuple-element.65), channel_id=1, source_target_pairs={{0,4},{4,0},{8,12},{12,8},{1,5},{5,1},{9,13},{13,9},{2,6},{6,2},{1... | collective-permute-start | bytes 1572872 | tf_op jit(solution)/shard_map/ppermute | solution.py:310
  106.7 10.7 %collective-permute-start.23 = (bf16[128,2048]{1,0:T(8,128)(2,1)S(1)}, bf16[128,2048]{1,0:T(8,128)(2,1)S(1)}, u32[]{:S(2)}, u32[]{:S(2)}) collective-permute-start(bf16[128,2048]{1,0:T(8,128)(2,1)S(1)} %get-tuple-element.76), channel_id=1, source_target_pairs={{0,4},{4,0},{8,12},{12,8},{1,5},{5,1},{9,13},{13,9},{2,6},{6,2},{1... | collective-permute-start | bytes 1572872 | tf_op jit(solution)/shard_map/ppermute | solution.py:310
  107.2 14.4 %collective-permute-start.8 = (bf16[128,2048]{1,0:T(8,128)(2,1)S(1)}, bf16[128,2048]{1,0:T(8,128)(2,1)S(1)}, u32[]{:S(2)}, u32[]{:S(2)}) collective-permute-start(bf16[128,2048]{1,0:T(8,128)(2,1)S(1)} %add_convert_fusion.7), channel_id=1, source_target_pairs={{0,8},{4,12},{8,0},{12,4},{1,9},{5,13},{9,1},{13,5},{2,10},{6,14},... | collective-permute-start | bytes 1572872 | tf_op jit(solution)/shard_map/ppermute | solution.py:286
  117.2 4.7 %collective-permute-start.31 = (bf16[128,2048]{1,0:T(8,128)(2,1)S(1)}, bf16[128,2048]{1,0:T(8,128)(2,1)S(1)}, u32[]{:S(2)}, u32[]{:S(2)}) collective-permute-start(bf16[128,2048]{1,0:T(8,128)(2,1)S(1)} %get-tuple-element.84), channel_id=1, source_target_pairs={{0,4},{4,0},{8,12},{12,8},{1,5},{5,1},{9,13},{13,9},{2,6},{6,2},{1... | collective-permute-start | bytes 1572872 | tf_op jit(solution)/shard_map/ppermute | solution.py:310
  117.4 15.5 %collective-permute-start.17 = (bf16[128,2048]{1,0:T(8,128)(2,1)S(1)}, bf16[128,2048]{1,0:T(8,128)(2,1)}, u32[]{:S(2)}, u32[]{:S(2)}) collective-permute-start(bf16[128,2048]{1,0:T(8,128)(2,1)S(1)} %add_convert_fusion.6), channel_id=1, source_target_pairs={{0,8},{4,12},{8,0},{12,4},{1,9},{5,13},{9,1},{13,5},{2,10},{6,14},... | collective-permute-start | bytes 1572872 | tf_op jit(solution)/shard_map/ppermute | solution.py:286
  121.6 24.8 %collective-permute-start.26 = (bf16[128,2048]{1,0:T(8,128)(2,1)}, bf16[128,2048]{1,0:T(8,128)(2,1)}, u32[]{:S(2)}, u32[]{:S(2)}) collective-permute-start(bf16[128,2048]{1,0:T(8,128)(2,1)} %refs_0_.1), channel_id=1, source_target_pairs={{0,2},{1,3},{2,0},{3,1},{4,6},{5,7},{6,4},{7,5},{8,10},{9,11},{10,... | collective-permute-start | bytes 1572872 | tf_op jit(solution)/shard_map/ppermute | solution.py:286
  121.9 22.3 %collective-permute-start.24 = (bf16[128,2048]{1,0:T(8,128)(2,1)}, bf16[128,2048]{1,0:T(8,128)(2,1)}, u32[]{:S(2)}, u32[]{:S(2)}) collective-permute-start(bf16[128,2048]{1,0:T(8,128)(2,1)} %add_convert_fusion.4), channel_id=1, source_target_pairs={{0,8},{4,12},{8,0},{12,4},{1,9},{5,13},{9,1},{13,5},{2,10},{6,14},... | collective-permute-start | bytes 1572872 | tf_op jit(solution)/shard_map/ppermute | solution.py:286
  132.9 13.5 %collective-permute-start.22 = (bf16[128,2048]{1,0:T(8,128)(2,1)}, bf16[128,2048]{1,0:T(8,128)(2,1)}, u32[]{:S(2)}, u32[]{:S(2)}) collective-permute-start(bf16[128,2048]{1,0:T(8,128)(2,1)} %get-tuple-element.74), channel_id=1, source_target_pairs={{0,4},{4,0},{8,12},{12,8},{1,5},{5,1},{9,13},{13,9},{2,6},{6,2},{1... | collective-permute-start | bytes 1572872 | tf_op jit(solution)/shard_map/ppermute | solution.py:310
  133.0 14.0 %collective-permute-start.30 = (bf16[128,2048]{1,0:T(8,128)(2,1)}, bf16[128,2048]{1,0:T(8,128)(2,1)}, u32[]{:S(2)}, u32[]{:S(2)}) collective-permute-start(bf16[128,2048]{1,0:T(8,128)(2,1)} %get-tuple-element.82), channel_id=1, source_target_pairs={{0,4},{4,0},{8,12},{12,8},{1,5},{5,1},{9,13},{13,9},{2,6},{6,2},{1... | collective-permute-start | bytes 1572872 | tf_op jit(solution)/shard_map/ppermute | solution.py:310
  133.8 21.1 %collective-permute-start.32 = (bf16[128,2048]{1,0:T(8,128)(2,1)}, bf16[128,2048]{1,0:T(8,128)(2,1)}, u32[]{:S(2)}, u32[]{:S(2)}) collective-permute-start(bf16[128,2048]{1,0:T(8,128)(2,1)} %add_convert_fusion.2), channel_id=1, source_target_pairs={{0,8},{4,12},{8,0},{12,4},{1,9},{5,13},{9,1},{13,5},{2,10},{6,14},... | collective-permute-start | bytes 1572872 | tf_op jit(solution)/shard_map/ppermute | solution.py:286
  144.2 24.9 %collective-permute-start.34 = (bf16[128,2048]{1,0:T(8,128)(2,1)}, bf16[128,2048]{1,0:T(8,128)(2,1)S(1)}, u32[]{:S(2)}, u32[]{:S(2)}) collective-permute-start(bf16[128,2048]{1,0:T(8,128)(2,1)} %refs_0_.1), channel_id=1, source_target_pairs={{0,4},{4,0},{8,12},{12,8},{1,5},{5,1},{9,13},{13,9},{2,6},{6,2},{1... | collective-permute-start | bytes 1572872 | tf_op jit(solution)/shard_map/ppermute | solution.py:310
  146.4 23.4 %collective-permute-start.35 = (bf16[128,2048]{1,0:T(8,128)(2,1)}, bf16[128,2048]{1,0:T(8,128)(2,1)S(1)}, u32[]{:S(2)}, u32[]{:S(2)}) collective-permute-start(bf16[128,2048]{1,0:T(8,128)(2,1)} %collective-permute-done.6.refs_1_), channel_id=1, source_target_pairs={{0,4},{4,0},{8,12},{12,8},{1,5},{5,1},{9,13},{13,9},{2,6},{6,2},{1... | collective-permute-start | bytes 1572872 | tf_op jit(solution)/shard_map/ppermute | solution.py:310
  146.4 24.4 %collective-permute-start.3 = (bf16[128,2048]{1,0:T(8,128)(2,1)S(1)}, bf16[128,2048]{1,0:T(8,128)(2,1)S(1)}, u32[]{:S(2)}, u32[]{:S(2)}) collective-permute-start(bf16[128,2048]{1,0:T(8,128)(2,1)S(1)} %copy-done.14), channel_id=1, source_target_pairs={{0,4},{4,0},{8,12},{12,8},{1,5},{5,1},{9,13},{13,9},{2,6},{6,2},{1... | collective-permute-start | bytes 1572872 | tf_op jit(solution)/shard_map/ppermute | solution.py:310
  146.9 13.9 %collective-permute-start.19 = (bf16[128,2048]{1,0:T(8,128)(2,1)S(1)}, bf16[128,2048]{1,0:T(8,128)(2,1)S(1)}, u32[]{:S(2)}, u32[]{:S(2)}) collective-permute-start(bf16[128,2048]{1,0:T(8,128)(2,1)S(1)} %add_convert_fusion.5), channel_id=1, source_target_pairs={{0,3},{1,0},{2,1},{3,2},{4,7},{5,4},{6,5},{7,6},{8,11},{9,8},{10,9... | collective-permute-start | bytes 1572872 | tf_op jit(solution)/shard_map/ppermute | solution.py:286
  154.9 13.7 %collective-permute-start.36 = (bf16[128,2048]{1,0:T(8,128)(2,1)}, bf16[128,2048]{1,0:T(8,128)(2,1)S(1)}, u32[]{:S(2)}, u32[]{:S(2)}) collective-permute-start(bf16[128,2048]{1,0:T(8,128)(2,1)} %collective-permute-done.25.refs_4_), channel_id=1, source_target_pairs={{0,8},{4,12},{8,0},{12,4},{1,9},{5,13},{9,1},{13,5},{2,10},{6,14},... | collective-permute-start | bytes 1572872 | tf_op jit(solution)/shard_map/ppermute | solution.py:286
  157.3 49.7 %copy-start.24 = (bf16[128,2048]{1,0:T(8,128)(2,1)S(1)}, bf16[128,2048]{1,0:T(8,128)(2,1)}, u32[]{:S(2)}) copy-start(bf16[128,2048]{1,0:T(8,128)(2,1)} %copy-done.23) | copy-start | bytes 1572868
  160.8 45.0 %collective-permute-start.37 = (bf16[128,2048]{1,0:T(8,128)(2,1)}, bf16[128,2048]{1,0:T(8,128)(2,1)S(1)}, u32[]{:S(2)}, u32[]{:S(2)}) collective-permute-start(bf16[128,2048]{1,0:T(8,128)(2,1)} %collective-permute-done.25.refs_4_), channel_id=1, source_target_pairs={{0,4},{4,0},{8,12},{12,8},{1,5},{5,1},{9,13},{13,9},{2,6},{6,2},{1... | collective-permute-start | bytes 1572872 | tf_op jit(solution)/shard_map/ppermute | solution.py:310
  168.6 39.7 %copy-start.30 = (bf16[128,2048]{1,0:T(8,128)(2,1)}, bf16[128,2048]{1,0:T(8,128)(2,1)S(1)}, u32[]{:S(2)}) copy-start(bf16[128,2048]{1,0:T(8,128)(2,1)S(1)} %collective-permute-done.36.refs_5_) | copy-start | bytes 1572868
  168.6 37.3 %collective-permute-start.27 = (bf16[128,2048]{1,0:T(8,128)(2,1)S(1)}, bf16[128,2048]{1,0:T(8,128)(2,1)S(1)}, u32[]{:S(2)}, u32[]{:S(2)}) collective-permute-start(bf16[128,2048]{1,0:T(8,128)(2,1)S(1)} %add_convert_fusion.3), channel_id=1, source_target_pairs={{0,1},{1,2},{2,3},{3,0},{4,5},{5,6},{6,7},{7,4},{8,9},{9,10},{10,1... | collective-permute-start | bytes 1572872 | tf_op jit(solution)/shard_map/ppermute | solution.py:286
  169.0 37.3 %collective-permute-start.33 = (bf16[128,2048]{1,0:T(8,128)(2,1)S(1)}, bf16[128,2048]{1,0:T(8,128)(2,1)S(1)}, u32[]{:S(2)}, u32[]{:S(2)}) collective-permute-start(bf16[128,2048]{1,0:T(8,128)(2,1)S(1)} %add_convert_fusion.1), channel_id=1, source_target_pairs={{0,2},{1,3},{2,0},{3,1},{4,6},{5,7},{6,4},{7,5},{8,10},{9,11},{10,... | collective-permute-start | bytes 1572872 | tf_op jit(solution)/shard_map/ppermute | solution.py:286
  169.8 36.7 %collective-permute-start.39 = (bf16[128,2048]{1,0:T(8,128)(2,1)S(1)}, bf16[128,2048]{1,0:T(8,128)(2,1)S(1)}, u32[]{:S(2)}, u32[]{:S(2)}) collective-permute-start(bf16[128,2048]{1,0:T(8,128)(2,1)S(1)} %copy-done.27), channel_id=1, source_target_pairs={{0,8},{4,12},{8,0},{12,4},{1,9},{5,13},{9,1},{13,5},{2,10},{6,14},... | collective-permute-start | bytes 1572872 | tf_op jit(solution)/shard_map/ppermute | solution.py:286
  170.8 36.1 %collective-permute-start.42 = (bf16[128,2048]{1,0:T(8,128)(2,1)}, bf16[128,2048]{1,0:T(8,128)(2,1)S(1)}, u32[]{:S(2)}, u32[]{:S(2)}) collective-permute-start(bf16[128,2048]{1,0:T(8,128)(2,1)} %collective-permute-done.26.refs_12_), channel_id=1, source_target_pairs={{0,8},{4,12},{8,0},{12,4},{1,9},{5,13},{9,1},{13,5},{2,10},{6,14},... | collective-permute-start | bytes 1572872 | tf_op jit(solution)/shard_map/ppermute | solution.py:286
  205.9 2.5 %collective-permute-start.40 = (bf16[128,2048]{1,0:T(8,128)(2,1)S(1)}, bf16[128,2048]{1,0:T(8,128)(2,1)S(1)}, u32[]{:S(2)}, u32[]{:S(2)}) collective-permute-start(bf16[128,2048]{1,0:T(8,128)(2,1)S(1)} %copy-done.27), channel_id=1, source_target_pairs={{0,4},{4,0},{8,12},{12,8},{1,5},{5,1},{9,13},{13,9},{2,6},{6,2},{1... | collective-permute-start | bytes 1572872 | tf_op jit(solution)/shard_map/ppermute | solution.py:310
  205.9 3.6 %collective-permute-start.43 = (bf16[128,2048]{1,0:T(8,128)(2,1)}, bf16[128,2048]{1,0:T(8,128)(2,1)S(1)}, u32[]{:S(2)}, u32[]{:S(2)}) collective-permute-start(bf16[128,2048]{1,0:T(8,128)(2,1)} %collective-permute-done.26.refs_12_), channel_id=1, source_target_pairs={{0,4},{4,0},{8,12},{12,8},{1,5},{5,1},{9,13},{13,9},{2,6},{6,2},{1... | collective-permute-start | bytes 1572872 | tf_op jit(solution)/shard_map/ppermute | solution.py:310
  206.4 3.1 %collective-permute-start.38 = (bf16[128,2048]{1,0:T(8,128)(2,1)S(1)}, bf16[128,2048]{1,0:T(8,128)(2,1)S(1)}, u32[]{:S(2)}, u32[]{:S(2)}) collective-permute-start(bf16[128,2048]{1,0:T(8,128)(2,1)S(1)} %collective-permute-done.36.refs_5_), channel_id=1, source_target_pairs={{0,4},{4,0},{8,12},{12,8},{1,5},{5,1},{9,13},{13,9},{2,6},{6,2},{1... | collective-permute-start | bytes 1572872 | tf_op jit(solution)/shard_map/ppermute | solution.py:310
  206.5 3.6 %collective-permute-start.41 = (bf16[128,2048]{1,0:T(8,128)(2,1)S(1)}, bf16[128,2048]{1,0:T(8,128)(2,1)S(1)}, u32[]{:S(2)}, u32[]{:S(2)}) collective-permute-start(bf16[128,2048]{1,0:T(8,128)(2,1)S(1)} %collective-permute-done.39.refs_9_), channel_id=1, source_target_pairs={{0,4},{4,0},{8,12},{12,8},{1,5},{5,1},{9,13},{13,9},{2,6},{6,2},{1... | collective-permute-start | bytes 1572872 | tf_op jit(solution)/shard_map/ppermute | solution.py:310
  206.9 3.9 %collective-permute-start.44 = (bf16[128,2048]{1,0:T(8,128)(2,1)S(1)}, bf16[128,2048]{1,0:T(8,128)(2,1)S(1)}, u32[]{:S(2)}, u32[]{:S(2)}) collective-permute-start(bf16[128,2048]{1,0:T(8,128)(2,1)S(1)} %collective-permute-done.42.refs_13_), channel_id=1, source_target_pairs={{0,4},{4,0},{8,12},{12,8},{1,5},{5,1},{9,13},{13,9},{2,6},{6,2},{1... | collective-permute-start | bytes 1572872 | tf_op jit(solution)/shard_map/ppermute | solution.py:310
  (37 other events, 262.1 us)

commit v2 on v0

--- a/solution.py
+++ b/solution.py
@@ -1,6 +1,10 @@
+import functools
+
 import jax
 import jax.numpy as jnp
 from jax import lax
+from jax.experimental import pallas as pl
+from jax.experimental.pallas import tpu as pltpu
 from jax.sharding import PartitionSpec as P
 
 
@@ -46,7 +50,7 @@
     return (slot_dx, slot_dprob, grad_gate, grad_up, grad_down)
 
 
-def local(tokens, grad_out, probs, routes, w_gate, w_up, w_down, gate_pre, up_pre):
+def exchange_local(tokens, grad_out, probs, routes, w_gate, w_up, w_down, gate_pre, up_pre):
     seq_count = lax.axis_size("seq")
     expert_count = lax.axis_size("expert")
     experts = seq_count * expert_count
@@ -100,6 +104,407 @@
     grad_tokens = summed.astype(jnp.bfloat16)
     grad_probs = back_p.reshape(-1)[own_places]
     return (grad_tokens, grad_probs, grad_gate[None], grad_up[None], grad_down[None])
+
+
+TILE = 512
+STEP = 1024
+VMEM = 60 << 20
+
+
+def dot_nt(a, b):
+    return lax.dot_general(a, b, (((1,), (1,)), ((), ())), preferred_element_type=jnp.float32)
+
+
+def dot_tn(a, b):
+    return lax.dot_general(a, b, (((0,), (0,)), ((), ())), preferred_element_type=jnp.float32)
+
+
+def slot_hits(slots, slot_cap):
+    shape = (slot_cap, slots.shape[1])
+    return lax.broadcasted_iota(jnp.int32, shape, 0) == jnp.broadcast_to(slots, shape)
+
+
+def slots_of(named, before):
+    taken = jnp.max(jnp.where(named, 1.0, 0.0), axis=0, keepdims=True)
+    ranked = jnp.dot(
+        jnp.broadcast_to(taken, named.shape).astype(jnp.bfloat16), before, preferred_element_type=jnp.float32
+    )
+    return jnp.where(taken > 0.0, ranked[:1], -1.0).astype(jnp.int32)
+
+
+def as_bf16(hits):
+    return jnp.where(hits, 1.0, 0.0).astype(jnp.bfloat16)
+
+
+def slope_kernel(gate_ref, up_ref, out_ref):
+    hid = gate_ref.shape[2]
+    gate_f = gate_ref[...].astype(jnp.float32)
+    up_f = up_ref[...].astype(jnp.float32)
+    logistic = jax.nn.sigmoid(gate_f)
+    active = gate_f * logistic
+    out_ref[:, :, :hid] = up_f * logistic * (1.0 + gate_f * (1.0 - logistic))
+    out_ref[:, :, hid:2 * hid] = active
+    out_ref[:, :, 2 * hid:] = active * up_f
+
+
+def slopes(gate_in, up_in):
+    blocks, slot_cap, hid = gate_in.shape
+    spec = pl.BlockSpec((2, slot_cap, hid), lambda i: (i, 0, 0))
+    return pl.pallas_call(
+        slope_kernel,
+        grid=(blocks // 2,),
+        out_shape=jax.ShapeDtypeStruct((blocks, slot_cap, 3 * hid), jnp.float32),
+        in_specs=[spec] * 2,
+        out_specs=pl.BlockSpec((2, slot_cap, 3 * hid), lambda i: (i, 0, 0)),
+        cost_estimate=pl.CostEstimate(
+            flops=10 * gate_in.size, bytes_accessed=16 * gate_in.size, transcendentals=gate_in.size
+        ),
+    )(gate_in, up_in)
+
+
+def round_kernel(
+    ids_ref, dy0, dy1, dy2, dy3, down_hbm, gate_w_hbm, up_w_hbm, slope_hbm,
+    dx0, dx1, dx2, dx3, rows_hbm, dgu_hbm, scaled_hbm, slot_ref,
+    dy_ref, info_ref, down_ref, both_w_ref, slope_ref,
+    dx_ref, extra_ref, rows_ref, dgu_ref, scaled_ref, in_sems, out_sems,
+):
+    pieces, results = (dy0, dy1, dy2, dy3), (dx0, dx1, dx2, dx3)
+    slot_cap, hid = slope_ref.shape[1], scaled_ref.shape[1]
+    height, width = dy0.shape
+    count = slot_ref.shape[2]
+    taken = 4 * slot_cap
+    half = width // 2
+
+    started = []
+
+    def fetch(source, target):
+        copy = pltpu.make_async_copy(source, target, in_sems.at[len(started)])
+        copy.start()
+        started.append(copy)
+        return copy
+
+    sent = []
+
+    def send(source, target):
+        copy = pltpu.make_async_copy(source, target, out_sems.at[len(sent)])
+        copy.start()
+        sent.append(copy)
+
+    infos = [fetch(pieces[i].at[count:height, :2 * count], info_ref.at[i]) for i in range(4)]
+    tiles = []
+    for part in range(2):
+        cols = slice(part * half, (part + 1) * half)
+        tiles.append(
+            [fetch(pieces[i].at[:count, cols], dy_ref.at[i * count:(i + 1) * count, cols]) for i in range(4)]
+            + [fetch(down_hbm.at[:, cols], down_ref.at[:, cols])]
+        )
+    ready = [fetch(slope_hbm.at[ids_ref[i]], slope_ref.at[i]) for i in range(4)]
+    weights = []
+    for part in range(2):
+        span = slice(part * half, (part + 1) * half)
+        weights.append(
+            [fetch(gate_w_hbm.at[span, :], both_w_ref.at[span, :hid]), fetch(up_w_hbm.at[span, :], both_w_ref.at[span, hid:])]
+        )
+
+    expert = ids_ref[4].astype(jnp.float32)
+    order = [lax.broadcasted_iota(jnp.int32, (count, count), axis) for axis in (0, 1)]
+    before = as_bf16(order[0] < order[1])
+    hits, named, probs = [], [], []
+    for i in range(4):
+        infos[i].wait()
+        routes = info_ref[i, :, :count].astype(jnp.float32)
+        given = info_ref[i, :, count:].astype(jnp.float32)
+        named.append(routes == expert)
+        probs.append(jnp.sum(jnp.where(named[i], given, 0.0), axis=0, keepdims=True))
+        slot = slots_of(named[i], before)
+        slot_ref[i] = slot
+        hits.append(slot_hits(slot, slot_cap))
+    pairs = []
+    for i in (0, 2):
+        none = jnp.zeros((slot_cap, count), jnp.bfloat16)
+        upper = jnp.concatenate([as_bf16(hits[i]), none], axis=1)
+        lower = jnp.concatenate([none, as_bf16(hits[i + 1])], axis=1)
+        pairs.append(jnp.concatenate([upper, lower], axis=0))
+
+    back = None
+    for part in range(2):
+        for copy in tiles[part]:
+            copy.wait()
+        for start in range(part * half, (part + 1) * half, STEP):
+            cols = slice(start, start + STEP)
+            for i in range(2):
+                span = slice(2 * i * slot_cap, (2 * i + 2) * slot_cap)
+                rows = jnp.dot(
+                    pairs[i], dy_ref[2 * i * count:(2 * i + 2) * count, cols], preferred_element_type=jnp.float32
+                )
+                rows_ref[span, cols] = rows.astype(jnp.bfloat16)
+            part_back = dot_nt(rows_ref[:, cols], down_ref[:, cols])
+            back = part_back if back is None else back + part_back
+        cols = slice(part * half, (part + 1) * half)
+        send(rows_ref.at[:, cols], rows_hbm.at[:, cols])
+
+    for i in range(4):
+        ready[i].wait()
+        span = slice(i * slot_cap, (i + 1) * slot_cap)
+        back_rows = back[span, :]
+        hidden = slope_ref[i, :, 2 * hid:]
+        weight = jnp.broadcast_to(probs[i], hits[i].shape)
+        weight = jnp.sum(jnp.where(hits[i], weight, 0.0), axis=1, keepdims=True)
+        dprob = jnp.sum(back_rows * hidden, axis=1, keepdims=True)
+        dprob = jnp.broadcast_to(dprob, hits[i].shape)
+        dprob = jnp.sum(jnp.where(hits[i], dprob, 0.0), axis=0, keepdims=True)
+        dprob = jnp.where(named[i], jnp.broadcast_to(dprob, named[i].shape), 0.0)
+        extra_ref[i, :, :count] = dprob.astype(jnp.bfloat16)
+        extra_ref[i, :, count:] = jnp.zeros((height - count, width - count), jnp.bfloat16)
+        send(extra_ref.at[i], results[i].at[count:height, :])
+        d_hidden = weight * back_rows
+        dgu_ref[span, :hid] = (d_hidden * slope_ref[i, :, :hid]).astype(jnp.bfloat16)
+        dgu_ref[span, hid:] = (d_hidden * slope_ref[i, :, hid:2 * hid]).astype(jnp.bfloat16)
+        scaled_ref[span, :] = (weight * hidden).astype(jnp.bfloat16)
+    send(dgu_ref, dgu_hbm)
+    send(scaled_ref, scaled_hbm)
+
+    for part in range(2):
+        for copy in weights[part]:
+            copy.wait()
+        for start in range(part * half, (part + 1) * half, STEP):
+            cols = slice(start, start + STEP)
+            slot_dx = dot_nt(dgu_ref[...], both_w_ref[cols, :]).astype(jnp.bfloat16)
+            for i in range(2):
+                span = slice(2 * i * slot_cap, (2 * i + 2) * slot_cap)
+                both = dot_tn(pairs[i], slot_dx[span, :]).astype(jnp.bfloat16)
+                dx_ref[2 * i * count:(2 * i + 2) * count, cols] = both
+        cols = slice(part * half, (part + 1) * half)
+        for i in (2, 3, 1, 0):
+            send(dx_ref.at[i * count:(i + 1) * count, cols], results[i].at[:count, cols])
+    for copy in sent:
+        copy.wait()
+
+
+def round_backward(ids, count, pieces, down_w, gate_w, up_w, parts):
+    height, width = pieces[0].shape
+    slot_cap, hid = parts.shape[1], parts.shape[2] // 3
+    taken = 4 * slot_cap
+    half = jnp.bfloat16
+    anywhere = pl.BlockSpec(memory_space=pl.ANY)
+    flops = 2 * taken * width * (3 * hid + 2 * count)
+    moved = 2 * (3 * width * hid + 8 * height * width + taken * (width + 5 * hid))
+    out = pl.pallas_call(
+        round_kernel,
+        out_shape=[jax.ShapeDtypeStruct((height, width), half)] * 4
+        + [
+            jax.ShapeDtypeStruct((taken, width), half),
+            jax.ShapeDtypeStruct((taken, 2 * hid), half),
+            jax.ShapeDtypeStruct((taken, hid), half),
+            jax.ShapeDtypeStruct((4, 1, count), jnp.int32),
+        ],
+        in_specs=[pl.BlockSpec(memory_space=pltpu.SMEM)] + [anywhere] * 8,
+        out_specs=[anywhere] * 7 + [pl.BlockSpec(memory_space=pltpu.VMEM)],
+        scratch_shapes=[
+            pltpu.VMEM((4 * count, width), half),
+            pltpu.VMEM((4, height - count, 2 * count), half),
+            pltpu.VMEM(down_w.shape, half),
+            pltpu.VMEM((width, 2 * hid), half),
+            pltpu.VMEM((4, slot_cap, 3 * hid), jnp.float32),
+            pltpu.VMEM((4 * count, width), half),
+            pltpu.VMEM((4, height - count, width), half),
+            pltpu.VMEM((taken, width), half),
+            pltpu.VMEM((taken, 2 * hid), half),
+            pltpu.VMEM((taken, hid), half),
+            pltpu.SemaphoreType.DMA((22,)),
+            pltpu.SemaphoreType.DMA((16,)),
+        ],
+        compiler_params=pltpu.CompilerParams(vmem_limit_bytes=VMEM),
+        cost_estimate=pl.CostEstimate(flops=flops, bytes_accessed=moved, transcendentals=0),
+    )(ids, *pieces, down_w, gate_w, up_w, parts)
+    return out[:4], out[4], out[5], out[6], out[7]
+
+
+def weight_kernel(rounds, slot_cap, *refs):
+    count = 4 * rounds
+    pieces, rows = refs[:count], refs[count:count + rounds]
+    dgu, scaled = refs[count + rounds:count + 2 * rounds], refs[count + 2 * rounds:count + 3 * rounds]
+    slots = refs[count + 3 * rounds:count + 4 * rounds]
+    gate_out, up_out, down_out, all_x, all_dy, all_dgu, all_scaled = refs[count + 4 * rounds:]
+    taken = 4 * slot_cap
+    hid = gate_out.shape[1]
+
+    @pl.when(pl.program_id(0) == 0)
+    def _():
+        for r in range(rounds):
+            all_dgu[r * taken:(r + 1) * taken, :] = dgu[r][...]
+            all_scaled[r * taken:(r + 1) * taken, :] = scaled[r][...]
+
+    for i in range(count):
+        select = as_bf16(slot_hits(slots[i // 4][i % 4], slot_cap))
+        picked = jnp.dot(select, pieces[i][...], preferred_element_type=jnp.float32)
+        all_x[i * slot_cap:(i + 1) * slot_cap, :] = picked.astype(jnp.bfloat16)
+    for r in range(rounds):
+        all_dy[r * taken:(r + 1) * taken, :] = rows[r][...]
+    grads = dot_tn(all_x[...], all_dgu[...])
+    gate_out[...] = grads[:, :hid].astype(jnp.bfloat16)
+    up_out[...] = grads[:, hid:].astype(jnp.bfloat16)
+    down_out[...] = dot_tn(all_scaled[...], all_dy[...]).astype(jnp.bfloat16)
+
+
+def weight_grads(pieces, rows, dgu, scaled, slots):
+    rounds, count = len(rows), len(pieces)
+    size, width = pieces[0].shape
+    taken, hid = scaled[0].shape
+    half = jnp.bfloat16
+
+    def columns(height):
+        return pl.BlockSpec((height, TILE), lambda i: (0, i))
+
+    def whole(shape):
+        return pl.BlockSpec(shape, lambda i: (0,) * len(shape))
+
+    slot_cap, total = taken // 4, rounds * taken
+    flops = 2 * total * width * (3 * hid + size)
+    moved = 2 * (count * size * width + total * (width + 3 * hid) + 3 * width * hid)
+    return pl.pallas_call(
+        functools.partial(weight_kernel, rounds, slot_cap),
+        grid=(width // TILE,),
+        out_shape=[
+            jax.ShapeDtypeStruct((width, hid), half),
+            jax.ShapeDtypeStruct((width, hid), half),
+            jax.ShapeDtypeStruct((hid, width), half),
+        ],
+        in_specs=[columns(size)] * count
+        + [columns(taken)] * rounds
+        + [whole((taken, 2 * hid))] * rounds
+        + [whole((taken, hid))] * rounds
+        + [whole(slots[0].shape)] * rounds,
+        out_specs=[
+            pl.BlockSpec((TILE, hid), lambda i: (i, 0)),
+            pl.BlockSpec((TILE, hid), lambda i: (i, 0)),
+            columns(hid),
+        ],
+        scratch_shapes=[
+            pltpu.VMEM((total, TILE), half),
+            pltpu.VMEM((total, TILE), half),
+            pltpu.VMEM((total, 2 * hid), half),
+            pltpu.VMEM((total, hid), half),
+        ],
+        compiler_params=pltpu.CompilerParams(vmem_limit_bytes=56 << 20),
+        cost_estimate=pl.CostEstimate(flops=flops, bytes_accessed=moved, transcendentals=0),
+    )(*pieces, *rows, *dgu, *scaled, *slots)
+
+
+def after(value, *others):
+    return value if not others else lax.optimization_barrier((value, *others))[0]
+
+
+class Links:
+    def __init__(self, depth):
+        self.depth, self.arrived = depth, []
+
+    def send(self, value, axis, pairs):
+        if len(self.arrived) >= self.depth:
+            value = after(value, self.arrived[-self.depth])
+        got = lax.ppermute(value, axis, pairs)
+        self.arrived.append(got)
+        return got
+
+
+def add(*terms):
+    total = terms[0].astype(jnp.float32)
+    for term in terms[1:]:
+        total = total + term.astype(jnp.float32)
+    return total.astype(jnp.bfloat16)
+
+
+def with_router(grad_out, routes, probs):
+    count, width = grad_out.shape
+    chosen = probs.shape[1]
+    extra = -(-chosen // 8) * 8
+    fill = ((0, extra - chosen), (0, 0))
+    routes = jnp.pad(routes.T.astype(jnp.bfloat16), fill, constant_values=-1)
+    info = jnp.concatenate([routes, jnp.pad(probs.T, fill)], axis=1)
+    return jnp.concatenate([grad_out, jnp.pad(info, ((0, 0), (0, width - 2 * count)))], axis=0)
+
+
+def gather_local(tokens, grad_out, probs, routes, w_gate, w_up, w_down, gate_pre, up_pre):
+    ring = lax.axis_size("seq")
+    experts = ring * lax.axis_size("expert")
+    count, width = tokens.shape
+    chosen = probs.shape[1]
+    slot_cap = gate_pre.shape[1] // experts
+    seq_place, expert_place = lax.axis_index("seq"), lax.axis_index("expert")
+    core_pairs = [(i, i ^ 1) for i in range(4)]
+    side_pairs = [(i, i ^ 2) for i in range(4)]
+    side, line = Links(2), Links(3)
+
+    def shift(value, by):
+        return line.send(value, "seq", [(i, (i + by) % ring) for i in range(ring)])
+
+    def across(value):
+        return side.send(value, "expert", side_pairs)
+
+    def other_core(value):
+        return lax.ppermute(value, "expert", core_pairs)
+
+    own_expert = expert_place * ring + seq_place
+
+    def ids_of(s):
+        place = (seq_place - s) % ring
+        return jnp.stack([(expert_place ^ flip) * ring + place for flip in (0, 2, 1, 3)] + [own_expert])
+
+    parts = slopes(gate_pre.reshape(experts, slot_cap, -1), up_pre.reshape(experts, slot_cap, -1))
+    rows, dgu, scaled, slots, own, away, sums = {}, {}, {}, {}, {}, {}, {}
+
+    def compute(s):
+        pieces = (dy[s], dy_side[s], other_core(dy[s]), other_core(dy_side[s]))
+        dx, rows[s], dgu[s], scaled[s], slots[s] = round_backward(
+            ids_of(s).astype(jnp.int32), count, pieces, w_down[0], w_gate[0], w_up[0], parts
+        )
+        own[s] = (dx[0], other_core(dx[2]))
+        away[s] = add(dx[1], other_core(dx[3]))
+
+    def give_back(s):
+        sums[s] = (*own[s], across(away[s]))
+        if s:
+            sums[s] = (shift(add(*sums[s]), -s),)
+
+    own_routes = lax.dynamic_slice_in_dim(routes, seq_place * count, count, 0)
+    dy, x = {0: with_router(grad_out, own_routes, probs)}, {0: tokens}
+    dy_side, x_side = {}, {}
+    shifts = sorted(range(ring), key=lambda s: (min(s, ring - s), s))
+    for s in shifts[1:]:
+        dy[s] = shift(dy[0], s)
+    dy_side[0] = across(dy[0])
+    x_side[0] = across(x[0])
+    done = []
+    for s in shifts[1:]:
+        dy_side[s] = across(after(dy[s], *done))
+        compute(shifts[len(done)])
+        done.append(slots[shifts[len(done)]])
+    for s in range(1, ring):
+        x[s] = shift(x[s - 1], 1)
+    for s in shifts:
+        if s not in slots:
+            compute(s)
+        give_back(s)
+    for s in range(1, ring):
+        x_side[s] = across(x[s])
+
+    back = [term for s in shifts for term in sums[s]]
+    total = add(*back)
+    pieces = []
+    for s in shifts:
+        pieces += [x[s], x_side[s], other_core(x[s]), other_core(x_side[s])]
+    grads = weight_grads(
+        pieces, *[[part[s] for s in shifts] for part in (rows, dgu, scaled, slots)]
+    )
+    grad_probs = total[count:count + chosen, :count].T
+    return (total[:count], grad_probs, *[grad[None] for grad in grads])
+
+
+def local(tokens, grad_out, probs, routes, w_gate, w_up, w_down, gate_pre, up_pre):
+    experts = lax.axis_size("seq") * lax.axis_size("expert")
+    gathers = experts * tokens.shape[0] <= 2 * gate_pre.shape[1] and experts <= 256
+    plan = gather_local if gathers and lax.axis_size("expert") == 4 else exchange_local
+    return plan(tokens, grad_out, probs, routes, w_gate, w_up, w_down, gate_pre, up_pre)
 
 
 def solution(mesh):

time: 490 us -> 197 us (0.40)
  waiting for transfers between devices: 299 us -> 107 us
  local copies, waits for them, and re-layouts: 115 us -> 7.9 us
  Pallas kernels: 0 us -> 52.1 us
  matrix products: 41.7 us -> 0 us
  starting transfers between devices: 27.8 us -> 19.4 us
    all_to_all x5 -> x0, waiting for transfers between devices: 299 us -> none  [the longest x1 111 us: local(): lax.all_to_all(send_dy, ('expert', 'seq'), split_axis=0, concat_axis=0, t...]
    ppermute x0 -> x45, waiting for transfers between devices: none -> 107 us  [the longest x21 107 us: send(): got = lax.ppermute(value, axis, pairs)]
    gather x16 -> x0, local copies, waits for them, and re-layouts: 103 us -> none  [the longest x8 40.8 us: local(): summed = summed + flat_x[own_places[:, column]].astype(jnp.float32)]
    pallas_call x0 -> x6, Pallas kernels: none -> 52.1 us  [the longest x4 32.7 us: round_backward(): pl.pallas_call(round_kernel, out_shape=[jax.ShapeDtypeStruct((height, wid...]
    dot_general x6 -> x0, matrix products: 41.7 us -> none  [the longest x1 7.82 us: expert_backward(): back_rows = jnp.dot(rows_dy, down_w.T, preferred_element_type=jnp.float32)]
    all_to_all x5 -> x0, starting transfers between devices: 27.8 us -> none  [the longest x1 7.36 us: local(): lax.all_to_all(send_p, ('expert', 'seq'), split_axis=0, concat_axis=0, ti...]
    ppermute x0 -> x45, starting transfers between devices: none -> 19.4 us  [the longest x21 16.9 us: send(): got = lax.ppermute(value, axis, pairs)]
  transfers between devices with their start and end apart: 5 -> 45, of which waited for: 4 -> 16; matrix products, arithmetic and copies ran while one was open for 13% -> 5% of each run, Pallas kernels for 0% -> 20%
where the time goes in v2:
time: 197 us; the launch traced here: 196 us
  waiting for transfers between devices  107 us (54%)
  Pallas kernels  52.1 us (26%)
  starting transfers between devices  19.4 us (10%)
  other arithmetic  8.61 us (4%)
  local copies, waits for them, and re-layouts  7.9 us (4%)
    ppermute x21, waiting for transfers between devices, send(): got = lax.ppermute(value, axis, pairs)  107 us
    pallas_call x4, Pallas kernels, round_backward(): pl.pallas_call(round_kernel, out_shape=[jax.ShapeDtypeStruct((height, wid...  32.7 us
    ppermute x21, starting transfers between devices, send(): got = lax.ppermute(value, axis, pairs)  16.9 us
    pallas_call x1, Pallas kernels, weight_grads(): pl.pallas_call(functools.partial(weight_kernel, rounds, slot_cap), grid=(...  12.7 us
    pallas_call x1, Pallas kernels, slopes(): pl.pallas_call(slope_kernel, grid=(blocks // 2,), out_shape=jax.ShapeDtyp...  6.73 us
    convert_element_type x8, other arithmetic, add(): return total.astype(jnp.bfloat16)  6.16 us
  transfers between devices with their start and end apart: 45, of which 16 were waited for; matrix products, arithmetic and copies ran while one was open for 5% of the time, Pallas kernels for 20%

profile of v2, /device:TPU:0, one launch (start us, length us, event | category | flops | bytes accessed | tf_op | source)
XLA Modules:
  0.0 196.3 jit_solution(1038523677946425641)
XLA Ops:
  0.6 0.7 fusion.3
  1.3 0.7 fusion.2
  2.0 1.1 pad_maximum_fusion.dy0
  3.1 3.0 %collective-permute-start = (bf16[136,2048]{1,0:T(8,128)(2,1)S(1)}, bf16[136,2048]{1,0:T(8,128)(2,1)S(1)}, u32[]{:S(2)}, u32[]{:S(2)}) collective-permute-start(bf16[136,2048]{1,0:T(8,128)(2,1)S(1)} %pad_maximum_fusion.dy0), channel_id=1, source_target_pairs={{0,8},{4,12},{8,0},{12,4},{1,9},{5,13},{9,1},{13,5},{2,10},{6,14},... | collective-permute-start | bytes 1671176 | tf_op jit(solution)/shard_map/ppermute | solution.py:405
  6.1 1.6 collective-permute-start.9
  7.7 11.0 %collective-permute-done.dy1 = bf16[136,2048]{1,0:T(8,128)(2,1)S(1)} collective-permute-done((bf16[136,2048]{1,0:T(8,128)(2,1)S(1)}, bf16[136,2048]{1,0:T(8,128)(2,1)S(1)}, u32[]{:S(2)}, u32[]{:S(2)}) %collective-permute-start) | collective-permute-done | bytes 557088 | tf_op jit(solution)/shard_map/ppermute | solution.py:405
  18.7 3.3 %collective-permute-done.9.dy0 = bf16[136,2048]{1,0:T(8,128)(2,1)S(1)} collective-permute-done((bf16[136,2048]{1,0:T(8,128)(2,1)S(1)}, bf16[136,2048]{1,0:T(8,128)(2,1)S(1)}, u32[]{:S(2)}, u32[]{:S(2)}) %collective-permute-start.9) | collective-permute-done | bytes 557088 | tf_op jit(solution)/shard_map/ppermute | solution.py:405
  22.6 1.7 collective-permute-start.5
  24.3 1.5 collective-permute-start.6
  25.9 0.7 stack.71.ids_ref
  26.6 6.7 %shard_map.128.slope_hbm = f32[16,80,1152]{2,1,0:T(8,128)} custom-call(bf16[16,80,384]{2,1,0:T(8,128)(2,1)} %bitcast.42, bf16[16,80,384]{2,1,0:T(8,128)(2,1)} %bitcast.43), custom_call_target="tpu_custom_call" | custom-call | flops 4915200 | bytes 7864320 | tf_op jit(solution)/shard_map/pallas_call | solution.py:153
  33.5 4.0 %collective-permute-done.10.dy1 = bf16[136,2048]{1,0:T(8,128)(2,1)S(1)} collective-permute-done((bf16[136,2048]{1,0:T(8,128)(2,1)S(1)}, bf16[136,2048]{1,0:T(8,128)(2,1)S(1)}, u32[]{:S(2)}, u32[]{:S(2)}) %collective-permute-start.10) | collective-permute-done | bytes 557088 | tf_op jit(solution)/shard_map/ppermute | solution.py:405
  37.5 8.2 %shard_map.129 = (bf16[136,2048]{1,0:T(8,128)(2,1)}, bf16[136,2048]{1,0:T(8,128)(2,1)}, bf16[136,2048]{1,0:T(8,128)(2,1)}, bf16[136,2048]{1,0:T(8,128)(2,1)}, bf...) custom-call(s32[5]{0:T(128)} %stack.71.ids_ref, ...), custom_call_target="tpu_custom_call" | custom-call | flops 1845493760 | bytes 11714560 | tf_op jit(solution)/shard_map/pallas_call | solution.py:292
  45.7 2.7 %collective-permute-done.6.refs_1_ = bf16[128,2048]{1,0:T(8,128)(2,1)} collective-permute-done((bf16[128,2048]{1,0:T(8,128)(2,1)}, bf16[128,2048]{1,0:T(8,128)(2,1)}, u32[]{:S(2)}, u32[]{:S(2)}) %collective-permute-start.6) | collective-permute-done | bytes 524320 | tf_op jit(solution)/shard_map/ppermute | solution.py:405
  49.0 0.7 stack.76.ids_ref
  50.2 8.2 %shard_map.130 = (bf16[136,2048]{1,0:T(8,128)(2,1)}, bf16[136,2048]{1,0:T(8,128)(2,1)}, bf16[136,2048]{1,0:T(8,128)(2,1)}, bf16[136,2048]{1,0:T(8,128)(2,1)}, bf...) custom-call(s32[5]{0:T(128)} %stack.76.ids_ref, ...), custom_call_target="tpu_custom_call" | custom-call | flops 1845493760 | bytes 11714560 | tf_op jit(solution)/shard_map/pallas_call | solution.py:292
  58.4 14.0 %collective-permute-done.15.dy0 = bf16[136,2048]{1,0:T(8,128)(2,1)S(1)} collective-permute-done((bf16[136,2048]{1,0:T(8,128)(2,1)S(1)}, bf16[136,2048]{1,0:T(8,128)(2,1)S(1)}, u32[]{:S(2)}, u32[]{:S(2)}) %collective-permute-start.15) | collective-permute-done | bytes 557088 | tf_op jit(solution)/shard_map/ppermute | solution.py:405
  72.4 0.7 collective-permute-start.16
  73.2 0.6 stack.86.ids_ref
  74.9 2.2 %add_convert_fusion.7 = bf16[136,2048]{1,0:T(8,128)(2,1)} fusion(bf16[136,2048]{1,0:T(8,128)(2,1)} %collective-permute-done.4, bf16[136,2048]{1,0:T(8,128)(2,1)} %get-tuple-element.60), kind=kLoop, calls=%fused_computation.7 | loop fusion | flops 1114112 | bytes 1671168 | tf_op jit(solution)/shard_map/convert_element_type | solution.py:414
  77.1 9.7 %collective-permute-done.16.dy1 = bf16[136,2048]{1,0:T(8,128)(2,1)S(1)} collective-permute-done((bf16[136,2048]{1,0:T(8,128)(2,1)S(1)}, bf16[136,2048]{1,0:T(8,128)(2,1)S(1)}, u32[]{:S(2)}, u32[]{:S(2)}) %collective-permute-start.16) | collective-permute-done | bytes 557088 | tf_op jit(solution)/shard_map/ppermute | solution.py:405
  86.7 0.7 collective-permute-start.8
  87.5 0.8 copy-done.8
  88.3 8.2 %shard_map.131 = (bf16[136,2048]{1,0:T(8,128)(2,1)}, bf16[136,2048]{1,0:T(8,128)(2,1)}, bf16[136,2048]{1,0:T(8,128)(2,1)}, bf16[136,2048]{1,0:T(8,128)(2,1)}, bf...) custom-call(s32[5]{0:T(128)} %stack.81.ids_ref, ...), custom_call_target="tpu_custom_call" | custom-call | flops 1845493760 | bytes 11714560 | tf_op jit(solution)/shard_map/pallas_call | solution.py:292
  96.6 1.4 add_convert_fusion.6
  98.0 1.4 collective-permute-start.17
  99.3 0.8 copy-done.12
  100.1 8.2 %shard_map.132 = (bf16[136,2048]{1,0:T(8,128)(2,1)}, bf16[136,2048]{1,0:T(8,128)(2,1)}, bf16[136,2048]{1,0:T(8,128)(2,1)}, bf16[136,2048]{1,0:T(8,128)(2,1)}, bf...) custom-call(s32[5]{0:T(128)} %stack.86.ids_ref, ...), custom_call_target="tpu_custom_call" | custom-call | flops 1845493760 | bytes 11714560 | tf_op jit(solution)/shard_map/pallas_call | solution.py:292
  109.1 0.8 collective-permute-start.24
  110.1 3.4 %collective-permute-done.17 = bf16[136,2048]{1,0:T(8,128)(2,1)S(1)} collective-permute-done((bf16[136,2048]{1,0:T(8,128)(2,1)S(1)}, bf16[136,2048]{1,0:T(8,128)(2,1)S(1)}, u32[]{:S(2)}, u32[]{:S(2)}) %collective-permute-start.17) | collective-permute-done | bytes 557088 | tf_op jit(solution)/shard_map/ppermute | solution.py:405
  114.3 10.6 %collective-permute-done.24 = bf16[136,2048]{1,0:T(8,128)(2,1)S(1)} collective-permute-done((bf16[136,2048]{1,0:T(8,128)(2,1)S(1)}, bf16[136,2048]{1,0:T(8,128)(2,1)S(1)}, u32[]{:S(2)}, u32[]{:S(2)}) %collective-permute-start.24) | collective-permute-done | bytes 557088 | tf_op jit(solution)/shard_map/ppermute | solution.py:405
  125.0 1.3 collective-permute-start.31
  126.6 0.8 copy-done.19
  127.4 0.7 collective-permute-start.36
  128.4 1.7 collective-permute-done.32.refs_8_
  130.2 10.4 %collective-permute-done.31 = bf16[136,2048]{1,0:T(8,128)(2,1)S(1)} collective-permute-done((bf16[136,2048]{1,0:T(8,128)(2,1)S(1)}, bf16[136,2048]{1,0:T(8,128)(2,1)S(1)}, u32[]{:S(2)}, u32[]{:S(2)}) %collective-permute-start.31) | collective-permute-done | bytes 557088 | tf_op jit(solution)/shard_map/ppermute | solution.py:405
  140.8 9.7 %collective-permute-done.36.refs_5_ = bf16[128,2048]{1,0:T(8,128)(2,1)S(1)} collective-permute-done((bf16[128,2048]{1,0:T(8,128)(2,1)}, bf16[128,2048]{1,0:T(8,128)(2,1)S(1)}, u32[]{:S(2)}, u32[]{:S(2)}) %collective-permute-start.36) | collective-permute-done | bytes 524320 | tf_op jit(solution)/shard_map/ppermute | solution.py:405
  150.5 1.4 collective-permute-start.39
  151.9 0.7 collective-permute-start.42
  152.6 3.7 %collective-permute-done.19 = bf16[136,2048]{1,0:T(8,128)(2,1)S(1)} collective-permute-done((bf16[136,2048]{1,0:T(8,128)(2,1)S(1)}, bf16[136,2048]{1,0:T(8,128)(2,1)S(1)}, u32[]{:S(2)}, u32[]{:S(2)}) %collective-permute-start.19) | collective-permute-done | bytes 557088 | tf_op jit(solution)/shard_map/ppermute | solution.py:405
  156.3 1.7 collective-permute-done.26
  158.0 7.4 %collective-permute-done.39.refs_9_ = bf16[128,2048]{1,0:T(8,128)(2,1)S(1)} collective-permute-done((bf16[128,2048]{1,0:T(8,128)(2,1)S(1)}, bf16[128,2048]{1,0:T(8,128)(2,1)S(1)}, u32[]{:S(2)}, u32[]{:S(2)}) %collective-permute-start.39) | collective-permute-done | bytes 524320 | tf_op jit(solution)/shard_map/ppermute | solution.py:405
  165.4 9.0 %collective-permute-done.42.refs_13_ = bf16[128,2048]{1,0:T(8,128)(2,1)S(1)} collective-permute-done((bf16[128,2048]{1,0:T(8,128)(2,1)}, bf16[128,2048]{1,0:T(8,128)(2,1)S(1)}, u32[]{:S(2)}, u32[]{:S(2)}) %collective-permute-start.42) | collective-permute-done | bytes 524320 | tf_op jit(solution)/shard_map/ppermute | solution.py:405
  174.4 4.5 %collective-permute-done.33 = bf16[136,2048]{1,0:T(8,128)(2,1)S(1)} collective-permute-done((bf16[136,2048]{1,0:T(8,128)(2,1)S(1)}, bf16[136,2048]{1,0:T(8,128)(2,1)S(1)}, u32[]{:S(2)}, u32[]{:S(2)}) %collective-permute-start.33) | collective-permute-done | bytes 557088 | tf_op jit(solution)/shard_map/ppermute | solution.py:405
  178.9 1.6 add_convert_fusion
  180.6 0.8 slice.8
  182.1 0.7 copy-done.29
  183.5 12.7 %shard_map.133 = (bf16[2048,384]{1,0:T(8,128)(2,1)}, bf16[2048,384]{1,0:T(8,128)(2,1)}, bf16[384,2048]{1,0:T(8,128)(2,1)}) custom-call(bf16[128,2048]{1,0:T(8,128)(2,1)} %refs_0_.1, bf16[128,2048]{1,0:T(8,128)(2,1)} %collective-permute-done.6.refs_1_, bf16[128,2048]{1,0:T(8,128)(2,1)} %copy-done.22, bf16[128,2048]{1,0:T(8,128)(2,1)} %copy-done.23, ...), custom_call_target="tpu_custom_call" | custom-call | flops 6710886400 | bytes 21299200 | tf_op jit(solution)/shard_map/pallas_call | solution.py:365
  (133 shorter events, 6.9 us)
Async XLA Ops:
  3.1 30.3 %copy-start = (bf16[136,2048]{1,0:T(8,128)(2,1)}, bf16[136,2048]{1,0:T(8,128)(2,1)S(1)}, u32[]{:S(2)}) copy-start(bf16[136,2048]{1,0:T(8,128)(2,1)S(1)} %pad_maximum_fusion.dy0) | copy-start | bytes 1671172
  3.1 15.6 %collective-permute-start = (bf16[136,2048]{1,0:T(8,128)(2,1)S(1)}, bf16[136,2048]{1,0:T(8,128)(2,1)S(1)}, u32[]{:S(2)}, u32[]{:S(2)}) collective-permute-start(bf16[136,2048]{1,0:T(8,128)(2,1)S(1)} %pad_maximum_fusion.dy0), channel_id=1, source_target_pairs={{0,8},{4,12},{8,0},{12,4},{1,9},{5,13},{9,1},{13,5},{2,10},{6,14},... | collective-permute-start | bytes 1671176 | tf_op jit(solution)/shard_map/ppermute | solution.py:405
  6.1 15.9 %collective-permute-start.9 = (bf16[136,2048]{1,0:T(8,128)(2,1)S(1)}, bf16[136,2048]{1,0:T(8,128)(2,1)S(1)}, u32[]{:S(2)}, u32[]{:S(2)}) collective-permute-start(bf16[136,2048]{1,0:T(8,128)(2,1)S(1)} %pad_maximum_fusion.dy0), channel_id=1, source_target_pairs={{0,1},{1,2},{2,3},{3,0},{4,5},{5,6},{6,7},{7,4},{8,9},{9,10},{10,1... | collective-permute-start | bytes 1671176 | tf_op jit(solution)/shard_map/ppermute | solution.py:405
  7.7 18.1 %collective-permute-start.1 = (bf16[136,2048]{1,0:T(8,128)(2,1)S(1)}, bf16[136,2048]{1,0:T(8,128)(2,1)S(1)}, u32[]{:S(2)}, u32[]{:S(2)}) collective-permute-start(bf16[136,2048]{1,0:T(8,128)(2,1)S(1)} %pad_maximum_fusion.dy0), channel_id=1, source_target_pairs={{0,4},{4,0},{8,12},{12,8},{1,5},{5,1},{9,13},{13,9},{2,6},{6,2},{1... | collective-permute-start | bytes 1671176 | tf_op jit(solution)/shard_map/ppermute | solution.py:445
  22.1 11.3 %collective-permute-start.2 = (bf16[136,2048]{1,0:T(8,128)(2,1)S(1)}, bf16[136,2048]{1,0:T(8,128)(2,1)}, u32[]{:S(2)}, u32[]{:S(2)}) collective-permute-start(bf16[136,2048]{1,0:T(8,128)(2,1)S(1)} %collective-permute-done.dy1), channel_id=1, source_target_pairs={{0,4},{4,0},{8,12},{12,8},{1,5},{5,1},{9,13},{13,9},{2,6},{6,2},{1... | collective-permute-start | bytes 1671176 | tf_op jit(solution)/shard_map/ppermute | solution.py:445
  22.1 15.4 %collective-permute-start.10 = (bf16[136,2048]{1,0:T(8,128)(2,1)S(1)}, bf16[136,2048]{1,0:T(8,128)(2,1)S(1)}, u32[]{:S(2)}, u32[]{:S(2)}) collective-permute-start(bf16[136,2048]{1,0:T(8,128)(2,1)S(1)} %collective-permute-done.9.dy0), channel_id=1, source_target_pairs={{0,8},{4,12},{8,0},{12,4},{1,9},{5,13},{9,1},{13,5},{2,10},{6,14},... | collective-permute-start | bytes 1671176 | tf_op jit(solution)/shard_map/ppermute | solution.py:405
  22.6 23.1 %collective-permute-start.5 = (bf16[136,2048]{1,0:T(8,128)(2,1)S(1)}, bf16[136,2048]{1,0:T(8,128)(2,1)S(1)}, u32[]{:S(2)}, u32[]{:S(2)}) collective-permute-start(bf16[136,2048]{1,0:T(8,128)(2,1)S(1)} %pad_maximum_fusion.dy0), channel_id=1, source_target_pairs={{0,3},{1,0},{2,1},{3,2},{4,7},{5,4},{6,5},{7,6},{8,11},{9,8},{10,9... | collective-permute-start | bytes 1671176 | tf_op jit(solution)/shard_map/ppermute | solution.py:405
  24.3 24.1 %collective-permute-start.6 = (bf16[128,2048]{1,0:T(8,128)(2,1)}, bf16[128,2048]{1,0:T(8,128)(2,1)}, u32[]{:S(2)}, u32[]{:S(2)}) collective-permute-start(bf16[128,2048]{1,0:T(8,128)(2,1)} %refs_0_.1), channel_id=1, source_target_pairs={{0,8},{4,12},{8,0},{12,4},{1,9},{5,13},{9,1},{13,5},{2,10},{6,14},... | collective-permute-start | bytes 1572872 | tf_op jit(solution)/shard_map/ppermute | solution.py:405
  25.8 23.1 %collective-permute-start.11 = (bf16[136,2048]{1,0:T(8,128)(2,1)S(1)}, bf16[136,2048]{1,0:T(8,128)(2,1)}, u32[]{:S(2)}, u32[]{:S(2)}) collective-permute-start(bf16[136,2048]{1,0:T(8,128)(2,1)S(1)} %collective-permute-done.9.dy0), channel_id=1, source_target_pairs={{0,4},{4,0},{8,12},{12,8},{1,5},{5,1},{9,13},{13,9},{2,6},{6,2},{1... | collective-permute-start | bytes 1671176 | tf_op jit(solution)/shard_map/ppermute | solution.py:445
  33.4 39.0 %collective-permute-start.15 = (bf16[136,2048]{1,0:T(8,128)(2,1)S(1)}, bf16[136,2048]{1,0:T(8,128)(2,1)S(1)}, u32[]{:S(2)}, u32[]{:S(2)}) collective-permute-start(bf16[136,2048]{1,0:T(8,128)(2,1)S(1)} %pad_maximum_fusion.dy0), channel_id=1, source_target_pairs={{0,2},{1,3},{2,0},{3,1},{4,6},{5,7},{6,4},{7,5},{8,10},{9,11},{10,... | collective-permute-start | bytes 1671176 | tf_op jit(solution)/shard_map/ppermute | solution.py:405
  37.5 12.2 %collective-permute-start.12 = (bf16[136,2048]{1,0:T(8,128)(2,1)S(1)}, bf16[136,2048]{1,0:T(8,128)(2,1)}, u32[]{:S(2)}, u32[]{:S(2)}) collective-permute-start(bf16[136,2048]{1,0:T(8,128)(2,1)S(1)} %collective-permute-done.10.dy1), channel_id=1, source_target_pairs={{0,4},{4,0},{8,12},{12,8},{1,5},{5,1},{9,13},{13,9},{2,6},{6,2},{1... | collective-permute-start | bytes 1671176 | tf_op jit(solution)/shard_map/ppermute | solution.py:445
  48.4 24.7 %collective-permute-start.7 = (bf16[136,2048]{1,0:T(8,128)(2,1)S(1)}, bf16[136,2048]{1,0:T(8,128)(2,1)S(1)}, u32[]{:S(2)}, u32[]{:S(2)}) collective-permute-start(bf16[136,2048]{1,0:T(8,128)(2,1)S(1)} %collective-permute-done.5.dy0), channel_id=1, source_target_pairs={{0,8},{4,12},{8,0},{12,4},{1,9},{5,13},{9,1},{13,5},{2,10},{6,14},... | collective-permute-start | bytes 1671176 | tf_op jit(solution)/shard_map/ppermute | solution.py:405
  49.0 25.8 %collective-permute-start.4 = (bf16[136,2048]{1,0:T(8,128)(2,1)}, bf16[136,2048]{1,0:T(8,128)(2,1)}, u32[]{:S(2)}, u32[]{:S(2)}) collective-permute-start(bf16[136,2048]{1,0:T(8,128)(2,1)} %get-tuple-element.61), channel_id=1, source_target_pairs={{0,4},{4,0},{8,12},{12,8},{1,5},{5,1},{9,13},{13,9},{2,6},{6,2},{1... | collective-permute-start | bytes 1671176 | tf_op jit(solution)/shard_map/ppermute | solution.py:445
  49.0 25.4 %collective-permute-start.18 = (bf16[128,2048]{1,0:T(8,128)(2,1)}, bf16[128,2048]{1,0:T(8,128)(2,1)}, u32[]{:S(2)}, u32[]{:S(2)}) collective-permute-start(bf16[128,2048]{1,0:T(8,128)(2,1)} %refs_0_.1), channel_id=1, source_target_pairs={{0,1},{1,2},{2,3},{3,0},{4,5},{5,6},{6,7},{7,4},{8,9},{9,10},{10,1... | collective-permute-start | bytes 1572872 | tf_op jit(solution)/shard_map/ppermute | solution.py:405
  49.7 27.4 %collective-permute-start.20 = (bf16[136,2048]{1,0:T(8,128)(2,1)S(1)}, bf16[136,2048]{1,0:T(8,128)(2,1)S(1)}, u32[]{:S(2)}, u32[]{:S(2)}) collective-permute-start(bf16[136,2048]{1,0:T(8,128)(2,1)S(1)} %collective-permute-done.5.dy0), channel_id=1, source_target_pairs={{0,4},{4,0},{8,12},{12,8},{1,5},{5,1},{9,13},{13,9},{2,6},{6,2},{1... | collective-permute-start | bytes 1671176 | tf_op jit(solution)/shard_map/ppermute | solution.py:445
  72.4 14.4 %collective-permute-start.16 = (bf16[136,2048]{1,0:T(8,128)(2,1)S(1)}, bf16[136,2048]{1,0:T(8,128)(2,1)S(1)}, u32[]{:S(2)}, u32[]{:S(2)}) collective-permute-start(bf16[136,2048]{1,0:T(8,128)(2,1)S(1)} %collective-permute-done.15.dy0), channel_id=1, source_target_pairs={{0,8},{4,12},{8,0},{12,4},{1,9},{5,13},{9,1},{13,5},{2,10},{6,14},... | collective-permute-start | bytes 1671176 | tf_op jit(solution)/shard_map/ppermute | solution.py:405
  73.1 14.3 %collective-permute-start.21 = (bf16[136,2048]{1,0:T(8,128)(2,1)S(1)}, bf16[136,2048]{1,0:T(8,128)(2,1)S(1)}, u32[]{:S(2)}, u32[]{:S(2)}) collective-permute-start(bf16[136,2048]{1,0:T(8,128)(2,1)S(1)} %collective-permute-done.7.dy1), channel_id=1, source_target_pairs={{0,4},{4,0},{8,12},{12,8},{1,5},{5,1},{9,13},{13,9},{2,6},{6,2},{1... | collective-permute-start | bytes 1671176 | tf_op jit(solution)/shard_map/ppermute | solution.py:445
  74.4 23.5 %collective-permute-start.27 = (bf16[136,2048]{1,0:T(8,128)(2,1)S(1)}, bf16[136,2048]{1,0:T(8,128)(2,1)S(1)}, u32[]{:S(2)}, u32[]{:S(2)}) collective-permute-start(bf16[136,2048]{1,0:T(8,128)(2,1)S(1)} %collective-permute-done.15.dy0), channel_id=1, source_target_pairs={{0,4},{4,0},{8,12},{12,8},{1,5},{5,1},{9,13},{13,9},{2,6},{6,2},{1... | collective-permute-start | bytes 1671176 | tf_op jit(solution)/shard_map/ppermute | solution.py:445
  74.8 21.7 %collective-permute-start.14 = (bf16[136,2048]{1,0:T(8,128)(2,1)}, bf16[136,2048]{1,0:T(8,128)(2,1)}, u32[]{:S(2)}, u32[]{:S(2)}) collective-permute-start(bf16[136,2048]{1,0:T(8,128)(2,1)} %get-tuple-element.70), channel_id=1, source_target_pairs={{0,4},{4,0},{8,12},{12,8},{1,5},{5,1},{9,13},{13,9},{2,6},{6,2},{1... | collective-permute-start | bytes 1671176 | tf_op jit(solution)/shard_map/ppermute | solution.py:445
  77.1 32.8 %collective-permute-start.25 = (bf16[128,2048]{1,0:T(8,128)(2,1)}, bf16[128,2048]{1,0:T(8,128)(2,1)}, u32[]{:S(2)}, u32[]{:S(2)}) collective-permute-start(bf16[128,2048]{1,0:T(8,128)(2,1)} %collective-permute-done.18.refs_4_), channel_id=1, source_target_pairs={{0,1},{1,2},{2,3},{3,0},{4,5},{5,6},{6,7},{7,4},{8,9},{9,10},{10,1... | collective-permute-start | bytes 1572872 | tf_op jit(solution)/shard_map/ppermute | solution.py:405
  86.7 22.3 %collective-permute-start.8 = (bf16[136,2048]{1,0:T(8,128)(2,1)}, bf16[136,2048]{1,0:T(8,128)(2,1)}, u32[]{:S(2)}, u32[]{:S(2)}) collective-permute-start(bf16[136,2048]{1,0:T(8,128)(2,1)} %add_convert_fusion.7), channel_id=1, source_target_pairs={{0,8},{4,12},{8,0},{12,4},{1,9},{5,13},{9,1},{13,5},{2,10},{6,14},... | collective-permute-start | bytes 1671176 | tf_op jit(solution)/shard_map/ppermute | solution.py:405
  87.5 11.9 %collective-permute-start.28 = (bf16[136,2048]{1,0:T(8,128)(2,1)S(1)}, bf16[136,2048]{1,0:T(8,128)(2,1)S(1)}, u32[]{:S(2)}, u32[]{:S(2)}) collective-permute-start(bf16[136,2048]{1,0:T(8,128)(2,1)S(1)} %collective-permute-done.16.dy1), channel_id=1, source_target_pairs={{0,4},{4,0},{8,12},{12,8},{1,5},{5,1},{9,13},{13,9},{2,6},{6,2},{1... | collective-permute-start | bytes 1671176 | tf_op jit(solution)/shard_map/ppermute | solution.py:445
  96.5 12.1 %collective-permute-start.23 = (bf16[136,2048]{1,0:T(8,128)(2,1)}, bf16[136,2048]{1,0:T(8,128)(2,1)S(1)}, u32[]{:S(2)}, u32[]{:S(2)}) collective-permute-start(bf16[136,2048]{1,0:T(8,128)(2,1)} %get-tuple-element.80), channel_id=1, source_target_pairs={{0,4},{4,0},{8,12},{12,8},{1,5},{5,1},{9,13},{13,9},{2,6},{6,2},{1... | collective-permute-start | bytes 1671176 | tf_op jit(solution)/shard_map/ppermute | solution.py:445
  98.0 15.5 %collective-permute-start.17 = (bf16[136,2048]{1,0:T(8,128)(2,1)S(1)}, bf16[136,2048]{1,0:T(8,128)(2,1)S(1)}, u32[]{:S(2)}, u32[]{:S(2)}) collective-permute-start(bf16[136,2048]{1,0:T(8,128)(2,1)S(1)} %add_convert_fusion.6), channel_id=1, source_target_pairs={{0,8},{4,12},{8,0},{12,4},{1,9},{5,13},{9,1},{13,5},{2,10},{6,14},... | collective-permute-start | bytes 1671176 | tf_op jit(solution)/shard_map/ppermute | solution.py:405
  108.3 5.1 %collective-permute-start.30 = (bf16[136,2048]{1,0:T(8,128)(2,1)}, bf16[136,2048]{1,0:T(8,128)(2,1)S(1)}, u32[]{:S(2)}, u32[]{:S(2)}) collective-permute-start(bf16[136,2048]{1,0:T(8,128)(2,1)} %get-tuple-element.87), channel_id=1, source_target_pairs={{0,4},{4,0},{8,12},{12,8},{1,5},{5,1},{9,13},{13,9},{2,6},{6,2},{1... | collective-permute-start | bytes 1671176 | tf_op jit(solution)/shard_map/ppermute | solution.py:445
  108.6 5.6 %collective-permute-start.13 = (bf16[136,2048]{1,0:T(8,128)(2,1)}, bf16[136,2048]{1,0:T(8,128)(2,1)S(1)}, u32[]{:S(2)}, u32[]{:S(2)}) collective-permute-start(bf16[136,2048]{1,0:T(8,128)(2,1)} %get-tuple-element.68), channel_id=1, source_target_pairs={{0,4},{4,0},{8,12},{12,8},{1,5},{5,1},{9,13},{13,9},{2,6},{6,2},{1... | collective-permute-start | bytes 1671176 | tf_op jit(solution)/shard_map/ppermute | solution.py:445
  109.1 15.9 %collective-permute-start.24 = (bf16[136,2048]{1,0:T(8,128)(2,1)S(1)}, bf16[136,2048]{1,0:T(8,128)(2,1)S(1)}, u32[]{:S(2)}, u32[]{:S(2)}) collective-permute-start(bf16[136,2048]{1,0:T(8,128)(2,1)S(1)} %add_convert_fusion.4), channel_id=1, source_target_pairs={{0,8},{4,12},{8,0},{12,4},{1,9},{5,13},{9,1},{13,5},{2,10},{6,14},... | collective-permute-start | bytes 1671176 | tf_op jit(solution)/shard_map/ppermute | solution.py:405
  109.9 4.2 %collective-permute-start.34 = (bf16[128,2048]{1,0:T(8,128)(2,1)}, bf16[128,2048]{1,0:T(8,128)(2,1)S(1)}, u32[]{:S(2)}, u32[]{:S(2)}) collective-permute-start(bf16[128,2048]{1,0:T(8,128)(2,1)} %refs_0_.1), channel_id=1, source_target_pairs={{0,4},{4,0},{8,12},{12,8},{1,5},{5,1},{9,13},{13,9},{2,6},{6,2},{1... | collective-permute-start | bytes 1572872 | tf_op jit(solution)/shard_map/ppermute | solution.py:445
  113.4 13.1 %collective-permute-start.35 = (bf16[128,2048]{1,0:T(8,128)(2,1)}, bf16[128,2048]{1,0:T(8,128)(2,1)S(1)}, u32[]{:S(2)}, u32[]{:S(2)}) collective-permute-start(bf16[128,2048]{1,0:T(8,128)(2,1)} %collective-permute-done.6.refs_1_), channel_id=1, source_target_pairs={{0,4},{4,0},{8,12},{12,8},{1,5},{5,1},{9,13},{13,9},{2,6},{6,2},{1... | collective-permute-start | bytes 1572872 | tf_op jit(solution)/shard_map/ppermute | solution.py:445
  113.5 13.9 %collective-permute-start.22 = (bf16[136,2048]{1,0:T(8,128)(2,1)S(1)}, bf16[136,2048]{1,0:T(8,128)(2,1)S(1)}, u32[]{:S(2)}, u32[]{:S(2)}) collective-permute-start(bf16[136,2048]{1,0:T(8,128)(2,1)S(1)} %copy-done.20), channel_id=1, source_target_pairs={{0,4},{4,0},{8,12},{12,8},{1,5},{5,1},{9,13},{13,9},{2,6},{6,2},{1... | collective-permute-start | bytes 1671176 | tf_op jit(solution)/shard_map/ppermute | solution.py:445
  114.1 16.0 %collective-permute-start.32 = (bf16[128,2048]{1,0:T(8,128)(2,1)}, bf16[128,2048]{1,0:T(8,128)(2,1)S(1)}, u32[]{:S(2)}, u32[]{:S(2)}) collective-permute-start(bf16[128,2048]{1,0:T(8,128)(2,1)} %collective-permute-done.25.refs_12_), channel_id=1, source_target_pairs={{0,1},{1,2},{2,3},{3,0},{4,5},{5,6},{6,7},{7,4},{8,9},{9,10},{10,1... | collective-permute-start | bytes 1572872 | tf_op jit(solution)/shard_map/ppermute | solution.py:405
  114.2 15.9 %collective-permute-start.29 = (bf16[136,2048]{1,0:T(8,128)(2,1)S(1)}, bf16[136,2048]{1,0:T(8,128)(2,1)S(1)}, u32[]{:S(2)}, u32[]{:S(2)}) collective-permute-start(bf16[136,2048]{1,0:T(8,128)(2,1)S(1)} %copy-done.21), channel_id=1, source_target_pairs={{0,4},{4,0},{8,12},{12,8},{1,5},{5,1},{9,13},{13,9},{2,6},{6,2},{1... | collective-permute-start | bytes 1671176 | tf_op jit(solution)/shard_map/ppermute | solution.py:445
  125.0 15.5 %collective-permute-start.31 = (bf16[136,2048]{1,0:T(8,128)(2,1)S(1)}, bf16[136,2048]{1,0:T(8,128)(2,1)S(1)}, u32[]{:S(2)}, u32[]{:S(2)}) collective-permute-start(bf16[136,2048]{1,0:T(8,128)(2,1)S(1)} %add_convert_fusion.2), channel_id=1, source_target_pairs={{0,8},{4,12},{8,0},{12,4},{1,9},{5,13},{9,1},{13,5},{2,10},{6,14},... | collective-permute-start | bytes 1671176 | tf_op jit(solution)/shard_map/ppermute | solution.py:405
  127.4 24.5 %collective-permute-start.3 = (bf16[136,2048]{1,0:T(8,128)(2,1)S(1)}, bf16[136,2048]{1,0:T(8,128)(2,1)S(1)}, u32[]{:S(2)}, u32[]{:S(2)}) collective-permute-start(bf16[136,2048]{1,0:T(8,128)(2,1)S(1)} %copy-done.19), channel_id=1, source_target_pairs={{0,4},{4,0},{8,12},{12,8},{1,5},{5,1},{9,13},{13,9},{2,6},{6,2},{1... | collective-permute-start | bytes 1671176 | tf_op jit(solution)/shard_map/ppermute | solution.py:445
  127.4 23.1 %collective-permute-start.36 = (bf16[128,2048]{1,0:T(8,128)(2,1)}, bf16[128,2048]{1,0:T(8,128)(2,1)S(1)}, u32[]{:S(2)}, u32[]{:S(2)}) collective-permute-start(bf16[128,2048]{1,0:T(8,128)(2,1)} %collective-permute-done.18.refs_4_), channel_id=1, source_target_pairs={{0,8},{4,12},{8,0},{12,4},{1,9},{5,13},{9,1},{13,5},{2,10},{6,14},... | collective-permute-start | bytes 1572872 | tf_op jit(solution)/shard_map/ppermute | solution.py:405
  130.1 20.4 %collective-permute-start.37 = (bf16[128,2048]{1,0:T(8,128)(2,1)}, bf16[128,2048]{1,0:T(8,128)(2,1)S(1)}, u32[]{:S(2)}, u32[]{:S(2)}) collective-permute-start(bf16[128,2048]{1,0:T(8,128)(2,1)} %collective-permute-done.18.refs_4_), channel_id=1, source_target_pairs={{0,4},{4,0},{8,12},{12,8},{1,5},{5,1},{9,13},{13,9},{2,6},{6,2},{1... | collective-permute-start | bytes 1572872 | tf_op jit(solution)/shard_map/ppermute | solution.py:445
  130.1 26.2 %collective-permute-start.19 = (bf16[136,2048]{1,0:T(8,128)(2,1)S(1)}, bf16[136,2048]{1,0:T(8,128)(2,1)S(1)}, u32[]{:S(2)}, u32[]{:S(2)}) collective-permute-start(bf16[136,2048]{1,0:T(8,128)(2,1)S(1)} %add_convert_fusion.5), channel_id=1, source_target_pairs={{0,3},{1,0},{2,1},{3,2},{4,7},{5,4},{6,5},{7,6},{8,11},{9,8},{10,9... | collective-permute-start | bytes 1671176 | tf_op jit(solution)/shard_map/ppermute | solution.py:405
  140.5 17.5 %collective-permute-start.26 = (bf16[136,2048]{1,0:T(8,128)(2,1)S(1)}, bf16[136,2048]{1,0:T(8,128)(2,1)S(1)}, u32[]{:S(2)}, u32[]{:S(2)}) collective-permute-start(bf16[136,2048]{1,0:T(8,128)(2,1)S(1)} %add_convert_fusion.3), channel_id=1, source_target_pairs={{0,1},{1,2},{2,3},{3,0},{4,5},{5,6},{6,7},{7,4},{8,9},{9,10},{10,1... | collective-permute-start | bytes 1671176 | tf_op jit(solution)/shard_map/ppermute | solution.py:405
  140.5 38.4 %copy-start.18 = (bf16[136,2048]{1,0:T(8,128)(2,1)S(1)}, bf16[136,2048]{1,0:T(8,128)(2,1)}, u32[]{:S(2)}) copy-start(bf16[136,2048]{1,0:T(8,128)(2,1)} %get-tuple-element.58) | copy-start | bytes 1671172
  150.5 30.1 %copy-start.25 = (bf16[128,2048]{1,0:T(8,128)(2,1)}, bf16[128,2048]{1,0:T(8,128)(2,1)S(1)}, u32[]{:S(2)}) copy-start(bf16[128,2048]{1,0:T(8,128)(2,1)S(1)} %collective-permute-done.36.refs_5_) | copy-start | bytes 1572868
  150.5 28.4 %collective-permute-start.33 = (bf16[136,2048]{1,0:T(8,128)(2,1)S(1)}, bf16[136,2048]{1,0:T(8,128)(2,1)S(1)}, u32[]{:S(2)}, u32[]{:S(2)}) collective-permute-start(bf16[136,2048]{1,0:T(8,128)(2,1)S(1)} %add_convert_fusion.1), channel_id=1, source_target_pairs={{0,2},{1,3},{2,0},{3,1},{4,6},{5,7},{6,4},{7,5},{8,10},{9,11},{10,... | collective-permute-start | bytes 1671176 | tf_op jit(solution)/shard_map/ppermute | solution.py:405
  150.5 14.9 %collective-permute-start.39 = (bf16[128,2048]{1,0:T(8,128)(2,1)S(1)}, bf16[128,2048]{1,0:T(8,128)(2,1)S(1)}, u32[]{:S(2)}, u32[]{:S(2)}) collective-permute-start(bf16[128,2048]{1,0:T(8,128)(2,1)S(1)} %collective-permute-done.32.refs_8_), channel_id=1, source_target_pairs={{0,8},{4,12},{8,0},{12,4},{1,9},{5,13},{9,1},{13,5},{2,10},{6,14},... | collective-permute-start | bytes 1572872 | tf_op jit(solution)/shard_map/ppermute | solution.py:405
  151.9 22.6 %collective-permute-start.42 = (bf16[128,2048]{1,0:T(8,128)(2,1)}, bf16[128,2048]{1,0:T(8,128)(2,1)S(1)}, u32[]{:S(2)}, u32[]{:S(2)}) collective-permute-start(bf16[128,2048]{1,0:T(8,128)(2,1)} %collective-permute-done.25.refs_12_), channel_id=1, source_target_pairs={{0,8},{4,12},{8,0},{12,4},{1,9},{5,13},{9,1},{13,5},{2,10},{6,14},... | collective-permute-start | bytes 1572872 | tf_op jit(solution)/shard_map/ppermute | solution.py:405
  156.3 25.7 %collective-permute-start.43 = (bf16[128,2048]{1,0:T(8,128)(2,1)}, bf16[128,2048]{1,0:T(8,128)(2,1)S(1)}, u32[]{:S(2)}, u32[]{:S(2)}) collective-permute-start(bf16[128,2048]{1,0:T(8,128)(2,1)} %collective-permute-done.25.refs_12_), channel_id=1, source_target_pairs={{0,4},{4,0},{8,12},{12,8},{1,5},{5,1},{9,13},{13,9},{2,6},{6,2},{1... | collective-permute-start | bytes 1572872 | tf_op jit(solution)/shard_map/ppermute | solution.py:445
  158.0 24.0 %collective-permute-start.40 = (bf16[128,2048]{1,0:T(8,128)(2,1)S(1)}, bf16[128,2048]{1,0:T(8,128)(2,1)S(1)}, u32[]{:S(2)}, u32[]{:S(2)}) collective-permute-start(bf16[128,2048]{1,0:T(8,128)(2,1)S(1)} %collective-permute-done.32.refs_8_), channel_id=1, source_target_pairs={{0,4},{4,0},{8,12},{12,8},{1,5},{5,1},{9,13},{13,9},{2,6},{6,2},{1... | collective-permute-start | bytes 1572872 | tf_op jit(solution)/shard_map/ppermute | solution.py:445
  165.4 16.6 %collective-permute-start.38 = (bf16[128,2048]{1,0:T(8,128)(2,1)S(1)}, bf16[128,2048]{1,0:T(8,128)(2,1)S(1)}, u32[]{:S(2)}, u32[]{:S(2)}) collective-permute-start(bf16[128,2048]{1,0:T(8,128)(2,1)S(1)} %collective-permute-done.36.refs_5_), channel_id=1, source_target_pairs={{0,4},{4,0},{8,12},{12,8},{1,5},{5,1},{9,13},{13,9},{2,6},{6,2},{1... | collective-permute-start | bytes 1572872 | tf_op jit(solution)/shard_map/ppermute | solution.py:445
  174.4 7.6 %collective-permute-start.41 = (bf16[128,2048]{1,0:T(8,128)(2,1)S(1)}, bf16[128,2048]{1,0:T(8,128)(2,1)S(1)}, u32[]{:S(2)}, u32[]{:S(2)}) collective-permute-start(bf16[128,2048]{1,0:T(8,128)(2,1)S(1)} %collective-permute-done.39.refs_9_), channel_id=1, source_target_pairs={{0,4},{4,0},{8,12},{12,8},{1,5},{5,1},{9,13},{13,9},{2,6},{6,2},{1... | collective-permute-start | bytes 1572872 | tf_op jit(solution)/shard_map/ppermute | solution.py:445
  178.9 3.1 %collective-permute-start.44 = (bf16[128,2048]{1,0:T(8,128)(2,1)S(1)}, bf16[128,2048]{1,0:T(8,128)(2,1)S(1)}, u32[]{:S(2)}, u32[]{:S(2)}) collective-permute-start(bf16[128,2048]{1,0:T(8,128)(2,1)S(1)} %collective-permute-done.42.refs_13_), channel_id=1, source_target_pairs={{0,4},{4,0},{8,12},{12,8},{1,5},{5,1},{9,13},{13,9},{2,6},{6,2},{1... | collective-permute-start | bytes 1572872 | tf_op jit(solution)/shard_map/ppermute | solution.py:445
  (31 other events, 274.3 us)

commit v3 on v2

--- a/solution.py
+++ b/solution.py
@@ -320,12 +320,57 @@
     return out[:4], out[4], out[5], out[6], out[7]
 
 
-def weight_kernel(rounds, slot_cap, *refs):
+def columns(height):
+    return pl.BlockSpec((height, TILE), lambda i: (0, i))
+
+
+def whole(array):
+    return pl.BlockSpec(array.shape, lambda i: (0,) * array.ndim)
+
+
+def down_kernel(rounds, *refs):
+    scaled, rows = refs[:rounds], refs[rounds:2 * rounds]
+    out, all_scaled, all_dy = refs[2 * rounds:]
+    taken = rows[0].shape[0]
+
+    @pl.when(pl.program_id(0) == 0)
+    def _():
+        for r in range(rounds):
+            all_scaled[r * taken:(r + 1) * taken, :] = scaled[r][...]
+
+    for r in range(rounds):
+        all_dy[r * taken:(r + 1) * taken, :] = rows[r][...]
+    out[...] = dot_tn(all_scaled[...], all_dy[...]).astype(jnp.bfloat16)
+
+
+def down_grad(scaled, rows):
+    rounds = len(rows)
+    taken, hid = scaled[0].shape
+    width = rows[0].shape[1]
+    total = rounds * taken
+    return pl.pallas_call(
+        functools.partial(down_kernel, rounds),
+        grid=(width // TILE,),
+        out_shape=jax.ShapeDtypeStruct((hid, width), jnp.bfloat16),
+        in_specs=[whole(part) for part in scaled] + [columns(taken)] * rounds,
+        out_specs=columns(hid),
+        scratch_shapes=[pltpu.VMEM((total, hid), jnp.bfloat16), pltpu.VMEM((total, TILE), jnp.bfloat16)],
+        compiler_params=pltpu.CompilerParams(vmem_limit_bytes=VMEM),
+        cost_estimate=pl.CostEstimate(
+            flops=2 * total * width * hid, bytes_accessed=2 * (total * (width + hid) + width * hid), transcendentals=0
+        ),
+    )(*scaled, *rows)
+
+
+def input_kernel(rounds, slot_cap, halved, *refs):
     count = 4 * rounds
-    pieces, rows = refs[:count], refs[count:count + rounds]
-    dgu, scaled = refs[count + rounds:count + 2 * rounds], refs[count + 2 * rounds:count + 3 * rounds]
-    slots = refs[count + 3 * rounds:count + 4 * rounds]
-    gate_out, up_out, down_out, all_x, all_dy, all_dgu, all_scaled = refs[count + 4 * rounds:]
+    pieces, refs = [], list(refs)
+    left = pl.program_id(0) < pl.num_programs(0) // 2
+    for split in halved:
+        piece = refs.pop(0)[...]
+        pieces.append(jnp.where(left, piece, refs.pop(0)[...]) if split else piece)
+    dgu, slots = refs[:rounds], refs[rounds:2 * rounds]
+    gate_out, up_out, all_x, all_dgu = refs[2 * rounds:]
     taken = 4 * slot_cap
     hid = gate_out.shape[1]
 
@@ -333,62 +378,47 @@
     def _():
         for r in range(rounds):
             all_dgu[r * taken:(r + 1) * taken, :] = dgu[r][...]
-            all_scaled[r * taken:(r + 1) * taken, :] = scaled[r][...]
 
     for i in range(count):
         select = as_bf16(slot_hits(slots[i // 4][i % 4], slot_cap))
-        picked = jnp.dot(select, pieces[i][...], preferred_element_type=jnp.float32)
+        picked = jnp.dot(select, pieces[i], preferred_element_type=jnp.float32)
         all_x[i * slot_cap:(i + 1) * slot_cap, :] = picked.astype(jnp.bfloat16)
-    for r in range(rounds):
-        all_dy[r * taken:(r + 1) * taken, :] = rows[r][...]
     grads = dot_tn(all_x[...], all_dgu[...])
     gate_out[...] = grads[:, :hid].astype(jnp.bfloat16)
     up_out[...] = grads[:, hid:].astype(jnp.bfloat16)
-    down_out[...] = dot_tn(all_scaled[...], all_dy[...]).astype(jnp.bfloat16)
-
-
-def weight_grads(pieces, rows, dgu, scaled, slots):
-    rounds, count = len(rows), len(pieces)
-    size, width = pieces[0].shape
-    taken, hid = scaled[0].shape
+
+
+def input_grads(width, pieces, dgu, slots):
+    rounds, count = len(dgu), len(pieces)
+    taken, both = dgu[0].shape
+    hid = both // 2
     half = jnp.bfloat16
-
-    def columns(height):
-        return pl.BlockSpec((height, TILE), lambda i: (0, i))
-
-    def whole(shape):
-        return pl.BlockSpec(shape, lambda i: (0,) * len(shape))
-
+    steps = width // TILE
+    halved = tuple(isinstance(piece, tuple) for piece in pieces)
+    flat, specs = [], []
+    for piece, split in zip(pieces, halved, strict=True):
+        flat += piece if split else (piece,)
+        size = flat[-1].shape[0]
+        if split:
+            last = flat[-1].shape[1] // TILE - steps
+            specs.append(pl.BlockSpec((size, TILE), lambda i: (0, jnp.minimum(i, steps // 2 - 1))))
+            specs.append(pl.BlockSpec((size, TILE), lambda i, last=last: (0, jnp.maximum(i, steps // 2) + last)))
+        else:
+            specs.append(columns(size))
     slot_cap, total = taken // 4, rounds * taken
-    flops = 2 * total * width * (3 * hid + size)
-    moved = 2 * (count * size * width + total * (width + 3 * hid) + 3 * width * hid)
+    flops = 2 * total * width * (2 * hid + size)
+    moved = 2 * (count * size * width + total * 2 * hid + 2 * width * hid)
+    strip = pl.BlockSpec((TILE, hid), lambda i: (i, 0))
     return pl.pallas_call(
-        functools.partial(weight_kernel, rounds, slot_cap),
-        grid=(width // TILE,),
-        out_shape=[
-            jax.ShapeDtypeStruct((width, hid), half),
-            jax.ShapeDtypeStruct((width, hid), half),
-            jax.ShapeDtypeStruct((hid, width), half),
-        ],
-        in_specs=[columns(size)] * count
-        + [columns(taken)] * rounds
-        + [whole((taken, 2 * hid))] * rounds
-        + [whole((taken, hid))] * rounds
-        + [whole(slots[0].shape)] * rounds,
-        out_specs=[
-            pl.BlockSpec((TILE, hid), lambda i: (i, 0)),
-            pl.BlockSpec((TILE, hid), lambda i: (i, 0)),
-            columns(hid),
-        ],
-        scratch_shapes=[
-            pltpu.VMEM((total, TILE), half),
-            pltpu.VMEM((total, TILE), half),
-            pltpu.VMEM((total, 2 * hid), half),
-            pltpu.VMEM((total, hid), half),
-        ],
-        compiler_params=pltpu.CompilerParams(vmem_limit_bytes=56 << 20),
+        functools.partial(input_kernel, rounds, slot_cap, halved),
+        grid=(steps,),
+        out_shape=[jax.ShapeDtypeStruct((width, hid), half)] * 2,
+        in_specs=specs + [whole(part) for part in dgu] + [whole(part) for part in slots],
+        out_specs=[strip] * 2,
+        scratch_shapes=[pltpu.VMEM((total, TILE), half), pltpu.VMEM((total, both), half)],
+        compiler_params=pltpu.CompilerParams(vmem_limit_bytes=VMEM),
         cost_estimate=pl.CostEstimate(flops=flops, bytes_accessed=moved, transcendentals=0),
-    )(*pieces, *rows, *dgu, *scaled, *slots)
+    )(*flat, *dgu, *slots)
 
 
 def after(value, *others):
@@ -490,14 +520,18 @@
 
     back = [term for s in shifts for term in sums[s]]
     total = add(*back)
-    pieces = []
-    for s in shifts:
-        pieces += [x[s], x_side[s], other_core(x[s]), other_core(x_side[s])]
-    grads = weight_grads(
-        pieces, *[[part[s] for s in shifts] for part in (rows, dgu, scaled, slots)]
+    pieces = {0: [tokens, x_side[0], other_core(tokens), other_core(x_side[0])]}
+    for s in range(1, ring):
+        held, side_held = other_core(x[s]), other_core(x_side[s])
+        pieces[s] = [x[s], x_side[s], held, side_held]
+    first = after(rows[shifts[0]], *[slots[s] for s in shifts])
+    grad_down = down_grad([scaled[s] for s in shifts], [first] + [rows[s] for s in shifts[1:]])
+    grad_gate, grad_up = input_grads(
+        width,
+        [piece for s in shifts for piece in pieces[s]], *[[part[s] for s in shifts] for part in (dgu, slots)]
     )
     grad_probs = total[count:count + chosen, :count].T
-    return (total[:count], grad_probs, *[grad[None] for grad in grads])
+    return (total[:count], grad_probs, grad_gate[None], grad_up[None], grad_down[None])
 
 
 def local(tokens, grad_out, probs, routes, w_gate, w_up, w_down, gate_pre, up_pre):

time: 197 us -> 195 us (0.990)
  waiting for transfers between devices: 107 us -> 100 us
  Pallas kernels: 52.1 us -> 56 us
    ppermute x21, waiting for transfers between devices: 107 us -> 100 us  [send(): got = lax.ppermute(value, axis, pairs)]
    pallas_call x1 -> x2, Pallas kernels: 12.7 us -> 16.6 us  [the longest x1 10.3 us: input_grads(): pl.pallas_call(functools.partial(input_kernel, rounds, slot_cap, halved),...]
  transfers between devices with their start and end apart: 45 -> 45, of which waited for: 16 -> 14; matrix products, arithmetic and copies ran while one was open for 5% -> 5% of each run, Pallas kernels for 20% -> 24%
where the time goes in v3:
time: 195 us; the launch traced here: 194 us
  waiting for transfers between devices  100 us (51%)
  Pallas kernels  56 us (29%)
  starting transfers between devices  20 us (10%)
  other arithmetic  8.93 us (5%)
  local copies, waits for them, and re-layouts  7.72 us (4%)
    ppermute x21, waiting for transfers between devices, send(): got = lax.ppermute(value, axis, pairs)  100 us
    pallas_call x4, Pallas kernels, round_backward(): pl.pallas_call(round_kernel, out_shape=[jax.ShapeDtypeStruct((height, wid...  32.7 us
    ppermute x21, starting transfers between devices, send(): got = lax.ppermute(value, axis, pairs)  16.9 us
    pallas_call x1, Pallas kernels, input_grads(): pl.pallas_call(functools.partial(input_kernel, rounds, slot_cap, halved),...  10.3 us
    pallas_call x1, Pallas kernels, slopes(): pl.pallas_call(slope_kernel, grid=(blocks // 2,), out_shape=jax.ShapeDtyp...  6.73 us
    convert_element_type x8, other arithmetic, add(): return total.astype(jnp.bfloat16)  6.48 us
    pallas_call x1, Pallas kernels, down_grad(): pl.pallas_call(functools.partial(down_kernel, rounds), grid=(width // TIL...  6.27 us
  transfers between devices with their start and end apart: 45, of which 14 were waited for; matrix products, arithmetic and copies ran while one was open for 5% of the time, Pallas kernels for 24%

profile of v3, /device:TPU:0, one launch (start us, length us, event | category | flops | bytes accessed | tf_op | source)
XLA Modules:
  0.0 194.1 jit_solution(14790329922560847196)
XLA Ops:
  0.6 0.7 fusion.3
  1.3 0.7 fusion.2
  2.0 1.1 pad_maximum_fusion.dy0
  3.1 3.0 %collective-permute-start = (bf16[136,2048]{1,0:T(8,128)(2,1)S(1)}, bf16[136,2048]{1,0:T(8,128)(2,1)S(1)}, u32[]{:S(2)}, u32[]{:S(2)}) collective-permute-start(bf16[136,2048]{1,0:T(8,128)(2,1)S(1)} %pad_maximum_fusion.dy0), channel_id=1, source_target_pairs={{0,8},{4,12},{8,0},{12,4},{1,9},{5,13},{9,1},{13,5},{2,10},{6,14},... | collective-permute-start | bytes 1671176 | tf_op jit(solution)/shard_map/ppermute | solution.py:435
  6.1 1.6 collective-permute-start.9
  7.7 11.0 %collective-permute-done.dy1 = bf16[136,2048]{1,0:T(8,128)(2,1)S(1)} collective-permute-done((bf16[136,2048]{1,0:T(8,128)(2,1)S(1)}, bf16[136,2048]{1,0:T(8,128)(2,1)S(1)}, u32[]{:S(2)}, u32[]{:S(2)}) %collective-permute-start) | collective-permute-done | bytes 557088 | tf_op jit(solution)/shard_map/ppermute | solution.py:435
  18.7 3.3 %collective-permute-done.9.dy0 = bf16[136,2048]{1,0:T(8,128)(2,1)S(1)} collective-permute-done((bf16[136,2048]{1,0:T(8,128)(2,1)S(1)}, bf16[136,2048]{1,0:T(8,128)(2,1)S(1)}, u32[]{:S(2)}, u32[]{:S(2)}) %collective-permute-start.9) | collective-permute-done | bytes 557088 | tf_op jit(solution)/shard_map/ppermute | solution.py:435
  22.6 1.7 collective-permute-start.5
  24.3 1.5 collective-permute-start.6
  25.9 0.8 stack.71.ids_ref
  26.6 6.7 %shard_map.128.slope_hbm = f32[16,80,1152]{2,1,0:T(8,128)} custom-call(bf16[16,80,384]{2,1,0:T(8,128)(2,1)} %bitcast.43, bf16[16,80,384]{2,1,0:T(8,128)(2,1)} %bitcast.44), custom_call_target="tpu_custom_call" | custom-call | flops 4915200 | bytes 7864320 | tf_op jit(solution)/shard_map/pallas_call | solution.py:153
  33.5 4.0 %collective-permute-done.10.dy1 = bf16[136,2048]{1,0:T(8,128)(2,1)S(1)} collective-permute-done((bf16[136,2048]{1,0:T(8,128)(2,1)S(1)}, bf16[136,2048]{1,0:T(8,128)(2,1)S(1)}, u32[]{:S(2)}, u32[]{:S(2)}) %collective-permute-start.10) | collective-permute-done | bytes 557088 | tf_op jit(solution)/shard_map/ppermute | solution.py:435
  37.5 8.2 %shard_map.129 = (bf16[136,2048]{1,0:T(8,128)(2,1)}, bf16[136,2048]{1,0:T(8,128)(2,1)}, bf16[136,2048]{1,0:T(8,128)(2,1)}, bf16[136,2048]{1,0:T(8,128)(2,1)}, bf...) custom-call(s32[5]{0:T(128)} %stack.71.ids_ref, ...), custom_call_target="tpu_custom_call" | custom-call | flops 1845493760 | bytes 11714560 | tf_op jit(solution)/shard_map/pallas_call | solution.py:292
  45.8 2.7 %collective-permute-done.6.refs_1_ = bf16[128,2048]{1,0:T(8,128)(2,1)} collective-permute-done((bf16[128,2048]{1,0:T(8,128)(2,1)}, bf16[128,2048]{1,0:T(8,128)(2,1)}, u32[]{:S(2)}, u32[]{:S(2)}) %collective-permute-start.6) | collective-permute-done | bytes 524320 | tf_op jit(solution)/shard_map/ppermute | solution.py:435
  49.0 0.7 stack.76.ids_ref
  50.2 8.1 %shard_map.130 = (bf16[136,2048]{1,0:T(8,128)(2,1)}, bf16[136,2048]{1,0:T(8,128)(2,1)}, bf16[136,2048]{1,0:T(8,128)(2,1)}, bf16[136,2048]{1,0:T(8,128)(2,1)}, bf...) custom-call(s32[5]{0:T(128)} %stack.76.ids_ref, ...), custom_call_target="tpu_custom_call" | custom-call | flops 1845493760 | bytes 11714560 | tf_op jit(solution)/shard_map/pallas_call | solution.py:292
  58.3 14.0 %collective-permute-done.15.dy0 = bf16[136,2048]{1,0:T(8,128)(2,1)S(1)} collective-permute-done((bf16[136,2048]{1,0:T(8,128)(2,1)S(1)}, bf16[136,2048]{1,0:T(8,128)(2,1)S(1)}, u32[]{:S(2)}, u32[]{:S(2)}) %collective-permute-start.15) | collective-permute-done | bytes 557088 | tf_op jit(solution)/shard_map/ppermute | solution.py:435
  72.3 0.8 collective-permute-start.16
  73.2 0.7 stack.86.ids_ref
  73.9 0.6 stack.81.ids_ref
  75.0 2.1 %add_convert_fusion.7 = bf16[136,2048]{1,0:T(8,128)(2,1)} fusion(bf16[136,2048]{1,0:T(8,128)(2,1)} %collective-permute-done.4, bf16[136,2048]{1,0:T(8,128)(2,1)} %get-tuple-element.60), kind=kLoop, calls=%fused_computation.7 | loop fusion | flops 1114112 | bytes 1671168 | tf_op jit(solution)/shard_map/convert_element_type | solution.py:444
  77.2 9.5 %collective-permute-done.16.dy1 = bf16[136,2048]{1,0:T(8,128)(2,1)S(1)} collective-permute-done((bf16[136,2048]{1,0:T(8,128)(2,1)S(1)}, bf16[136,2048]{1,0:T(8,128)(2,1)S(1)}, u32[]{:S(2)}, u32[]{:S(2)}) %collective-permute-start.16) | collective-permute-done | bytes 557088 | tf_op jit(solution)/shard_map/ppermute | solution.py:435
  86.7 0.7 collective-permute-start.8
  87.5 0.8 copy-done.8
  88.2 8.2 %shard_map.131 = (bf16[136,2048]{1,0:T(8,128)(2,1)}, bf16[136,2048]{1,0:T(8,128)(2,1)}, bf16[136,2048]{1,0:T(8,128)(2,1)}, bf16[136,2048]{1,0:T(8,128)(2,1)}, bf...) custom-call(s32[5]{0:T(128)} %stack.81.ids_ref, ...), custom_call_target="tpu_custom_call" | custom-call | flops 1845493760 | bytes 11714560 | tf_op jit(solution)/shard_map/pallas_call | solution.py:292
  96.5 1.4 add_convert_fusion.6
  97.9 1.4 collective-permute-start.17
  99.3 0.8 copy-done.12
  100.1 8.1 %shard_map.132 = (bf16[136,2048]{1,0:T(8,128)(2,1)}, bf16[136,2048]{1,0:T(8,128)(2,1)}, bf16[136,2048]{1,0:T(8,128)(2,1)}, bf16[136,2048]{1,0:T(8,128)(2,1)}, bf...) custom-call(s32[5]{0:T(128)} %stack.86.ids_ref, ...), custom_call_target="tpu_custom_call" | custom-call | flops 1845493760 | bytes 11714560 | tf_op jit(solution)/shard_map/pallas_call | solution.py:292
  109.0 0.9 collective-permute-start.24
  110.0 3.4 %collective-permute-done.17 = bf16[136,2048]{1,0:T(8,128)(2,1)S(1)} collective-permute-done((bf16[136,2048]{1,0:T(8,128)(2,1)S(1)}, bf16[136,2048]{1,0:T(8,128)(2,1)S(1)}, u32[]{:S(2)}, u32[]{:S(2)}) %collective-permute-start.17) | collective-permute-done | bytes 557088 | tf_op jit(solution)/shard_map/ppermute | solution.py:435
  114.3 10.6 %collective-permute-done.24 = bf16[136,2048]{1,0:T(8,128)(2,1)S(1)} collective-permute-done((bf16[136,2048]{1,0:T(8,128)(2,1)S(1)}, bf16[136,2048]{1,0:T(8,128)(2,1)S(1)}, u32[]{:S(2)}, u32[]{:S(2)}) %collective-permute-start.24) | collective-permute-done | bytes 557088 | tf_op jit(solution)/shard_map/ppermute | solution.py:435
  125.0 1.3 collective-permute-start.31
  126.5 0.8 copy-done.19
  127.3 0.7 collective-permute-start.36
  128.3 1.8 collective-permute-done.32.refs_8_
  130.2 10.3 %collective-permute-done.31 = bf16[136,2048]{1,0:T(8,128)(2,1)S(1)} collective-permute-done((bf16[136,2048]{1,0:T(8,128)(2,1)S(1)}, bf16[136,2048]{1,0:T(8,128)(2,1)S(1)}, u32[]{:S(2)}, u32[]{:S(2)}) %collective-permute-start.31) | collective-permute-done | bytes 557088 | tf_op jit(solution)/shard_map/ppermute | solution.py:435
  140.7 9.9 %collective-permute-done.36.refs_5_ = bf16[128,2048]{1,0:T(8,128)(2,1)} collective-permute-done((bf16[128,2048]{1,0:T(8,128)(2,1)}, bf16[128,2048]{1,0:T(8,128)(2,1)}, u32[]{:S(2)}, u32[]{:S(2)}) %collective-permute-start.36) | collective-permute-done | bytes 524320 | tf_op jit(solution)/shard_map/ppermute | solution.py:435
  150.7 1.4 collective-permute-start.39
  152.0 0.7 collective-permute-start.42
  152.8 6.3 %shard_map.134 = bf16[384,2048]{1,0:T(8,128)(2,1)} custom-call(bf16[320,384]{1,0:T(8,128)(2,1)} %get-tuple-element.102.refs_0_, bf16[320,384]{1,0:T(8,128)(2,1)} %get-tuple-element.103.refs_1_, bf16[320,384]{1,0:T(8,128)(2,1)} %get-tuple-element.104.refs_2_, bf16[320,384]{1,0:T(8,128)(2,1)} %get-tuple-element.105.refs_3_, ...), custom_call_target="tpu_custom_call" | custom-call | flops 2013265920 | bytes 7798784 | tf_op jit(solution)/shard_map/pallas_call | solution.py:351
  159.6 6.3 %collective-permute-done.39.refs_9_ = bf16[128,2048]{1,0:T(8,128)(2,1)} collective-permute-done((bf16[128,2048]{1,0:T(8,128)(2,1)}, bf16[128,2048]{1,0:T(8,128)(2,1)}, u32[]{:S(2)}, u32[]{:S(2)}) %collective-permute-start.39) | collective-permute-done | bytes 524320 | tf_op jit(solution)/shard_map/ppermute | solution.py:435
  165.9 9.1 %collective-permute-done.42.refs_13_ = bf16[128,2048]{1,0:T(8,128)(2,1)} collective-permute-done((bf16[128,2048]{1,0:T(8,128)(2,1)}, bf16[128,2048]{1,0:T(8,128)(2,1)}, u32[]{:S(2)}, u32[]{:S(2)}) %collective-permute-start.42) | collective-permute-done | bytes 524320 | tf_op jit(solution)/shard_map/ppermute | solution.py:435
  175.1 4.0 %collective-permute-done.33 = bf16[136,2048]{1,0:T(8,128)(2,1)} collective-permute-done((bf16[136,2048]{1,0:T(8,128)(2,1)S(1)}, bf16[136,2048]{1,0:T(8,128)(2,1)}, u32[]{:S(2)}, u32[]{:S(2)}) %collective-permute-start.33) | collective-permute-done | bytes 557088 | tf_op jit(solution)/shard_map/ppermute | solution.py:435
  179.1 1.9 add_convert_fusion
  181.1 0.8 slice.8
  182.5 0.7 copy-done.25
  183.7 10.3 %shard_map.133 = (bf16[2048,384]{1,0:T(8,128)(2,1)}, bf16[2048,384]{1,0:T(8,128)(2,1)}) custom-call(bf16[128,2048]{1,0:T(8,128)(2,1)} %refs_0_.1, bf16[128,2048]{1,0:T(8,128)(2,1)} %collective-permute-done.6.refs_1_, bf16[128,2048]{1,0:T(8,128)(2,1)} %copy-done.22, bf16[128,2048]{1,0:T(8,128)(2,1)} %copy-done.23, ...), custom_call_target="tpu_custom_call" | custom-call | flops 4697620480 | bytes 13500416 | tf_op jit(solution)/shard_map/pallas_call | solution.py:412
  (122 shorter events, 6.5 us)
Async XLA Ops:
  3.1 30.3 %copy-start = (bf16[136,2048]{1,0:T(8,128)(2,1)}, bf16[136,2048]{1,0:T(8,128)(2,1)S(1)}, u32[]{:S(2)}) copy-start(bf16[136,2048]{1,0:T(8,128)(2,1)S(1)} %pad_maximum_fusion.dy0) | copy-start | bytes 1671172
  3.1 15.6 %collective-permute-start = (bf16[136,2048]{1,0:T(8,128)(2,1)S(1)}, bf16[136,2048]{1,0:T(8,128)(2,1)S(1)}, u32[]{:S(2)}, u32[]{:S(2)}) collective-permute-start(bf16[136,2048]{1,0:T(8,128)(2,1)S(1)} %pad_maximum_fusion.dy0), channel_id=1, source_target_pairs={{0,8},{4,12},{8,0},{12,4},{1,9},{5,13},{9,1},{13,5},{2,10},{6,14},... | collective-permute-start | bytes 1671176 | tf_op jit(solution)/shard_map/ppermute | solution.py:435
  6.1 15.9 %collective-permute-start.9 = (bf16[136,2048]{1,0:T(8,128)(2,1)S(1)}, bf16[136,2048]{1,0:T(8,128)(2,1)S(1)}, u32[]{:S(2)}, u32[]{:S(2)}) collective-permute-start(bf16[136,2048]{1,0:T(8,128)(2,1)S(1)} %pad_maximum_fusion.dy0), channel_id=1, source_target_pairs={{0,1},{1,2},{2,3},{3,0},{4,5},{5,6},{6,7},{7,4},{8,9},{9,10},{10,1... | collective-permute-start | bytes 1671176 | tf_op jit(solution)/shard_map/ppermute | solution.py:435
  7.7 18.1 %collective-permute-start.1 = (bf16[136,2048]{1,0:T(8,128)(2,1)S(1)}, bf16[136,2048]{1,0:T(8,128)(2,1)S(1)}, u32[]{:S(2)}, u32[]{:S(2)}) collective-permute-start(bf16[136,2048]{1,0:T(8,128)(2,1)S(1)} %pad_maximum_fusion.dy0), channel_id=1, source_target_pairs={{0,4},{4,0},{8,12},{12,8},{1,5},{5,1},{9,13},{13,9},{2,6},{6,2},{1... | collective-permute-start | bytes 1671176 | tf_op jit(solution)/shard_map/ppermute | solution.py:475
  22.1 11.3 %collective-permute-start.2 = (bf16[136,2048]{1,0:T(8,128)(2,1)S(1)}, bf16[136,2048]{1,0:T(8,128)(2,1)}, u32[]{:S(2)}, u32[]{:S(2)}) collective-permute-start(bf16[136,2048]{1,0:T(8,128)(2,1)S(1)} %collective-permute-done.dy1), channel_id=1, source_target_pairs={{0,4},{4,0},{8,12},{12,8},{1,5},{5,1},{9,13},{13,9},{2,6},{6,2},{1... | collective-permute-start | bytes 1671176 | tf_op jit(solution)/shard_map/ppermute | solution.py:475
  22.1 15.4 %collective-permute-start.10 = (bf16[136,2048]{1,0:T(8,128)(2,1)S(1)}, bf16[136,2048]{1,0:T(8,128)(2,1)S(1)}, u32[]{:S(2)}, u32[]{:S(2)}) collective-permute-start(bf16[136,2048]{1,0:T(8,128)(2,1)S(1)} %collective-permute-done.9.dy0), channel_id=1, source_target_pairs={{0,8},{4,12},{8,0},{12,4},{1,9},{5,13},{9,1},{13,5},{2,10},{6,14},... | collective-permute-start | bytes 1671176 | tf_op jit(solution)/shard_map/ppermute | solution.py:435
  22.6 23.1 %collective-permute-start.5 = (bf16[136,2048]{1,0:T(8,128)(2,1)S(1)}, bf16[136,2048]{1,0:T(8,128)(2,1)S(1)}, u32[]{:S(2)}, u32[]{:S(2)}) collective-permute-start(bf16[136,2048]{1,0:T(8,128)(2,1)S(1)} %pad_maximum_fusion.dy0), channel_id=1, source_target_pairs={{0,3},{1,0},{2,1},{3,2},{4,7},{5,4},{6,5},{7,6},{8,11},{9,8},{10,9... | collective-permute-start | bytes 1671176 | tf_op jit(solution)/shard_map/ppermute | solution.py:435
  24.3 24.1 %collective-permute-start.6 = (bf16[128,2048]{1,0:T(8,128)(2,1)}, bf16[128,2048]{1,0:T(8,128)(2,1)}, u32[]{:S(2)}, u32[]{:S(2)}) collective-permute-start(bf16[128,2048]{1,0:T(8,128)(2,1)} %refs_0_.1), channel_id=1, source_target_pairs={{0,8},{4,12},{8,0},{12,4},{1,9},{5,13},{9,1},{13,5},{2,10},{6,14},... | collective-permute-start | bytes 1572872 | tf_op jit(solution)/shard_map/ppermute | solution.py:435
  25.8 23.1 %collective-permute-start.11 = (bf16[136,2048]{1,0:T(8,128)(2,1)S(1)}, bf16[136,2048]{1,0:T(8,128)(2,1)}, u32[]{:S(2)}, u32[]{:S(2)}) collective-permute-start(bf16[136,2048]{1,0:T(8,128)(2,1)S(1)} %collective-permute-done.9.dy0), channel_id=1, source_target_pairs={{0,4},{4,0},{8,12},{12,8},{1,5},{5,1},{9,13},{13,9},{2,6},{6,2},{1... | collective-permute-start | bytes 1671176 | tf_op jit(solution)/shard_map/ppermute | solution.py:475
  33.4 39.0 %collective-permute-start.15 = (bf16[136,2048]{1,0:T(8,128)(2,1)S(1)}, bf16[136,2048]{1,0:T(8,128)(2,1)S(1)}, u32[]{:S(2)}, u32[]{:S(2)}) collective-permute-start(bf16[136,2048]{1,0:T(8,128)(2,1)S(1)} %pad_maximum_fusion.dy0), channel_id=1, source_target_pairs={{0,2},{1,3},{2,0},{3,1},{4,6},{5,7},{6,4},{7,5},{8,10},{9,11},{10,... | collective-permute-start | bytes 1671176 | tf_op jit(solution)/shard_map/ppermute | solution.py:435
  37.5 12.2 %collective-permute-start.12 = (bf16[136,2048]{1,0:T(8,128)(2,1)S(1)}, bf16[136,2048]{1,0:T(8,128)(2,1)}, u32[]{:S(2)}, u32[]{:S(2)}) collective-permute-start(bf16[136,2048]{1,0:T(8,128)(2,1)S(1)} %collective-permute-done.10.dy1), channel_id=1, source_target_pairs={{0,4},{4,0},{8,12},{12,8},{1,5},{5,1},{9,13},{13,9},{2,6},{6,2},{1... | collective-permute-start | bytes 1671176 | tf_op jit(solution)/shard_map/ppermute | solution.py:475
  48.4 24.7 %collective-permute-start.7 = (bf16[136,2048]{1,0:T(8,128)(2,1)S(1)}, bf16[136,2048]{1,0:T(8,128)(2,1)S(1)}, u32[]{:S(2)}, u32[]{:S(2)}) collective-permute-start(bf16[136,2048]{1,0:T(8,128)(2,1)S(1)} %collective-permute-done.5.dy0), channel_id=1, source_target_pairs={{0,8},{4,12},{8,0},{12,4},{1,9},{5,13},{9,1},{13,5},{2,10},{6,14},... | collective-permute-start | bytes 1671176 | tf_op jit(solution)/shard_map/ppermute | solution.py:435
  49.0 25.9 %collective-permute-start.4 = (bf16[136,2048]{1,0:T(8,128)(2,1)}, bf16[136,2048]{1,0:T(8,128)(2,1)}, u32[]{:S(2)}, u32[]{:S(2)}) collective-permute-start(bf16[136,2048]{1,0:T(8,128)(2,1)} %get-tuple-element.61), channel_id=1, source_target_pairs={{0,4},{4,0},{8,12},{12,8},{1,5},{5,1},{9,13},{13,9},{2,6},{6,2},{1... | collective-permute-start | bytes 1671176 | tf_op jit(solution)/shard_map/ppermute | solution.py:475
  49.0 25.5 %collective-permute-start.18 = (bf16[128,2048]{1,0:T(8,128)(2,1)}, bf16[128,2048]{1,0:T(8,128)(2,1)}, u32[]{:S(2)}, u32[]{:S(2)}) collective-permute-start(bf16[128,2048]{1,0:T(8,128)(2,1)} %refs_0_.1), channel_id=1, source_target_pairs={{0,1},{1,2},{2,3},{3,0},{4,5},{5,6},{6,7},{7,4},{8,9},{9,10},{10,1... | collective-permute-start | bytes 1572872 | tf_op jit(solution)/shard_map/ppermute | solution.py:435
  49.7 27.5 %collective-permute-start.20 = (bf16[136,2048]{1,0:T(8,128)(2,1)S(1)}, bf16[136,2048]{1,0:T(8,128)(2,1)S(1)}, u32[]{:S(2)}, u32[]{:S(2)}) collective-permute-start(bf16[136,2048]{1,0:T(8,128)(2,1)S(1)} %collective-permute-done.5.dy0), channel_id=1, source_target_pairs={{0,4},{4,0},{8,12},{12,8},{1,5},{5,1},{9,13},{13,9},{2,6},{6,2},{1... | collective-permute-start | bytes 1671176 | tf_op jit(solution)/shard_map/ppermute | solution.py:475
  72.3 24.1 %copy-start.2 = (bf16[136,2048]{1,0:T(8,128)(2,1)}, bf16[136,2048]{1,0:T(8,128)(2,1)S(1)}, u32[]{:S(2)}) copy-start(bf16[136,2048]{1,0:T(8,128)(2,1)S(1)} %collective-permute-done.15.dy0) | copy-start | bytes 1671172
  72.3 14.3 %collective-permute-start.16 = (bf16[136,2048]{1,0:T(8,128)(2,1)S(1)}, bf16[136,2048]{1,0:T(8,128)(2,1)S(1)}, u32[]{:S(2)}, u32[]{:S(2)}) collective-permute-start(bf16[136,2048]{1,0:T(8,128)(2,1)S(1)} %collective-permute-done.15.dy0), channel_id=1, source_target_pairs={{0,8},{4,12},{8,0},{12,4},{1,9},{5,13},{9,1},{13,5},{2,10},{6,14},... | collective-permute-start | bytes 1671176 | tf_op jit(solution)/shard_map/ppermute | solution.py:435
  73.1 14.3 %collective-permute-start.21 = (bf16[136,2048]{1,0:T(8,128)(2,1)S(1)}, bf16[136,2048]{1,0:T(8,128)(2,1)S(1)}, u32[]{:S(2)}, u32[]{:S(2)}) collective-permute-start(bf16[136,2048]{1,0:T(8,128)(2,1)S(1)} %collective-permute-done.7.dy1), channel_id=1, source_target_pairs={{0,4},{4,0},{8,12},{12,8},{1,5},{5,1},{9,13},{13,9},{2,6},{6,2},{1... | collective-permute-start | bytes 1671176 | tf_op jit(solution)/shard_map/ppermute | solution.py:475
  74.5 23.4 %collective-permute-start.27 = (bf16[136,2048]{1,0:T(8,128)(2,1)S(1)}, bf16[136,2048]{1,0:T(8,128)(2,1)S(1)}, u32[]{:S(2)}, u32[]{:S(2)}) collective-permute-start(bf16[136,2048]{1,0:T(8,128)(2,1)S(1)} %collective-permute-done.15.dy0), channel_id=1, source_target_pairs={{0,4},{4,0},{8,12},{12,8},{1,5},{5,1},{9,13},{13,9},{2,6},{6,2},{1... | collective-permute-start | bytes 1671176 | tf_op jit(solution)/shard_map/ppermute | solution.py:475
  74.9 21.5 %collective-permute-start.14 = (bf16[136,2048]{1,0:T(8,128)(2,1)}, bf16[136,2048]{1,0:T(8,128)(2,1)}, u32[]{:S(2)}, u32[]{:S(2)}) collective-permute-start(bf16[136,2048]{1,0:T(8,128)(2,1)} %get-tuple-element.70), channel_id=1, source_target_pairs={{0,4},{4,0},{8,12},{12,8},{1,5},{5,1},{9,13},{13,9},{2,6},{6,2},{1... | collective-permute-start | bytes 1671176 | tf_op jit(solution)/shard_map/ppermute | solution.py:475
  77.2 32.7 %collective-permute-start.25 = (bf16[128,2048]{1,0:T(8,128)(2,1)}, bf16[128,2048]{1,0:T(8,128)(2,1)}, u32[]{:S(2)}, u32[]{:S(2)}) collective-permute-start(bf16[128,2048]{1,0:T(8,128)(2,1)} %collective-permute-done.18.refs_4_), channel_id=1, source_target_pairs={{0,1},{1,2},{2,3},{3,0},{4,5},{5,6},{6,7},{7,4},{8,9},{9,10},{10,1... | collective-permute-start | bytes 1572872 | tf_op jit(solution)/shard_map/ppermute | solution.py:435
  86.7 22.3 %collective-permute-start.8 = (bf16[136,2048]{1,0:T(8,128)(2,1)}, bf16[136,2048]{1,0:T(8,128)(2,1)}, u32[]{:S(2)}, u32[]{:S(2)}) collective-permute-start(bf16[136,2048]{1,0:T(8,128)(2,1)} %add_convert_fusion.7), channel_id=1, source_target_pairs={{0,8},{4,12},{8,0},{12,4},{1,9},{5,13},{9,1},{13,5},{2,10},{6,14},... | collective-permute-start | bytes 1671176 | tf_op jit(solution)/shard_map/ppermute | solution.py:435
  87.4 11.9 %collective-permute-start.28 = (bf16[136,2048]{1,0:T(8,128)(2,1)S(1)}, bf16[136,2048]{1,0:T(8,128)(2,1)S(1)}, u32[]{:S(2)}, u32[]{:S(2)}) collective-permute-start(bf16[136,2048]{1,0:T(8,128)(2,1)S(1)} %collective-permute-done.16.dy1), channel_id=1, source_target_pairs={{0,4},{4,0},{8,12},{12,8},{1,5},{5,1},{9,13},{13,9},{2,6},{6,2},{1... | collective-permute-start | bytes 1671176 | tf_op jit(solution)/shard_map/ppermute | solution.py:475
  96.5 12.1 %collective-permute-start.23 = (bf16[136,2048]{1,0:T(8,128)(2,1)}, bf16[136,2048]{1,0:T(8,128)(2,1)S(1)}, u32[]{:S(2)}, u32[]{:S(2)}) collective-permute-start(bf16[136,2048]{1,0:T(8,128)(2,1)} %get-tuple-element.80), channel_id=1, source_target_pairs={{0,4},{4,0},{8,12},{12,8},{1,5},{5,1},{9,13},{13,9},{2,6},{6,2},{1... | collective-permute-start | bytes 1671176 | tf_op jit(solution)/shard_map/ppermute | solution.py:475
  97.9 15.5 %collective-permute-start.17 = (bf16[136,2048]{1,0:T(8,128)(2,1)S(1)}, bf16[136,2048]{1,0:T(8,128)(2,1)S(1)}, u32[]{:S(2)}, u32[]{:S(2)}) collective-permute-start(bf16[136,2048]{1,0:T(8,128)(2,1)S(1)} %add_convert_fusion.6), channel_id=1, source_target_pairs={{0,8},{4,12},{8,0},{12,4},{1,9},{5,13},{9,1},{13,5},{2,10},{6,14},... | collective-permute-start | bytes 1671176 | tf_op jit(solution)/shard_map/ppermute | solution.py:435
  108.3 5.2 %collective-permute-start.30 = (bf16[136,2048]{1,0:T(8,128)(2,1)}, bf16[136,2048]{1,0:T(8,128)(2,1)S(1)}, u32[]{:S(2)}, u32[]{:S(2)}) collective-permute-start(bf16[136,2048]{1,0:T(8,128)(2,1)} %get-tuple-element.87), channel_id=1, source_target_pairs={{0,4},{4,0},{8,12},{12,8},{1,5},{5,1},{9,13},{13,9},{2,6},{6,2},{1... | collective-permute-start | bytes 1671176 | tf_op jit(solution)/shard_map/ppermute | solution.py:475
  108.5 5.6 %collective-permute-start.13 = (bf16[136,2048]{1,0:T(8,128)(2,1)}, bf16[136,2048]{1,0:T(8,128)(2,1)S(1)}, u32[]{:S(2)}, u32[]{:S(2)}) collective-permute-start(bf16[136,2048]{1,0:T(8,128)(2,1)} %get-tuple-element.68), channel_id=1, source_target_pairs={{0,4},{4,0},{8,12},{12,8},{1,5},{5,1},{9,13},{13,9},{2,6},{6,2},{1... | collective-permute-start | bytes 1671176 | tf_op jit(solution)/shard_map/ppermute | solution.py:475
  109.0 15.9 %collective-permute-start.24 = (bf16[136,2048]{1,0:T(8,128)(2,1)S(1)}, bf16[136,2048]{1,0:T(8,128)(2,1)S(1)}, u32[]{:S(2)}, u32[]{:S(2)}) collective-permute-start(bf16[136,2048]{1,0:T(8,128)(2,1)S(1)} %add_convert_fusion.4), channel_id=1, source_target_pairs={{0,8},{4,12},{8,0},{12,4},{1,9},{5,13},{9,1},{13,5},{2,10},{6,14},... | collective-permute-start | bytes 1671176 | tf_op jit(solution)/shard_map/ppermute | solution.py:435
  109.9 4.2 %collective-permute-start.34 = (bf16[128,2048]{1,0:T(8,128)(2,1)}, bf16[128,2048]{1,0:T(8,128)(2,1)S(1)}, u32[]{:S(2)}, u32[]{:S(2)}) collective-permute-start(bf16[128,2048]{1,0:T(8,128)(2,1)} %refs_0_.1), channel_id=1, source_target_pairs={{0,4},{4,0},{8,12},{12,8},{1,5},{5,1},{9,13},{13,9},{2,6},{6,2},{1... | collective-permute-start | bytes 1572872 | tf_op jit(solution)/shard_map/ppermute | solution.py:475
  113.4 13.1 %collective-permute-start.35 = (bf16[128,2048]{1,0:T(8,128)(2,1)}, bf16[128,2048]{1,0:T(8,128)(2,1)S(1)}, u32[]{:S(2)}, u32[]{:S(2)}) collective-permute-start(bf16[128,2048]{1,0:T(8,128)(2,1)} %collective-permute-done.6.refs_1_), channel_id=1, source_target_pairs={{0,4},{4,0},{8,12},{12,8},{1,5},{5,1},{9,13},{13,9},{2,6},{6,2},{1... | collective-permute-start | bytes 1572872 | tf_op jit(solution)/shard_map/ppermute | solution.py:475
  113.4 13.9 %collective-permute-start.22 = (bf16[136,2048]{1,0:T(8,128)(2,1)S(1)}, bf16[136,2048]{1,0:T(8,128)(2,1)S(1)}, u32[]{:S(2)}, u32[]{:S(2)}) collective-permute-start(bf16[136,2048]{1,0:T(8,128)(2,1)S(1)} %copy-done.20), channel_id=1, source_target_pairs={{0,4},{4,0},{8,12},{12,8},{1,5},{5,1},{9,13},{13,9},{2,6},{6,2},{1... | collective-permute-start | bytes 1671176 | tf_op jit(solution)/shard_map/ppermute | solution.py:475
  114.1 16.1 %collective-permute-start.32 = (bf16[128,2048]{1,0:T(8,128)(2,1)}, bf16[128,2048]{1,0:T(8,128)(2,1)}, u32[]{:S(2)}, u32[]{:S(2)}) collective-permute-start(bf16[128,2048]{1,0:T(8,128)(2,1)} %collective-permute-done.25.refs_12_), channel_id=1, source_target_pairs={{0,1},{1,2},{2,3},{3,0},{4,5},{5,6},{6,7},{7,4},{8,9},{9,10},{10,1... | collective-permute-start | bytes 1572872 | tf_op jit(solution)/shard_map/ppermute | solution.py:435
  114.2 16.0 %collective-permute-start.29 = (bf16[136,2048]{1,0:T(8,128)(2,1)S(1)}, bf16[136,2048]{1,0:T(8,128)(2,1)S(1)}, u32[]{:S(2)}, u32[]{:S(2)}) collective-permute-start(bf16[136,2048]{1,0:T(8,128)(2,1)S(1)} %copy-done.21), channel_id=1, source_target_pairs={{0,4},{4,0},{8,12},{12,8},{1,5},{5,1},{9,13},{13,9},{2,6},{6,2},{1... | collective-permute-start | bytes 1671176 | tf_op jit(solution)/shard_map/ppermute | solution.py:475
  125.0 15.5 %collective-permute-start.31 = (bf16[136,2048]{1,0:T(8,128)(2,1)S(1)}, bf16[136,2048]{1,0:T(8,128)(2,1)S(1)}, u32[]{:S(2)}, u32[]{:S(2)}) collective-permute-start(bf16[136,2048]{1,0:T(8,128)(2,1)S(1)} %add_convert_fusion.2), channel_id=1, source_target_pairs={{0,8},{4,12},{8,0},{12,4},{1,9},{5,13},{9,1},{13,5},{2,10},{6,14},... | collective-permute-start | bytes 1671176 | tf_op jit(solution)/shard_map/ppermute | solution.py:435
  127.3 24.7 %collective-permute-start.3 = (bf16[136,2048]{1,0:T(8,128)(2,1)S(1)}, bf16[136,2048]{1,0:T(8,128)(2,1)S(1)}, u32[]{:S(2)}, u32[]{:S(2)}) collective-permute-start(bf16[136,2048]{1,0:T(8,128)(2,1)S(1)} %copy-done.19), channel_id=1, source_target_pairs={{0,4},{4,0},{8,12},{12,8},{1,5},{5,1},{9,13},{13,9},{2,6},{6,2},{1... | collective-permute-start | bytes 1671176 | tf_op jit(solution)/shard_map/ppermute | solution.py:475
  127.3 23.3 %collective-permute-start.36 = (bf16[128,2048]{1,0:T(8,128)(2,1)}, bf16[128,2048]{1,0:T(8,128)(2,1)}, u32[]{:S(2)}, u32[]{:S(2)}) collective-permute-start(bf16[128,2048]{1,0:T(8,128)(2,1)} %collective-permute-done.18.refs_4_), channel_id=1, source_target_pairs={{0,8},{4,12},{8,0},{12,4},{1,9},{5,13},{9,1},{13,5},{2,10},{6,14},... | collective-permute-start | bytes 1572872 | tf_op jit(solution)/shard_map/ppermute | solution.py:435
  130.2 20.5 %collective-permute-start.37 = (bf16[128,2048]{1,0:T(8,128)(2,1)}, bf16[128,2048]{1,0:T(8,128)(2,1)S(1)}, u32[]{:S(2)}, u32[]{:S(2)}) collective-permute-start(bf16[128,2048]{1,0:T(8,128)(2,1)} %collective-permute-done.18.refs_4_), channel_id=1, source_target_pairs={{0,4},{4,0},{8,12},{12,8},{1,5},{5,1},{9,13},{13,9},{2,6},{6,2},{1... | collective-permute-start | bytes 1572872 | tf_op jit(solution)/shard_map/ppermute | solution.py:475
  130.2 28.9 %collective-permute-start.19 = (bf16[136,2048]{1,0:T(8,128)(2,1)S(1)}, bf16[136,2048]{1,0:T(8,128)(2,1)S(1)}, u32[]{:S(2)}, u32[]{:S(2)}) collective-permute-start(bf16[136,2048]{1,0:T(8,128)(2,1)S(1)} %add_convert_fusion.5), channel_id=1, source_target_pairs={{0,3},{1,0},{2,1},{3,2},{4,7},{5,4},{6,5},{7,6},{8,11},{9,8},{10,9... | collective-permute-start | bytes 1671176 | tf_op jit(solution)/shard_map/ppermute | solution.py:435
  140.5 18.6 %collective-permute-start.26 = (bf16[136,2048]{1,0:T(8,128)(2,1)S(1)}, bf16[136,2048]{1,0:T(8,128)(2,1)}, u32[]{:S(2)}, u32[]{:S(2)}) collective-permute-start(bf16[136,2048]{1,0:T(8,128)(2,1)S(1)} %add_convert_fusion.3), channel_id=1, source_target_pairs={{0,1},{1,2},{2,3},{3,0},{4,5},{5,6},{6,7},{7,4},{8,9},{9,10},{10,1... | collective-permute-start | bytes 1671176 | tf_op jit(solution)/shard_map/ppermute | solution.py:435
  150.6 28.4 %collective-permute-start.33 = (bf16[136,2048]{1,0:T(8,128)(2,1)S(1)}, bf16[136,2048]{1,0:T(8,128)(2,1)}, u32[]{:S(2)}, u32[]{:S(2)}) collective-permute-start(bf16[136,2048]{1,0:T(8,128)(2,1)S(1)} %add_convert_fusion.1), channel_id=1, source_target_pairs={{0,2},{1,3},{2,0},{3,1},{4,6},{5,7},{6,4},{7,5},{8,10},{9,11},{10,... | collective-permute-start | bytes 1671176 | tf_op jit(solution)/shard_map/ppermute | solution.py:435
  150.7 15.2 %collective-permute-start.39 = (bf16[128,2048]{1,0:T(8,128)(2,1)}, bf16[128,2048]{1,0:T(8,128)(2,1)}, u32[]{:S(2)}, u32[]{:S(2)}) collective-permute-start(bf16[128,2048]{1,0:T(8,128)(2,1)} %collective-permute-done.32.refs_8_), channel_id=1, source_target_pairs={{0,8},{4,12},{8,0},{12,4},{1,9},{5,13},{9,1},{13,5},{2,10},{6,14},... | collective-permute-start | bytes 1572872 | tf_op jit(solution)/shard_map/ppermute | solution.py:435
  152.0 23.0 %collective-permute-start.42 = (bf16[128,2048]{1,0:T(8,128)(2,1)}, bf16[128,2048]{1,0:T(8,128)(2,1)}, u32[]{:S(2)}, u32[]{:S(2)}) collective-permute-start(bf16[128,2048]{1,0:T(8,128)(2,1)} %collective-permute-done.25.refs_12_), channel_id=1, source_target_pairs={{0,8},{4,12},{8,0},{12,4},{1,9},{5,13},{9,1},{13,5},{2,10},{6,14},... | collective-permute-start | bytes 1572872 | tf_op jit(solution)/shard_map/ppermute | solution.py:435
  152.8 26.4 %copy-start.18 = (bf16[136,2048]{1,0:T(8,128)(2,1)S(1)}, bf16[136,2048]{1,0:T(8,128)(2,1)}, u32[]{:S(2)}) copy-start(bf16[136,2048]{1,0:T(8,128)(2,1)} %get-tuple-element.58) | copy-start | bytes 1671172
  159.0 23.5 %collective-permute-start.43 = (bf16[128,2048]{1,0:T(8,128)(2,1)}, bf16[128,2048]{1,0:T(8,128)(2,1)S(1)}, u32[]{:S(2)}, u32[]{:S(2)}) collective-permute-start(bf16[128,2048]{1,0:T(8,128)(2,1)} %collective-permute-done.25.refs_12_), channel_id=1, source_target_pairs={{0,4},{4,0},{8,12},{12,8},{1,5},{5,1},{9,13},{13,9},{2,6},{6,2},{1... | collective-permute-start | bytes 1572872 | tf_op jit(solution)/shard_map/ppermute | solution.py:475
  159.1 23.4 %collective-permute-start.40 = (bf16[128,2048]{1,0:T(8,128)(2,1)}, bf16[128,2048]{1,0:T(8,128)(2,1)S(1)}, u32[]{:S(2)}, u32[]{:S(2)}) collective-permute-start(bf16[128,2048]{1,0:T(8,128)(2,1)} %collective-permute-done.32.refs_8_), channel_id=1, source_target_pairs={{0,4},{4,0},{8,12},{12,8},{1,5},{5,1},{9,13},{13,9},{2,6},{6,2},{1... | collective-permute-start | bytes 1572872 | tf_op jit(solution)/shard_map/ppermute | solution.py:475
  165.9 16.6 %collective-permute-start.38 = (bf16[128,2048]{1,0:T(8,128)(2,1)}, bf16[128,2048]{1,0:T(8,128)(2,1)}, u32[]{:S(2)}, u32[]{:S(2)}) collective-permute-start(bf16[128,2048]{1,0:T(8,128)(2,1)} %collective-permute-done.36.refs_5_), channel_id=1, source_target_pairs={{0,4},{4,0},{8,12},{12,8},{1,5},{5,1},{9,13},{13,9},{2,6},{6,2},{1... | collective-permute-start | bytes 1572872 | tf_op jit(solution)/shard_map/ppermute | solution.py:475
  175.0 7.5 %collective-permute-start.41 = (bf16[128,2048]{1,0:T(8,128)(2,1)}, bf16[128,2048]{1,0:T(8,128)(2,1)}, u32[]{:S(2)}, u32[]{:S(2)}) collective-permute-start(bf16[128,2048]{1,0:T(8,128)(2,1)} %collective-permute-done.39.refs_9_), channel_id=1, source_target_pairs={{0,4},{4,0},{8,12},{12,8},{1,5},{5,1},{9,13},{13,9},{2,6},{6,2},{1... | collective-permute-start | bytes 1572872 | tf_op jit(solution)/shard_map/ppermute | solution.py:475
  179.0 3.5 %collective-permute-start.44 = (bf16[128,2048]{1,0:T(8,128)(2,1)}, bf16[128,2048]{1,0:T(8,128)(2,1)S(1)}, u32[]{:S(2)}, u32[]{:S(2)}) collective-permute-start(bf16[128,2048]{1,0:T(8,128)(2,1)} %collective-permute-done.42.refs_13_), channel_id=1, source_target_pairs={{0,4},{4,0},{8,12},{12,8},{1,5},{5,1},{9,13},{13,9},{2,6},{6,2},{1... | collective-permute-start | bytes 1572872 | tf_op jit(solution)/shard_map/ppermute | solution.py:475
  (25 other events, 170.1 us)

commit v4 on v3

--- a/solution.py
+++ b/solution.py
@@ -1,4 +1,5 @@
 import functools
+import math
 
 import jax
 import jax.numpy as jnp
@@ -149,13 +150,14 @@
 
 def slopes(gate_in, up_in):
     blocks, slot_cap, hid = gate_in.shape
-    spec = pl.BlockSpec((2, slot_cap, hid), lambda i: (i, 0, 0))
+    step = math.gcd(blocks, 4)
+    spec = pl.BlockSpec((step, slot_cap, hid), lambda i: (i, 0, 0))
     return pl.pallas_call(
         slope_kernel,
-        grid=(blocks // 2,),
+        grid=(blocks // step,),
         out_shape=jax.ShapeDtypeStruct((blocks, slot_cap, 3 * hid), jnp.float32),
         in_specs=[spec] * 2,
-        out_specs=pl.BlockSpec((2, slot_cap, 3 * hid), lambda i: (i, 0, 0)),
+        out_specs=pl.BlockSpec((step, slot_cap, 3 * hid), lambda i: (i, 0, 0)),
         cost_estimate=pl.CostEstimate(
             flops=10 * gate_in.size, bytes_accessed=16 * gate_in.size, transcendentals=gate_in.size
         ),

time: 195 us -> 194 us (level)
  transfers between devices with their start and end apart: 45 -> 45, of which waited for: 14 -> 14; matrix products, arithmetic and copies ran while one was open for 5% -> 5% of each run, Pallas kernels for 24% -> 23%
where the time goes in v4:
time: 194 us
  waiting for transfers between devices  100 us (52%)
  Pallas kernels  54.3 us (28%)
  starting transfers between devices  21 us (11%)
  other arithmetic  8.93 us (5%)
  local copies, waits for them, and re-layouts  7.94 us (4%)
    ppermute x21, waiting for transfers between devices, send(): got = lax.ppermute(value, axis, pairs)  100 us
    pallas_call x4, Pallas kernels, round_backward(): pl.pallas_call(round_kernel, out_shape=[jax.ShapeDtypeStruct((height, wid...  32.7 us
    ppermute x21, starting transfers between devices, send(): got = lax.ppermute(value, axis, pairs)  18 us
    pallas_call x1, Pallas kernels, input_grads(): pl.pallas_call(functools.partial(input_kernel, rounds, slot_cap, halved),...  10.3 us
    convert_element_type x8, other arithmetic, add(): return total.astype(jnp.bfloat16)  6.48 us
    pallas_call x1, Pallas kernels, down_grad(): pl.pallas_call(functools.partial(down_kernel, rounds), grid=(width // TIL...  6.27 us
    pallas_call x1, Pallas kernels, slopes(): pl.pallas_call(slope_kernel, grid=(blocks // step,), out_shape=jax.ShapeD...  5.07 us
  transfers between devices with their start and end apart: 45, of which 14 were waited for; matrix products, arithmetic and copies ran while one was open for 5% of the time, Pallas kernels for 23%

profile of v4, /device:TPU:0, one launch (start us, length us, event | category | flops | bytes accessed | tf_op | source)
XLA Modules:
  0.0 193.8 jit_solution(4034490322738636126)
XLA Ops:
  0.6 0.7 fusion.3
  1.3 0.7 fusion.2
  2.0 1.1 pad_maximum_fusion.dy0
  3.1 3.0 %collective-permute-start = (bf16[136,2048]{1,0:T(8,128)(2,1)S(1)}, bf16[136,2048]{1,0:T(8,128)(2,1)S(1)}, u32[]{:S(2)}, u32[]{:S(2)}) collective-permute-start(bf16[136,2048]{1,0:T(8,128)(2,1)S(1)} %pad_maximum_fusion.dy0), channel_id=1, source_target_pairs={{0,8},{4,12},{8,0},{12,4},{1,9},{5,13},{9,1},{13,5},{2,10},{6,14},... | collective-permute-start | bytes 1671176 | tf_op jit(solution)/shard_map/ppermute | solution.py:437
  6.1 1.6 collective-permute-start.9
  7.7 11.0 %collective-permute-done.dy1 = bf16[136,2048]{1,0:T(8,128)(2,1)S(1)} collective-permute-done((bf16[136,2048]{1,0:T(8,128)(2,1)S(1)}, bf16[136,2048]{1,0:T(8,128)(2,1)S(1)}, u32[]{:S(2)}, u32[]{:S(2)}) %collective-permute-start) | collective-permute-done | bytes 557088 | tf_op jit(solution)/shard_map/ppermute | solution.py:437
  18.7 3.3 %collective-permute-done.9.dy0 = bf16[136,2048]{1,0:T(8,128)(2,1)S(1)} collective-permute-done((bf16[136,2048]{1,0:T(8,128)(2,1)S(1)}, bf16[136,2048]{1,0:T(8,128)(2,1)S(1)}, u32[]{:S(2)}, u32[]{:S(2)}) %collective-permute-start.9) | collective-permute-done | bytes 557088 | tf_op jit(solution)/shard_map/ppermute | solution.py:437
  22.6 1.7 collective-permute-start.5
  24.3 1.5 collective-permute-start.6
  25.9 0.8 stack.71.ids_ref
  26.6 5.1 %shard_map.128.slope_hbm = f32[16,80,1152]{2,1,0:T(8,128)} custom-call(bf16[16,80,384]{2,1,0:T(8,128)(2,1)} %bitcast.43, bf16[16,80,384]{2,1,0:T(8,128)(2,1)} %bitcast.44), custom_call_target="tpu_custom_call" | custom-call | flops 4915200 | bytes 7864320 | tf_op jit(solution)/shard_map/pallas_call | solution.py:155
  31.8 5.7 %collective-permute-done.10.dy1 = bf16[136,2048]{1,0:T(8,128)(2,1)S(1)} collective-permute-done((bf16[136,2048]{1,0:T(8,128)(2,1)S(1)}, bf16[136,2048]{1,0:T(8,128)(2,1)S(1)}, u32[]{:S(2)}, u32[]{:S(2)}) %collective-permute-start.10) | collective-permute-done | bytes 557088 | tf_op jit(solution)/shard_map/ppermute | solution.py:437
  37.5 8.2 %shard_map.129 = (bf16[136,2048]{1,0:T(8,128)(2,1)}, bf16[136,2048]{1,0:T(8,128)(2,1)}, bf16[136,2048]{1,0:T(8,128)(2,1)}, bf16[136,2048]{1,0:T(8,128)(2,1)}, bf...) custom-call(s32[5]{0:T(128)} %stack.71.ids_ref, ...), custom_call_target="tpu_custom_call" | custom-call | flops 1845493760 | bytes 11714560 | tf_op jit(solution)/shard_map/pallas_call | solution.py:294
  45.8 2.7 %collective-permute-done.6.refs_1_ = bf16[128,2048]{1,0:T(8,128)(2,1)} collective-permute-done((bf16[128,2048]{1,0:T(8,128)(2,1)}, bf16[128,2048]{1,0:T(8,128)(2,1)}, u32[]{:S(2)}, u32[]{:S(2)}) %collective-permute-start.6) | collective-permute-done | bytes 524320 | tf_op jit(solution)/shard_map/ppermute | solution.py:437
  49.0 0.7 stack.76.ids_ref
  50.2 8.1 %shard_map.130 = (bf16[136,2048]{1,0:T(8,128)(2,1)}, bf16[136,2048]{1,0:T(8,128)(2,1)}, bf16[136,2048]{1,0:T(8,128)(2,1)}, bf16[136,2048]{1,0:T(8,128)(2,1)}, bf...) custom-call(s32[5]{0:T(128)} %stack.76.ids_ref, ...), custom_call_target="tpu_custom_call" | custom-call | flops 1845493760 | bytes 11714560 | tf_op jit(solution)/shard_map/pallas_call | solution.py:294
  58.3 13.3 %collective-permute-done.15.dy0 = bf16[136,2048]{1,0:T(8,128)(2,1)S(1)} collective-permute-done((bf16[136,2048]{1,0:T(8,128)(2,1)S(1)}, bf16[136,2048]{1,0:T(8,128)(2,1)S(1)}, u32[]{:S(2)}, u32[]{:S(2)}) %collective-permute-start.15) | collective-permute-done | bytes 557088 | tf_op jit(solution)/shard_map/ppermute | solution.py:437
  71.6 1.5 collective-permute-start.16
  73.2 0.7 stack.86.ids_ref
  73.9 0.6 stack.81.ids_ref
  75.0 2.1 %add_convert_fusion.7 = bf16[136,2048]{1,0:T(8,128)(2,1)} fusion(bf16[136,2048]{1,0:T(8,128)(2,1)} %collective-permute-done.4, bf16[136,2048]{1,0:T(8,128)(2,1)} %get-tuple-element.60), kind=kLoop, calls=%fused_computation.7 | loop fusion | flops 1114112 | bytes 1671168 | tf_op jit(solution)/shard_map/convert_element_type | solution.py:446
  77.2 8.4 %collective-permute-done.16.dy1 = bf16[136,2048]{1,0:T(8,128)(2,1)S(1)} collective-permute-done((bf16[136,2048]{1,0:T(8,128)(2,1)S(1)}, bf16[136,2048]{1,0:T(8,128)(2,1)S(1)}, u32[]{:S(2)}, u32[]{:S(2)}) %collective-permute-start.16) | collective-permute-done | bytes 557088 | tf_op jit(solution)/shard_map/ppermute | solution.py:437
  85.6 1.5 collective-permute-start.8
  87.1 0.8 copy-done.8
  87.9 8.2 %shard_map.131 = (bf16[136,2048]{1,0:T(8,128)(2,1)}, bf16[136,2048]{1,0:T(8,128)(2,1)}, bf16[136,2048]{1,0:T(8,128)(2,1)}, bf16[136,2048]{1,0:T(8,128)(2,1)}, bf...) custom-call(s32[5]{0:T(128)} %stack.81.ids_ref, ...), custom_call_target="tpu_custom_call" | custom-call | flops 1845493760 | bytes 11714560 | tf_op jit(solution)/shard_map/pallas_call | solution.py:294
  96.2 1.4 add_convert_fusion.6
  97.6 0.6 collective-permute-start.17
  98.4 0.8 copy-done.12
  99.2 8.1 %shard_map.132 = (bf16[136,2048]{1,0:T(8,128)(2,1)}, bf16[136,2048]{1,0:T(8,128)(2,1)}, bf16[136,2048]{1,0:T(8,128)(2,1)}, bf16[136,2048]{1,0:T(8,128)(2,1)}, bf...) custom-call(s32[5]{0:T(128)} %stack.86.ids_ref, ...), custom_call_target="tpu_custom_call" | custom-call | flops 1845493760 | bytes 11714560 | tf_op jit(solution)/shard_map/pallas_call | solution.py:294
  108.2 1.3 collective-permute-start.24
  109.5 3.6 %collective-permute-done.17 = bf16[136,2048]{1,0:T(8,128)(2,1)S(1)} collective-permute-done((bf16[136,2048]{1,0:T(8,128)(2,1)S(1)}, bf16[136,2048]{1,0:T(8,128)(2,1)S(1)}, u32[]{:S(2)}, u32[]{:S(2)}) %collective-permute-start.17) | collective-permute-done | bytes 557088 | tf_op jit(solution)/shard_map/ppermute | solution.py:437
  114.0 10.6 %collective-permute-done.24 = bf16[136,2048]{1,0:T(8,128)(2,1)S(1)} collective-permute-done((bf16[136,2048]{1,0:T(8,128)(2,1)S(1)}, bf16[136,2048]{1,0:T(8,128)(2,1)S(1)}, u32[]{:S(2)}, u32[]{:S(2)}) %collective-permute-start.24) | collective-permute-done | bytes 557088 | tf_op jit(solution)/shard_map/ppermute | solution.py:437
  125.4 0.8 copy-done.19
  126.2 1.5 collective-permute-start.36
  128.0 1.8 collective-permute-done.32.refs_8_
  129.8 10.3 %collective-permute-done.31 = bf16[136,2048]{1,0:T(8,128)(2,1)S(1)} collective-permute-done((bf16[136,2048]{1,0:T(8,128)(2,1)S(1)}, bf16[136,2048]{1,0:T(8,128)(2,1)S(1)}, u32[]{:S(2)}, u32[]{:S(2)}) %collective-permute-start.31) | collective-permute-done | bytes 557088 | tf_op jit(solution)/shard_map/ppermute | solution.py:437
  140.4 9.9 %collective-permute-done.36.refs_5_ = bf16[128,2048]{1,0:T(8,128)(2,1)} collective-permute-done((bf16[128,2048]{1,0:T(8,128)(2,1)}, bf16[128,2048]{1,0:T(8,128)(2,1)}, u32[]{:S(2)}, u32[]{:S(2)}) %collective-permute-start.36) | collective-permute-done | bytes 524320 | tf_op jit(solution)/shard_map/ppermute | solution.py:437
  150.3 0.6 collective-permute-start.39
  150.9 1.5 collective-permute-start.42
  152.4 6.3 %shard_map.134 = bf16[384,2048]{1,0:T(8,128)(2,1)} custom-call(bf16[320,384]{1,0:T(8,128)(2,1)} %get-tuple-element.102.refs_0_, bf16[320,384]{1,0:T(8,128)(2,1)} %get-tuple-element.103.refs_1_, bf16[320,384]{1,0:T(8,128)(2,1)} %get-tuple-element.104.refs_2_, bf16[320,384]{1,0:T(8,128)(2,1)} %get-tuple-element.105.refs_3_, ...), custom_call_target="tpu_custom_call" | custom-call | flops 2013265920 | bytes 7798784 | tf_op jit(solution)/shard_map/pallas_call | solution.py:353
  159.2 6.3 %collective-permute-done.39.refs_9_ = bf16[128,2048]{1,0:T(8,128)(2,1)} collective-permute-done((bf16[128,2048]{1,0:T(8,128)(2,1)}, bf16[128,2048]{1,0:T(8,128)(2,1)}, u32[]{:S(2)}, u32[]{:S(2)}) %collective-permute-start.39) | collective-permute-done | bytes 524320 | tf_op jit(solution)/shard_map/ppermute | solution.py:437
  165.5 9.1 %collective-permute-done.42.refs_13_ = bf16[128,2048]{1,0:T(8,128)(2,1)} collective-permute-done((bf16[128,2048]{1,0:T(8,128)(2,1)}, bf16[128,2048]{1,0:T(8,128)(2,1)}, u32[]{:S(2)}, u32[]{:S(2)}) %collective-permute-start.42) | collective-permute-done | bytes 524320 | tf_op jit(solution)/shard_map/ppermute | solution.py:437
  174.7 4.0 %collective-permute-done.33 = bf16[136,2048]{1,0:T(8,128)(2,1)} collective-permute-done((bf16[136,2048]{1,0:T(8,128)(2,1)S(1)}, bf16[136,2048]{1,0:T(8,128)(2,1)}, u32[]{:S(2)}, u32[]{:S(2)}) %collective-permute-start.33) | collective-permute-done | bytes 557088 | tf_op jit(solution)/shard_map/ppermute | solution.py:437
  178.8 1.9 add_convert_fusion
  180.7 0.8 slice.8
  181.5 0.6 slice_bitcast_fusion
  182.2 0.7 copy-done.25
  183.3 10.3 %shard_map.133 = (bf16[2048,384]{1,0:T(8,128)(2,1)}, bf16[2048,384]{1,0:T(8,128)(2,1)}) custom-call(bf16[128,2048]{1,0:T(8,128)(2,1)} %refs_0_.1, bf16[128,2048]{1,0:T(8,128)(2,1)} %collective-permute-done.6.refs_1_, bf16[128,2048]{1,0:T(8,128)(2,1)} %copy-done.22, bf16[128,2048]{1,0:T(8,128)(2,1)} %copy-done.23, ...), custom_call_target="tpu_custom_call" | custom-call | flops 4697620480 | bytes 13500416 | tf_op jit(solution)/shard_map/pallas_call | solution.py:414
  (122 shorter events, 6.6 us)
Async XLA Ops:
  3.1 28.6 %copy-start = (bf16[136,2048]{1,0:T(8,128)(2,1)}, bf16[136,2048]{1,0:T(8,128)(2,1)S(1)}, u32[]{:S(2)}) copy-start(bf16[136,2048]{1,0:T(8,128)(2,1)S(1)} %pad_maximum_fusion.dy0) | copy-start | bytes 1671172
  3.1 15.6 %collective-permute-start = (bf16[136,2048]{1,0:T(8,128)(2,1)S(1)}, bf16[136,2048]{1,0:T(8,128)(2,1)S(1)}, u32[]{:S(2)}, u32[]{:S(2)}) collective-permute-start(bf16[136,2048]{1,0:T(8,128)(2,1)S(1)} %pad_maximum_fusion.dy0), channel_id=1, source_target_pairs={{0,8},{4,12},{8,0},{12,4},{1,9},{5,13},{9,1},{13,5},{2,10},{6,14},... | collective-permute-start | bytes 1671176 | tf_op jit(solution)/shard_map/ppermute | solution.py:437
  6.1 15.9 %collective-permute-start.9 = (bf16[136,2048]{1,0:T(8,128)(2,1)S(1)}, bf16[136,2048]{1,0:T(8,128)(2,1)S(1)}, u32[]{:S(2)}, u32[]{:S(2)}) collective-permute-start(bf16[136,2048]{1,0:T(8,128)(2,1)S(1)} %pad_maximum_fusion.dy0), channel_id=1, source_target_pairs={{0,1},{1,2},{2,3},{3,0},{4,5},{5,6},{6,7},{7,4},{8,9},{9,10},{10,1... | collective-permute-start | bytes 1671176 | tf_op jit(solution)/shard_map/ppermute | solution.py:437
  7.7 18.1 %collective-permute-start.1 = (bf16[136,2048]{1,0:T(8,128)(2,1)S(1)}, bf16[136,2048]{1,0:T(8,128)(2,1)S(1)}, u32[]{:S(2)}, u32[]{:S(2)}) collective-permute-start(bf16[136,2048]{1,0:T(8,128)(2,1)S(1)} %pad_maximum_fusion.dy0), channel_id=1, source_target_pairs={{0,4},{4,0},{8,12},{12,8},{1,5},{5,1},{9,13},{13,9},{2,6},{6,2},{1... | collective-permute-start | bytes 1671176 | tf_op jit(solution)/shard_map/ppermute | solution.py:477
  22.1 9.7 %collective-permute-start.2 = (bf16[136,2048]{1,0:T(8,128)(2,1)S(1)}, bf16[136,2048]{1,0:T(8,128)(2,1)}, u32[]{:S(2)}, u32[]{:S(2)}) collective-permute-start(bf16[136,2048]{1,0:T(8,128)(2,1)S(1)} %collective-permute-done.dy1), channel_id=1, source_target_pairs={{0,4},{4,0},{8,12},{12,8},{1,5},{5,1},{9,13},{13,9},{2,6},{6,2},{1... | collective-permute-start | bytes 1671176 | tf_op jit(solution)/shard_map/ppermute | solution.py:477
  22.1 15.4 %collective-permute-start.10 = (bf16[136,2048]{1,0:T(8,128)(2,1)S(1)}, bf16[136,2048]{1,0:T(8,128)(2,1)S(1)}, u32[]{:S(2)}, u32[]{:S(2)}) collective-permute-start(bf16[136,2048]{1,0:T(8,128)(2,1)S(1)} %collective-permute-done.9.dy0), channel_id=1, source_target_pairs={{0,8},{4,12},{8,0},{12,4},{1,9},{5,13},{9,1},{13,5},{2,10},{6,14},... | collective-permute-start | bytes 1671176 | tf_op jit(solution)/shard_map/ppermute | solution.py:437
  22.6 23.1 %collective-permute-start.5 = (bf16[136,2048]{1,0:T(8,128)(2,1)S(1)}, bf16[136,2048]{1,0:T(8,128)(2,1)S(1)}, u32[]{:S(2)}, u32[]{:S(2)}) collective-permute-start(bf16[136,2048]{1,0:T(8,128)(2,1)S(1)} %pad_maximum_fusion.dy0), channel_id=1, source_target_pairs={{0,3},{1,0},{2,1},{3,2},{4,7},{5,4},{6,5},{7,6},{8,11},{9,8},{10,9... | collective-permute-start | bytes 1671176 | tf_op jit(solution)/shard_map/ppermute | solution.py:437
  24.3 24.1 %collective-permute-start.6 = (bf16[128,2048]{1,0:T(8,128)(2,1)}, bf16[128,2048]{1,0:T(8,128)(2,1)}, u32[]{:S(2)}, u32[]{:S(2)}) collective-permute-start(bf16[128,2048]{1,0:T(8,128)(2,1)} %refs_0_.1), channel_id=1, source_target_pairs={{0,8},{4,12},{8,0},{12,4},{1,9},{5,13},{9,1},{13,5},{2,10},{6,14},... | collective-permute-start | bytes 1572872 | tf_op jit(solution)/shard_map/ppermute | solution.py:437
  25.8 23.1 %collective-permute-start.11 = (bf16[136,2048]{1,0:T(8,128)(2,1)S(1)}, bf16[136,2048]{1,0:T(8,128)(2,1)}, u32[]{:S(2)}, u32[]{:S(2)}) collective-permute-start(bf16[136,2048]{1,0:T(8,128)(2,1)S(1)} %collective-permute-done.9.dy0), channel_id=1, source_target_pairs={{0,4},{4,0},{8,12},{12,8},{1,5},{5,1},{9,13},{13,9},{2,6},{6,2},{1... | collective-permute-start | bytes 1671176 | tf_op jit(solution)/shard_map/ppermute | solution.py:477
  31.7 39.9 %collective-permute-start.15 = (bf16[136,2048]{1,0:T(8,128)(2,1)S(1)}, bf16[136,2048]{1,0:T(8,128)(2,1)S(1)}, u32[]{:S(2)}, u32[]{:S(2)}) collective-permute-start(bf16[136,2048]{1,0:T(8,128)(2,1)S(1)} %pad_maximum_fusion.dy0), channel_id=1, source_target_pairs={{0,2},{1,3},{2,0},{3,1},{4,6},{5,7},{6,4},{7,5},{8,10},{9,11},{10,... | collective-permute-start | bytes 1671176 | tf_op jit(solution)/shard_map/ppermute | solution.py:437
  37.5 12.2 %collective-permute-start.12 = (bf16[136,2048]{1,0:T(8,128)(2,1)S(1)}, bf16[136,2048]{1,0:T(8,128)(2,1)}, u32[]{:S(2)}, u32[]{:S(2)}) collective-permute-start(bf16[136,2048]{1,0:T(8,128)(2,1)S(1)} %collective-permute-done.10.dy1), channel_id=1, source_target_pairs={{0,4},{4,0},{8,12},{12,8},{1,5},{5,1},{9,13},{13,9},{2,6},{6,2},{1... | collective-permute-start | bytes 1671176 | tf_op jit(solution)/shard_map/ppermute | solution.py:477
  48.4 24.7 %collective-permute-start.7 = (bf16[136,2048]{1,0:T(8,128)(2,1)S(1)}, bf16[136,2048]{1,0:T(8,128)(2,1)S(1)}, u32[]{:S(2)}, u32[]{:S(2)}) collective-permute-start(bf16[136,2048]{1,0:T(8,128)(2,1)S(1)} %collective-permute-done.5.dy0), channel_id=1, source_target_pairs={{0,8},{4,12},{8,0},{12,4},{1,9},{5,13},{9,1},{13,5},{2,10},{6,14},... | collective-permute-start | bytes 1671176 | tf_op jit(solution)/shard_map/ppermute | solution.py:437
  49.0 25.9 %collective-permute-start.4 = (bf16[136,2048]{1,0:T(8,128)(2,1)}, bf16[136,2048]{1,0:T(8,128)(2,1)}, u32[]{:S(2)}, u32[]{:S(2)}) collective-permute-start(bf16[136,2048]{1,0:T(8,128)(2,1)} %get-tuple-element.61), channel_id=1, source_target_pairs={{0,4},{4,0},{8,12},{12,8},{1,5},{5,1},{9,13},{13,9},{2,6},{6,2},{1... | collective-permute-start | bytes 1671176 | tf_op jit(solution)/shard_map/ppermute | solution.py:477
  49.0 25.5 %collective-permute-start.18 = (bf16[128,2048]{1,0:T(8,128)(2,1)}, bf16[128,2048]{1,0:T(8,128)(2,1)}, u32[]{:S(2)}, u32[]{:S(2)}) collective-permute-start(bf16[128,2048]{1,0:T(8,128)(2,1)} %refs_0_.1), channel_id=1, source_target_pairs={{0,1},{1,2},{2,3},{3,0},{4,5},{5,6},{6,7},{7,4},{8,9},{9,10},{10,1... | collective-permute-start | bytes 1572872 | tf_op jit(solution)/shard_map/ppermute | solution.py:437
  49.7 27.5 %collective-permute-start.20 = (bf16[136,2048]{1,0:T(8,128)(2,1)S(1)}, bf16[136,2048]{1,0:T(8,128)(2,1)S(1)}, u32[]{:S(2)}, u32[]{:S(2)}) collective-permute-start(bf16[136,2048]{1,0:T(8,128)(2,1)S(1)} %collective-permute-done.5.dy0), channel_id=1, source_target_pairs={{0,4},{4,0},{8,12},{12,8},{1,5},{5,1},{9,13},{13,9},{2,6},{6,2},{1... | collective-permute-start | bytes 1671176 | tf_op jit(solution)/shard_map/ppermute | solution.py:477
  71.6 24.4 %copy-start.2 = (bf16[136,2048]{1,0:T(8,128)(2,1)}, bf16[136,2048]{1,0:T(8,128)(2,1)S(1)}, u32[]{:S(2)}) copy-start(bf16[136,2048]{1,0:T(8,128)(2,1)S(1)} %collective-permute-done.15.dy0) | copy-start | bytes 1671172
  71.6 13.9 %collective-permute-start.16 = (bf16[136,2048]{1,0:T(8,128)(2,1)S(1)}, bf16[136,2048]{1,0:T(8,128)(2,1)S(1)}, u32[]{:S(2)}, u32[]{:S(2)}) collective-permute-start(bf16[136,2048]{1,0:T(8,128)(2,1)S(1)} %collective-permute-done.15.dy0), channel_id=1, source_target_pairs={{0,8},{4,12},{8,0},{12,4},{1,9},{5,13},{9,1},{13,5},{2,10},{6,14},... | collective-permute-start | bytes 1671176 | tf_op jit(solution)/shard_map/ppermute | solution.py:437
  73.1 13.9 %collective-permute-start.21 = (bf16[136,2048]{1,0:T(8,128)(2,1)S(1)}, bf16[136,2048]{1,0:T(8,128)(2,1)S(1)}, u32[]{:S(2)}, u32[]{:S(2)}) collective-permute-start(bf16[136,2048]{1,0:T(8,128)(2,1)S(1)} %collective-permute-done.7.dy1), channel_id=1, source_target_pairs={{0,4},{4,0},{8,12},{12,8},{1,5},{5,1},{9,13},{13,9},{2,6},{6,2},{1... | collective-permute-start | bytes 1671176 | tf_op jit(solution)/shard_map/ppermute | solution.py:477
  74.5 23.0 %collective-permute-start.27 = (bf16[136,2048]{1,0:T(8,128)(2,1)S(1)}, bf16[136,2048]{1,0:T(8,128)(2,1)S(1)}, u32[]{:S(2)}, u32[]{:S(2)}) collective-permute-start(bf16[136,2048]{1,0:T(8,128)(2,1)S(1)} %collective-permute-done.15.dy0), channel_id=1, source_target_pairs={{0,4},{4,0},{8,12},{12,8},{1,5},{5,1},{9,13},{13,9},{2,6},{6,2},{1... | collective-permute-start | bytes 1671176 | tf_op jit(solution)/shard_map/ppermute | solution.py:477
  74.9 21.2 %collective-permute-start.14 = (bf16[136,2048]{1,0:T(8,128)(2,1)}, bf16[136,2048]{1,0:T(8,128)(2,1)}, u32[]{:S(2)}, u32[]{:S(2)}) collective-permute-start(bf16[136,2048]{1,0:T(8,128)(2,1)} %get-tuple-element.70), channel_id=1, source_target_pairs={{0,4},{4,0},{8,12},{12,8},{1,5},{5,1},{9,13},{13,9},{2,6},{6,2},{1... | collective-permute-start | bytes 1671176 | tf_op jit(solution)/shard_map/ppermute | solution.py:477
  77.2 32.3 %collective-permute-start.25 = (bf16[128,2048]{1,0:T(8,128)(2,1)}, bf16[128,2048]{1,0:T(8,128)(2,1)}, u32[]{:S(2)}, u32[]{:S(2)}) collective-permute-start(bf16[128,2048]{1,0:T(8,128)(2,1)} %collective-permute-done.18.refs_4_), channel_id=1, source_target_pairs={{0,1},{1,2},{2,3},{3,0},{4,5},{5,6},{6,7},{7,4},{8,9},{9,10},{10,1... | collective-permute-start | bytes 1572872 | tf_op jit(solution)/shard_map/ppermute | solution.py:437
  85.6 22.6 %collective-permute-start.8 = (bf16[136,2048]{1,0:T(8,128)(2,1)}, bf16[136,2048]{1,0:T(8,128)(2,1)}, u32[]{:S(2)}, u32[]{:S(2)}) collective-permute-start(bf16[136,2048]{1,0:T(8,128)(2,1)} %add_convert_fusion.7), channel_id=1, source_target_pairs={{0,8},{4,12},{8,0},{12,4},{1,9},{5,13},{9,1},{13,5},{2,10},{6,14},... | collective-permute-start | bytes 1671176 | tf_op jit(solution)/shard_map/ppermute | solution.py:437
  87.1 11.1 %collective-permute-start.28 = (bf16[136,2048]{1,0:T(8,128)(2,1)S(1)}, bf16[136,2048]{1,0:T(8,128)(2,1)S(1)}, u32[]{:S(2)}, u32[]{:S(2)}) collective-permute-start(bf16[136,2048]{1,0:T(8,128)(2,1)S(1)} %collective-permute-done.16.dy1), channel_id=1, source_target_pairs={{0,4},{4,0},{8,12},{12,8},{1,5},{5,1},{9,13},{13,9},{2,6},{6,2},{1... | collective-permute-start | bytes 1671176 | tf_op jit(solution)/shard_map/ppermute | solution.py:477
  96.1 11.8 %collective-permute-start.23 = (bf16[136,2048]{1,0:T(8,128)(2,1)}, bf16[136,2048]{1,0:T(8,128)(2,1)S(1)}, u32[]{:S(2)}, u32[]{:S(2)}) collective-permute-start(bf16[136,2048]{1,0:T(8,128)(2,1)} %get-tuple-element.80), channel_id=1, source_target_pairs={{0,4},{4,0},{8,12},{12,8},{1,5},{5,1},{9,13},{13,9},{2,6},{6,2},{1... | collective-permute-start | bytes 1671176 | tf_op jit(solution)/shard_map/ppermute | solution.py:477
  97.6 15.5 %collective-permute-start.17 = (bf16[136,2048]{1,0:T(8,128)(2,1)S(1)}, bf16[136,2048]{1,0:T(8,128)(2,1)S(1)}, u32[]{:S(2)}, u32[]{:S(2)}) collective-permute-start(bf16[136,2048]{1,0:T(8,128)(2,1)S(1)} %add_convert_fusion.6), channel_id=1, source_target_pairs={{0,8},{4,12},{8,0},{12,4},{1,9},{5,13},{9,1},{13,5},{2,10},{6,14},... | collective-permute-start | bytes 1671176 | tf_op jit(solution)/shard_map/ppermute | solution.py:437
  107.3 5.7 %collective-permute-start.30 = (bf16[136,2048]{1,0:T(8,128)(2,1)}, bf16[136,2048]{1,0:T(8,128)(2,1)S(1)}, u32[]{:S(2)}, u32[]{:S(2)}) collective-permute-start(bf16[136,2048]{1,0:T(8,128)(2,1)} %get-tuple-element.87), channel_id=1, source_target_pairs={{0,4},{4,0},{8,12},{12,8},{1,5},{5,1},{9,13},{13,9},{2,6},{6,2},{1... | collective-permute-start | bytes 1671176 | tf_op jit(solution)/shard_map/ppermute | solution.py:477
  107.9 5.9 %collective-permute-start.13 = (bf16[136,2048]{1,0:T(8,128)(2,1)}, bf16[136,2048]{1,0:T(8,128)(2,1)S(1)}, u32[]{:S(2)}, u32[]{:S(2)}) collective-permute-start(bf16[136,2048]{1,0:T(8,128)(2,1)} %get-tuple-element.68), channel_id=1, source_target_pairs={{0,4},{4,0},{8,12},{12,8},{1,5},{5,1},{9,13},{13,9},{2,6},{6,2},{1... | collective-permute-start | bytes 1671176 | tf_op jit(solution)/shard_map/ppermute | solution.py:477
  108.2 16.4 %collective-permute-start.24 = (bf16[136,2048]{1,0:T(8,128)(2,1)S(1)}, bf16[136,2048]{1,0:T(8,128)(2,1)S(1)}, u32[]{:S(2)}, u32[]{:S(2)}) collective-permute-start(bf16[136,2048]{1,0:T(8,128)(2,1)S(1)} %add_convert_fusion.4), channel_id=1, source_target_pairs={{0,8},{4,12},{8,0},{12,4},{1,9},{5,13},{9,1},{13,5},{2,10},{6,14},... | collective-permute-start | bytes 1671176 | tf_op jit(solution)/shard_map/ppermute | solution.py:437
  109.5 4.3 %collective-permute-start.34 = (bf16[128,2048]{1,0:T(8,128)(2,1)}, bf16[128,2048]{1,0:T(8,128)(2,1)S(1)}, u32[]{:S(2)}, u32[]{:S(2)}) collective-permute-start(bf16[128,2048]{1,0:T(8,128)(2,1)} %refs_0_.1), channel_id=1, source_target_pairs={{0,4},{4,0},{8,12},{12,8},{1,5},{5,1},{9,13},{13,9},{2,6},{6,2},{1... | collective-permute-start | bytes 1572872 | tf_op jit(solution)/shard_map/ppermute | solution.py:477
  113.1 12.4 %collective-permute-start.35 = (bf16[128,2048]{1,0:T(8,128)(2,1)}, bf16[128,2048]{1,0:T(8,128)(2,1)S(1)}, u32[]{:S(2)}, u32[]{:S(2)}) collective-permute-start(bf16[128,2048]{1,0:T(8,128)(2,1)} %collective-permute-done.6.refs_1_), channel_id=1, source_target_pairs={{0,4},{4,0},{8,12},{12,8},{1,5},{5,1},{9,13},{13,9},{2,6},{6,2},{1... | collective-permute-start | bytes 1572872 | tf_op jit(solution)/shard_map/ppermute | solution.py:477
  113.1 13.1 %collective-permute-start.22 = (bf16[136,2048]{1,0:T(8,128)(2,1)S(1)}, bf16[136,2048]{1,0:T(8,128)(2,1)S(1)}, u32[]{:S(2)}, u32[]{:S(2)}) collective-permute-start(bf16[136,2048]{1,0:T(8,128)(2,1)S(1)} %copy-done.20), channel_id=1, source_target_pairs={{0,4},{4,0},{8,12},{12,8},{1,5},{5,1},{9,13},{13,9},{2,6},{6,2},{1... | collective-permute-start | bytes 1671176 | tf_op jit(solution)/shard_map/ppermute | solution.py:477
  113.7 16.1 %collective-permute-start.32 = (bf16[128,2048]{1,0:T(8,128)(2,1)}, bf16[128,2048]{1,0:T(8,128)(2,1)}, u32[]{:S(2)}, u32[]{:S(2)}) collective-permute-start(bf16[128,2048]{1,0:T(8,128)(2,1)} %collective-permute-done.25.refs_12_), channel_id=1, source_target_pairs={{0,1},{1,2},{2,3},{3,0},{4,5},{5,6},{6,7},{7,4},{8,9},{9,10},{10,1... | collective-permute-start | bytes 1572872 | tf_op jit(solution)/shard_map/ppermute | solution.py:437
  113.8 16.0 %collective-permute-start.29 = (bf16[136,2048]{1,0:T(8,128)(2,1)S(1)}, bf16[136,2048]{1,0:T(8,128)(2,1)S(1)}, u32[]{:S(2)}, u32[]{:S(2)}) collective-permute-start(bf16[136,2048]{1,0:T(8,128)(2,1)S(1)} %copy-done.21), channel_id=1, source_target_pairs={{0,4},{4,0},{8,12},{12,8},{1,5},{5,1},{9,13},{13,9},{2,6},{6,2},{1... | collective-permute-start | bytes 1671176 | tf_op jit(solution)/shard_map/ppermute | solution.py:477
  124.6 15.5 %collective-permute-start.31 = (bf16[136,2048]{1,0:T(8,128)(2,1)S(1)}, bf16[136,2048]{1,0:T(8,128)(2,1)S(1)}, u32[]{:S(2)}, u32[]{:S(2)}) collective-permute-start(bf16[136,2048]{1,0:T(8,128)(2,1)S(1)} %add_convert_fusion.2), channel_id=1, source_target_pairs={{0,8},{4,12},{8,0},{12,4},{1,9},{5,13},{9,1},{13,5},{2,10},{6,14},... | collective-permute-start | bytes 1671176 | tf_op jit(solution)/shard_map/ppermute | solution.py:437
  126.2 24.7 %collective-permute-start.3 = (bf16[136,2048]{1,0:T(8,128)(2,1)S(1)}, bf16[136,2048]{1,0:T(8,128)(2,1)S(1)}, u32[]{:S(2)}, u32[]{:S(2)}) collective-permute-start(bf16[136,2048]{1,0:T(8,128)(2,1)S(1)} %copy-done.19), channel_id=1, source_target_pairs={{0,4},{4,0},{8,12},{12,8},{1,5},{5,1},{9,13},{13,9},{2,6},{6,2},{1... | collective-permute-start | bytes 1671176 | tf_op jit(solution)/shard_map/ppermute | solution.py:477
  126.2 24.1 %collective-permute-start.36 = (bf16[128,2048]{1,0:T(8,128)(2,1)}, bf16[128,2048]{1,0:T(8,128)(2,1)}, u32[]{:S(2)}, u32[]{:S(2)}) collective-permute-start(bf16[128,2048]{1,0:T(8,128)(2,1)} %collective-permute-done.18.refs_4_), channel_id=1, source_target_pairs={{0,8},{4,12},{8,0},{12,4},{1,9},{5,13},{9,1},{13,5},{2,10},{6,14},... | collective-permute-start | bytes 1572872 | tf_op jit(solution)/shard_map/ppermute | solution.py:437
  129.8 20.5 %collective-permute-start.37 = (bf16[128,2048]{1,0:T(8,128)(2,1)}, bf16[128,2048]{1,0:T(8,128)(2,1)S(1)}, u32[]{:S(2)}, u32[]{:S(2)}) collective-permute-start(bf16[128,2048]{1,0:T(8,128)(2,1)} %collective-permute-done.18.refs_4_), channel_id=1, source_target_pairs={{0,4},{4,0},{8,12},{12,8},{1,5},{5,1},{9,13},{13,9},{2,6},{6,2},{1... | collective-permute-start | bytes 1572872 | tf_op jit(solution)/shard_map/ppermute | solution.py:477
  129.8 28.9 %collective-permute-start.19 = (bf16[136,2048]{1,0:T(8,128)(2,1)S(1)}, bf16[136,2048]{1,0:T(8,128)(2,1)S(1)}, u32[]{:S(2)}, u32[]{:S(2)}) collective-permute-start(bf16[136,2048]{1,0:T(8,128)(2,1)S(1)} %add_convert_fusion.5), channel_id=1, source_target_pairs={{0,3},{1,0},{2,1},{3,2},{4,7},{5,4},{6,5},{7,6},{8,11},{9,8},{10,9... | collective-permute-start | bytes 1671176 | tf_op jit(solution)/shard_map/ppermute | solution.py:437
  140.1 18.6 %collective-permute-start.26 = (bf16[136,2048]{1,0:T(8,128)(2,1)S(1)}, bf16[136,2048]{1,0:T(8,128)(2,1)}, u32[]{:S(2)}, u32[]{:S(2)}) collective-permute-start(bf16[136,2048]{1,0:T(8,128)(2,1)S(1)} %add_convert_fusion.3), channel_id=1, source_target_pairs={{0,1},{1,2},{2,3},{3,0},{4,5},{5,6},{6,7},{7,4},{8,9},{9,10},{10,1... | collective-permute-start | bytes 1671176 | tf_op jit(solution)/shard_map/ppermute | solution.py:437
  150.3 28.4 %collective-permute-start.33 = (bf16[136,2048]{1,0:T(8,128)(2,1)S(1)}, bf16[136,2048]{1,0:T(8,128)(2,1)}, u32[]{:S(2)}, u32[]{:S(2)}) collective-permute-start(bf16[136,2048]{1,0:T(8,128)(2,1)S(1)} %add_convert_fusion.1), channel_id=1, source_target_pairs={{0,2},{1,3},{2,0},{3,1},{4,6},{5,7},{6,4},{7,5},{8,10},{9,11},{10,... | collective-permute-start | bytes 1671176 | tf_op jit(solution)/shard_map/ppermute | solution.py:437
  150.3 15.2 %collective-permute-start.39 = (bf16[128,2048]{1,0:T(8,128)(2,1)}, bf16[128,2048]{1,0:T(8,128)(2,1)}, u32[]{:S(2)}, u32[]{:S(2)}) collective-permute-start(bf16[128,2048]{1,0:T(8,128)(2,1)} %collective-permute-done.32.refs_8_), channel_id=1, source_target_pairs={{0,8},{4,12},{8,0},{12,4},{1,9},{5,13},{9,1},{13,5},{2,10},{6,14},... | collective-permute-start | bytes 1572872 | tf_op jit(solution)/shard_map/ppermute | solution.py:437
  150.9 23.8 %collective-permute-start.42 = (bf16[128,2048]{1,0:T(8,128)(2,1)}, bf16[128,2048]{1,0:T(8,128)(2,1)}, u32[]{:S(2)}, u32[]{:S(2)}) collective-permute-start(bf16[128,2048]{1,0:T(8,128)(2,1)} %collective-permute-done.25.refs_12_), channel_id=1, source_target_pairs={{0,8},{4,12},{8,0},{12,4},{1,9},{5,13},{9,1},{13,5},{2,10},{6,14},... | collective-permute-start | bytes 1572872 | tf_op jit(solution)/shard_map/ppermute | solution.py:437
  152.4 26.4 %copy-start.18 = (bf16[136,2048]{1,0:T(8,128)(2,1)S(1)}, bf16[136,2048]{1,0:T(8,128)(2,1)}, u32[]{:S(2)}) copy-start(bf16[136,2048]{1,0:T(8,128)(2,1)} %get-tuple-element.58) | copy-start | bytes 1671172
  158.7 23.5 %collective-permute-start.43 = (bf16[128,2048]{1,0:T(8,128)(2,1)}, bf16[128,2048]{1,0:T(8,128)(2,1)S(1)}, u32[]{:S(2)}, u32[]{:S(2)}) collective-permute-start(bf16[128,2048]{1,0:T(8,128)(2,1)} %collective-permute-done.25.refs_12_), channel_id=1, source_target_pairs={{0,4},{4,0},{8,12},{12,8},{1,5},{5,1},{9,13},{13,9},{2,6},{6,2},{1... | collective-permute-start | bytes 1572872 | tf_op jit(solution)/shard_map/ppermute | solution.py:477
  158.8 23.4 %collective-permute-start.40 = (bf16[128,2048]{1,0:T(8,128)(2,1)}, bf16[128,2048]{1,0:T(8,128)(2,1)S(1)}, u32[]{:S(2)}, u32[]{:S(2)}) collective-permute-start(bf16[128,2048]{1,0:T(8,128)(2,1)} %collective-permute-done.32.refs_8_), channel_id=1, source_target_pairs={{0,4},{4,0},{8,12},{12,8},{1,5},{5,1},{9,13},{13,9},{2,6},{6,2},{1... | collective-permute-start | bytes 1572872 | tf_op jit(solution)/shard_map/ppermute | solution.py:477
  165.5 16.6 %collective-permute-start.38 = (bf16[128,2048]{1,0:T(8,128)(2,1)}, bf16[128,2048]{1,0:T(8,128)(2,1)}, u32[]{:S(2)}, u32[]{:S(2)}) collective-permute-start(bf16[128,2048]{1,0:T(8,128)(2,1)} %collective-permute-done.36.refs_5_), channel_id=1, source_target_pairs={{0,4},{4,0},{8,12},{12,8},{1,5},{5,1},{9,13},{13,9},{2,6},{6,2},{1... | collective-permute-start | bytes 1572872 | tf_op jit(solution)/shard_map/ppermute | solution.py:477
  174.7 7.5 %collective-permute-start.41 = (bf16[128,2048]{1,0:T(8,128)(2,1)}, bf16[128,2048]{1,0:T(8,128)(2,1)}, u32[]{:S(2)}, u32[]{:S(2)}) collective-permute-start(bf16[128,2048]{1,0:T(8,128)(2,1)} %collective-permute-done.39.refs_9_), channel_id=1, source_target_pairs={{0,4},{4,0},{8,12},{12,8},{1,5},{5,1},{9,13},{13,9},{2,6},{6,2},{1... | collective-permute-start | bytes 1572872 | tf_op jit(solution)/shard_map/ppermute | solution.py:477
  178.6 3.5 %collective-permute-start.44 = (bf16[128,2048]{1,0:T(8,128)(2,1)}, bf16[128,2048]{1,0:T(8,128)(2,1)S(1)}, u32[]{:S(2)}, u32[]{:S(2)}) collective-permute-start(bf16[128,2048]{1,0:T(8,128)(2,1)} %collective-permute-done.42.refs_13_), channel_id=1, source_target_pairs={{0,4},{4,0},{8,12},{12,8},{1,5},{5,1},{9,13},{13,9},{2,6},{6,2},{1... | collective-permute-start | bytes 1572872 | tf_op jit(solution)/shard_map/ppermute | solution.py:477
  (25 other events, 166.2 us)
